TPU v7x, 32 devices: a whole 2x2x4 slice. The times are simulated.
32 devices in a mesh: dp: 8 (over z, x), rep: 4 (over y, core).
Axes of the slice: x: 2, y: 2, z: 4, core: 2. Of those that a mesh axis runs over, the one named last changes fastest.
Arguments:
- tokens: bfloat16 [128, 256, 512], P(('dp', 'rep')), may hold values from -6 to 6
- cotangent: bfloat16 [128, 256, 512], P(('dp', 'rep')), may hold values from -6 to 6
- target_lengths: int32 [128], P(('dp', 'rep')), may hold values from 32 to 256, as said below
- task_mask: int32 [128, 256], P(('dp', 'rep')), may hold values 0 or 1
- memory_lengths: int32 [128], P(('dp', 'rep')), may hold values from 256 to 1024, as said below
- position_buckets: int32 [256, 256], replicated, may hold values from 0 to 510
- memory: bfloat16 [8, 16, 1024, 512], P(None, 'rep', 'dp'), may hold values from -6 to 6
- self_gain: float32 [512], replicated, may hold values from 0.25 to 1.75
- self_shift: float32 [512], replicated, may hold values from -1.75 to 1.75
- query_weight: bfloat16 [512, 512], replicated, may hold values from -0.25 to 0.25
- query_bias: float32 [512], replicated, may hold values from -1.75 to 1.75
- key_weight: bfloat16 [512, 512], replicated, may hold values from -0.25 to 0.25
- value_weight: bfloat16 [512, 512], replicated, may hold values from -0.25 to 0.25
- value_bias: float32 [512], replicated, may hold values from -1.75 to 1.75
- position_table: float32 [511, 8], replicated, may hold values from -6 to 6
- head_scale: float32 [8], replicated, may hold values from 0.5 to 1.5
- output_weight: bfloat16 [512, 512], replicated, may hold values from -1 to 1
- output_bias: float32 [512], replicated, may hold values from -1.75 to 1.75
- cross_gain: float32 [512], replicated, may hold values from 0.25 to 1.75
- cross_shift: float32 [512], replicated, may hold values from -1.75 to 1.75
- cross_query: bfloat16 [512, 512], replicated, may hold values from -0.25 to 0.25
- cross_query_bias: float32 [512], replicated, may hold values from -1.75 to 1.75
- cross_key: bfloat16 [512, 512], replicated, may hold values from -0.25 to 0.25
- cross_value: bfloat16 [512, 512], replicated, may hold values from -0.25 to 0.25
- cross_value_bias: float32 [512], replicated, may hold values from -1.75 to 1.75
- post_gain: float32 [512], replicated, may hold values from 0.25 to 1.75
- post_shift: float32 [512], replicated, may hold values from -1.75 to 1.75
- cross_output: bfloat16 [512, 512], replicated, may hold values from -0.25 to 0.25
- cross_output_bias: float32 [512], replicated, may hold values from -1.75 to 1.75
- feed_gain: float32 [512], replicated, may hold values from 0.25 to 1.75
- feed_shift: float32 [512], replicated, may hold values from -1.75 to 1.75
- inner_weight: bfloat16 [512, 2048], replicated, may hold values from -0.25 to 0.25
- inner_bias: float32 [2048], replicated, may hold values from -1.75 to 1.75
- inner_gain: float32 [2048], replicated, may hold values from 0.25 to 1.75
- inner_shift: float32 [2048], replicated, may hold values from -1.75 to 1.75
- outer_weight: bfloat16 [2048, 512], replicated, may hold values from -0.125 to 0.125
- outer_bias: float32 [512], replicated, may hold values from -1.75 to 1.75
Outputs:
- layer_output: bfloat16 [128, 256, 512], P(('dp', 'rep'))
- tokens_gradient: bfloat16 [128, 256, 512], P(('dp', 'rep'))
- memory_gradient: bfloat16 [8, 16, 1024, 512], P(None, 'rep', 'dp')
- gradient_self_gain: float32 [512], replicated
- gradient_self_shift: float32 [512], replicated
- gradient_query_weight: float32 [512, 512], replicated
- gradient_query_bias: float32 [512], replicated
- gradient_key_weight: float32 [512, 512], replicated
- gradient_value_weight: float32 [512, 512], replicated
- gradient_value_bias: float32 [512], replicated
- gradient_position_table: float32 [511, 8], replicated
- gradient_head_scale: float32 [8], replicated
- gradient_output_weight: float32 [512, 512], replicated
- gradient_output_bias: float32 [512], replicated
- gradient_cross_gain: float32 [512], replicated
- gradient_cross_shift: float32 [512], replicated
- gradient_cross_query: float32 [512, 512], replicated
- gradient_cross_query_bias: float32 [512], replicated
- gradient_cross_key: float32 [512, 512], replicated
- gradient_cross_value: float32 [512, 512], replicated
- gradient_cross_value_bias: float32 [512], replicated
- gradient_post_gain: float32 [512], replicated
- gradient_post_shift: float32 [512], replicated
- gradient_cross_output: float32 [512, 512], replicated
- gradient_cross_output_bias: float32 [512], replicated
- gradient_feed_gain: float32 [512], replicated
- gradient_feed_shift: float32 [512], replicated
- gradient_inner_weight: float32 [512, 2048], replicated
- gradient_inner_bias: float32 [2048], replicated
- gradient_inner_gain: float32 [2048], replicated
- gradient_inner_shift: float32 [2048], replicated
- gradient_outer_weight: float32 [2048, 512], replicated
- gradient_outer_bias: float32 [512], replicated
Inputs may be any that keep to these rules, and one draw needn't show every extreme that they name: `target_lengths`: some sequence has 256 real tokens in every draw; later positions are padding. `memory_lengths`: some sequence has all 1024 memory positions real in every draw.
All inputs are finite; a program needn't handle non-finite values. No bound on the sum of `task_mask` on one device may be relied on, other than what follows from the above.
Results may differ from a plain program's by a relative error of at most 0.017.
Values may be sent and summed in bfloat16 or wider, within the bound.
A program may use at most 192 MiB of HBM per device.

v0:
```python
import jax
import jax.numpy as jnp
from jax import lax
from jax.sharding import PartitionSpec as P

big_negative = -1e30


def layer_norm(value_in, norm_gain, norm_shift):
    center = value_in - jnp.mean(value_in, axis=-1, keepdims=True)
    spread = jnp.mean(center * center, axis=-1, keepdims=True)
    return center * lax.rsqrt(spread + 1e-05) * norm_gain + norm_shift


def gelu_exact(value_in):
    return jax.nn.gelu(value_in, approximate=False)


def matmul(left_side, right_side):
    return jnp.dot(left_side, right_side, preferred_element_type=jnp.float32)


def outer_sum(left_side, right_side):
    return lax.dot_general(
        left_side, right_side, (((0,), (0,)), ((), ())), preferred_element_type=jnp.float32
    )


def back_product(grad_in, weight):
    return lax.dot_general(
        grad_in, weight, (((grad_in.ndim - 1,), (1,)), ((), ())), preferred_element_type=jnp.float32
    )


def split_heads(matrix, head_count, seq_count, span):
    return matrix.reshape(seq_count, span, head_count, -1).transpose(2, 0, 1, 3)


def merge_heads(stacked):
    head_count, seq_count, span, head_size = stacked.shape
    return stacked.transpose(1, 2, 0, 3).reshape(seq_count * span, head_count * head_size)


def bucket_blocks(position_buckets):
    length = position_buckets.shape[0]
    row_block = 64
    return position_buckets.reshape(length // row_block, row_block, length)


def scores_of(query_block, key_block, extra_bias, allowed):
    raw_scores = (
        jnp.einsum("sqd,skd->sqk", query_block, key_block, preferred_element_type=jnp.float32)
        + extra_bias
    )
    return jnp.where(allowed, raw_scores, big_negative)


def attend_forward(query_block, key_block, value_block, extra_bias, allowed):
    scores = scores_of(query_block, key_block, extra_bias, allowed)
    row_top = jnp.max(scores, axis=-1, keepdims=True)
    weights = jnp.exp(scores - row_top)
    row_total = jnp.sum(weights, axis=-1, keepdims=True)
    rounded = (weights / row_total).astype(jnp.bfloat16)
    attended = jnp.einsum("sqk,skd->sqd", rounded, value_block, preferred_element_type=jnp.float32)
    return (attended, (row_top + jnp.log(row_total))[..., 0])


def attend_backward(query_block, key_block, value_block, extra_bias, allowed, logsum, upstream):
    scores = scores_of(query_block, key_block, extra_bias, allowed)
    weights = jnp.exp(scores - logsum[..., None])
    grad_weights = jnp.einsum(
        "sqd,skd->sqk", upstream, value_block, preferred_element_type=jnp.float32
    )
    row_inner = jnp.sum(weights * grad_weights, axis=-1, keepdims=True)
    dscores = (weights * (grad_weights - row_inner)).astype(jnp.bfloat16)
    dquery = jnp.einsum("sqk,skd->sqd", dscores, key_block, preferred_element_type=jnp.float32)
    grad_keys = jnp.einsum("sqk,sqd->skd", dscores, query_block, preferred_element_type=jnp.float32)
    dvalues = jnp.einsum(
        "sqk,sqd->skd", weights.astype(jnp.bfloat16), upstream, preferred_element_type=jnp.float32
    )
    return (dquery, grad_keys, dvalues, jnp.sum(dscores.astype(jnp.float32), axis=0))


def local(
    tokens,
    cotangent,
    target_lengths,
    task_mask,
    memory_lengths,
    position_buckets,
    memory,
    self_gain,
    self_shift,
    query_weight,
    query_bias,
    key_weight,
    value_weight,
    value_bias,
    position_table,
    head_scale,
    output_weight,
    output_bias,
    cross_gain,
    cross_shift,
    cross_query,
    cross_query_bias,
    cross_key,
    cross_value,
    cross_value_bias,
    post_gain,
    post_shift,
    cross_output,
    cross_output_bias,
    feed_gain,
    feed_shift,
    inner_weight,
    inner_bias,
    inner_gain,
    inner_shift,
    outer_weight,
    outer_bias,
):
    seq_count = tokens.shape[0]
    length = tokens.shape[1]
    model_width = tokens.shape[2]
    head_count = head_scale.shape[0]
    bucket_count = position_table.shape[0]
    row_count = seq_count * length
    mem_total = memory.shape[2] * lax.axis_size("dp")
    bucket_ids = jnp.arange(bucket_count, dtype=jnp.int32)
    bucket_rows = bucket_blocks(position_buckets)
    local_key = matmul(memory, cross_key).astype(jnp.bfloat16)
    local_value = (matmul(memory, cross_value) + cross_value_bias).astype(jnp.bfloat16)
    key_arrived, value_arrived = (
        lax.all_to_all(local_key, "dp", split_axis=0, concat_axis=2, tiled=True),
        lax.all_to_all(local_value, "dp", split_axis=0, concat_axis=2, tiled=True),
    )
    key_two = key_arrived.reshape(seq_count * mem_total, model_width)
    value_two = value_arrived.reshape(seq_count * mem_total, model_width)
    places = jnp.arange(length)
    causal = places[None, :, None] >= places[None, None, :]
    self_allowed = causal & (places[None, None, :] < target_lengths[:, None, None])
    cross_allowed = jnp.arange(mem_total)[None, None, :] < memory_lengths[:, None, None]
    stream_zero = tokens.astype(jnp.float32).reshape(row_count, model_width)
    normed_one, norm_one_back = jax.vjp(layer_norm, stream_zero, self_gain, self_shift)
    normed_one_low = normed_one.astype(jnp.bfloat16)
    query_one = ((matmul(normed_one_low, query_weight) + query_bias) * 0.125).astype(jnp.bfloat16)
    key_one = matmul(normed_one_low, key_weight).astype(jnp.bfloat16)
    value_one = (matmul(normed_one_low, value_weight) + value_bias).astype(jnp.bfloat16)

    def bias_rows(rows_ids):
        one_hot = (rows_ids[:, :, None] == bucket_ids[None, None, :]).astype(jnp.float32)
        return jnp.einsum("qkb,bh->hqk", one_hot, position_table, precision=lax.Precision.HIGHEST)

    bias_heads = jnp.transpose(lax.map(bias_rows, bucket_rows), (1, 0, 2, 3)).reshape(
        head_count, length, length
    )
    heads_query = split_heads(query_one, head_count, seq_count, length)
    heads_key = split_heads(key_one, head_count, seq_count, length)
    heads_value = split_heads(value_one, head_count, seq_count, length)

    def self_forward(packed):
        return attend_forward(packed[0], packed[1], packed[2], packed[3], self_allowed)

    out_one, logsum_one = lax.map(self_forward, (heads_query, heads_key, heads_value, bias_heads))
    mixed_one = merge_heads(out_one * head_scale[:, None, None, None]).astype(jnp.bfloat16)
    stream_one = stream_zero + matmul(mixed_one, output_weight) + output_bias
    normed_two, norm_two_back = jax.vjp(layer_norm, stream_one, cross_gain, cross_shift)
    normed_two_low = normed_two.astype(jnp.bfloat16)
    query_two = ((matmul(normed_two_low, cross_query) + cross_query_bias) * 0.125).astype(
        jnp.bfloat16
    )
    heads_query_two = split_heads(query_two, head_count, seq_count, length)
    heads_key_two = split_heads(key_two, head_count, seq_count, mem_total)
    heads_value_two = split_heads(value_two, head_count, seq_count, mem_total)

    def cross_forward(packed):
        return attend_forward(packed[0], packed[1], packed[2], 0.0, cross_allowed)

    out_two, logsum_two = lax.map(cross_forward, (heads_query_two, heads_key_two, heads_value_two))
    post_two, post_back = jax.vjp(layer_norm, merge_heads(out_two), post_gain, post_shift)
    post_low = post_two.astype(jnp.bfloat16)
    stream_two = stream_one + matmul(post_low, cross_output) + cross_output_bias
    normed_three, norm_three_back = jax.vjp(layer_norm, stream_two, feed_gain, feed_shift)
    normed_three_low = normed_three.astype(jnp.bfloat16)
    inner_pre = matmul(normed_three_low, inner_weight) + inner_bias
    activated, gelu_back = jax.vjp(gelu_exact, inner_pre)
    normed_inner, inner_back = jax.vjp(layer_norm, activated, inner_gain, inner_shift)
    normed_inner_low = normed_inner.astype(jnp.bfloat16)
    stream_three = stream_two + matmul(normed_inner_low, outer_weight) + outer_bias
    layer_output = stream_three.astype(jnp.bfloat16).reshape(seq_count, length, model_width)
    keep = task_mask.astype(jnp.float32) * (places[None, :] < target_lengths[:, None]).astype(
        jnp.float32
    )
    grad_three = (cotangent.astype(jnp.float32) * keep[:, :, None]).reshape(row_count, model_width)
    sum_outer_bias = jnp.sum(grad_three, axis=0)
    low_three = grad_three.astype(jnp.bfloat16)
    sum_outer_weight = outer_sum(normed_inner_low, low_three)
    grad_activated, sum_inner_gain, sum_inner_shift = inner_back(
        back_product(low_three, outer_weight)
    )
    grad_inner = gelu_back(grad_activated)[0]
    sum_inner_bias = jnp.sum(grad_inner, axis=0)
    low_inner = grad_inner.astype(jnp.bfloat16)
    sum_inner_weight = outer_sum(normed_three_low, low_inner)
    part_two, sum_feed_gain, sum_feed_shift = norm_three_back(back_product(low_inner, inner_weight))
    grad_two = grad_three + part_two
    sum_cross_output_bias = jnp.sum(grad_two, axis=0)
    low_two = grad_two.astype(jnp.bfloat16)
    sum_cross_output = outer_sum(post_low, low_two)
    grad_merged, sum_post_gain, sum_post_shift = post_back(back_product(low_two, cross_output))
    upstream_two = split_heads(grad_merged.astype(jnp.bfloat16), head_count, seq_count, length)

    def cross_backward(packed):
        return attend_backward(
            packed[0], packed[1], packed[2], 0.0, cross_allowed, packed[3], packed[4]
        )

    dquery_two, dkey_two, dvalue_two, unused_bias = lax.map(
        cross_backward, (heads_query_two, heads_key_two, heads_value_two, logsum_two, upstream_two)
    )
    low_query_two = merge_heads(dquery_two).astype(jnp.bfloat16) * 0.125
    low_key_two = merge_heads(dkey_two).astype(jnp.bfloat16)
    low_value_two = merge_heads(dvalue_two).astype(jnp.bfloat16)
    sum_cross_query = outer_sum(normed_two_low, low_query_two)
    sum_cross_query_bias = jnp.sum(low_query_two.astype(jnp.float32), axis=0)
    sum_cross_value_bias = jnp.sum(low_value_two.astype(jnp.float32), axis=0)
    key_back, value_back = (
        lax.all_to_all(
            low_key_two.reshape(1, seq_count, mem_total, model_width),
            "dp",
            split_axis=2,
            concat_axis=0,
            tiled=True,
        ),
        lax.all_to_all(
            low_value_two.reshape(1, seq_count, mem_total, model_width),
            "dp",
            split_axis=2,
            concat_axis=0,
            tiled=True,
        ),
    )
    memory_gradient = (
        back_product(key_back, cross_key) + back_product(value_back, cross_value)
    ).astype(jnp.bfloat16)
    sum_cross_key = lax.dot_general(
        memory, key_back, (((0, 1, 2), (0, 1, 2)), ((), ())), preferred_element_type=jnp.float32
    )
    sum_cross_value = lax.dot_general(
        memory, value_back, (((0, 1, 2), (0, 1, 2)), ((), ())), preferred_element_type=jnp.float32
    )
    part_one, sum_cross_gain, sum_cross_shift = norm_two_back(
        back_product(low_query_two, cross_query)
    )
    grad_one = grad_two + part_one
    sum_output_bias = jnp.sum(grad_one, axis=0)
    low_one = grad_one.astype(jnp.bfloat16)
    sum_output_weight = outer_sum(mixed_one, low_one)
    grad_mixed = split_heads(back_product(low_one, output_weight), head_count, seq_count, length)
    sum_head_scale = jnp.sum(out_one * grad_mixed, axis=(1, 2, 3))
    upstream_one = (grad_mixed * head_scale[:, None, None, None]).astype(jnp.bfloat16)

    def self_backward(packed):
        return attend_backward(
            packed[0], packed[1], packed[2], packed[3], self_allowed, packed[4], packed[5]
        )

    dquery_one, dkey_one, dvalue_one, bias_grads = lax.map(
        self_backward, (heads_query, heads_key, heads_value, bias_heads, logsum_one, upstream_one)
    )
    block_count = bucket_rows.shape[0]
    grad_blocks = jnp.transpose(
        bias_grads.reshape(head_count, block_count, length // block_count, length), (1, 0, 2, 3)
    )

    def bucket_sums(total, packed):
        one_hot = (packed[0][:, :, None] == bucket_ids[None, None, :]).astype(jnp.float32)
        return (
            total + jnp.einsum("qkb,hqk->bh", one_hot, packed[1], precision=lax.Precision.HIGHEST),
            None,
        )

    sum_position_table, unused_end = lax.scan(
        bucket_sums, jnp.zeros((bucket_count, head_count), jnp.float32), (bucket_rows, grad_blocks)
    )
    low_query_one = merge_heads(dquery_one).astype(jnp.bfloat16) * 0.125
    low_key_one = merge_heads(dkey_one).astype(jnp.bfloat16)
    low_value_one = merge_heads(dvalue_one).astype(jnp.bfloat16)
    sum_query_weight = outer_sum(normed_one_low, low_query_one)
    sum_query_bias = jnp.sum(low_query_one.astype(jnp.float32), axis=0)
    sum_key_weight = outer_sum(normed_one_low, low_key_one)
    sum_value_weight = outer_sum(normed_one_low, low_value_one)
    sum_value_bias = jnp.sum(low_value_one.astype(jnp.float32), axis=0)
    grad_normed_one = (
        back_product(low_query_one, query_weight)
        + back_product(low_key_one, key_weight)
        + back_product(low_value_one, value_weight)
    )
    part_zero, sum_self_gain, sum_self_shift = norm_one_back(grad_normed_one)
    tokens_gradient = (
        (grad_one + part_zero).astype(jnp.bfloat16).reshape(seq_count, length, model_width)
    )
    totals = lax.psum(
        (
            sum_self_gain,
            sum_self_shift,
            sum_query_weight,
            sum_query_bias,
            sum_key_weight,
            sum_value_weight,
            sum_value_bias,
            sum_position_table,
            sum_head_scale,
            sum_output_weight,
            sum_output_bias,
            sum_cross_gain,
            sum_cross_shift,
            sum_cross_query,
            sum_cross_query_bias,
            sum_cross_key,
            sum_cross_value,
            sum_cross_value_bias,
            sum_post_gain,
            sum_post_shift,
            sum_cross_output,
            sum_cross_output_bias,
            sum_feed_gain,
            sum_feed_shift,
            sum_inner_weight,
            sum_inner_bias,
            sum_inner_gain,
            sum_inner_shift,
            sum_outer_weight,
            sum_outer_bias,
        ),
        ("dp", "rep"),
    )
    return (layer_output, tokens_gradient, memory_gradient) + tuple(totals)


def solution(mesh):
    in_specs = (
        P(("dp", "rep"), None, None),
        P(("dp", "rep"), None, None),
        P(("dp", "rep")),
        P(("dp", "rep"), None),
        P(("dp", "rep")),
        P(),
        P(None, "rep", "dp", None),
        P(),
        P(),
        P(),
        P(),
        P(),
        P(),
        P(),
        P(),
        P(),
        P(),
        P(),
        P(),
        P(),
        P(),
        P(),
        P(),
        P(),
        P(),
        P(),
        P(),
        P(),
        P(),
        P(),
        P(),
        P(),
        P(),
        P(),
        P(),
        P(),
        P(),
    )
    out_specs = (
        P(("dp", "rep"), None, None),
        P(("dp", "rep"), None, None),
        P(None, "rep", "dp", None),
        P(),
        P(),
        P(),
        P(),
        P(),
        P(),
        P(),
        P(),
        P(),
        P(),
        P(),
        P(),
        P(),
        P(),
        P(),
        P(),
        P(),
        P(),
        P(),
        P(),
        P(),
        P(),
        P(),
        P(),
        P(),
        P(),
        P(),
        P(),
        P(),
        P(),
    )
    return jax.shard_map(local, mesh=mesh, in_specs=in_specs, out_specs=out_specs, check_vma=False)
```

profile of v0, /device:TPU:0, one launch (start us, length us, event | category | flops | bytes accessed | tf_op | source)
XLA Modules:
  0.0 1245.8 jit_solution(17681116033645077815)
XLA Ops:
  52.7 77.0 %while.86 = (s32[]{:T(128)}, f32[4,8,64,256]{3,1,2,0:T(8,128)}, s32[4,64,256]{2,1,0:T(8,128)}, f32[511,8]{0,1:T(8,128)S(1)}) while((s32[]{:T(128)}, f32[4,8,64,256]{3,1,2,0:T(8,128)}, s32[4,64,256]{2,1,0:T(8,128)}, f32[511,8]{0,1:T(8,128)S(1)}) %tuple.235), condition=%wide.region_3.4_spmd.clone.clone, body=%wide.region_2.3_spmd.clone.sunk.clone | while | flops 812105728 | bytes 737817 | solution.py:155
  53.5 18.4 %fusion.310 = f32[4,8,64,256]{3,1,2,0:T(8,128)} fusion(f32[4,8,64,256]{3,1,2,0:T(8,128)} %get-tuple-element.1226, s32[]{:T(128)} %get-tuple-element.1225, s32[64,256]{1,0:T(8,128)S(1)} %dynamic-slice_bitcast_fusion.18, f32[511,8]{0,1:T(8,128)S(1)} %get-tuple-element.1232), kind=kOutput, calls=%fused_computation.10.clone.1.clone | convolution fusion | flops 812105728 | bytes 606688 | tf_op jit(solution)/shard_map/while/body/eval_jaxpr/qkb,bh->hqk/dot_general | solution.py:153
  72.8 18.4 %fusion.310 = f32[4,8,64,256]{3,1,2,0:T(8,128)} fusion(f32[4,8,64,256]{3,1,2,0:T(8,128)} %get-tuple-element.1226, s32[]{:T(128)} %get-tuple-element.1225, s32[64,256]{1,0:T(8,128)S(1)} %dynamic-slice_bitcast_fusion.18, f32[511,8]{0,1:T(8,128)S(1)} %get-tuple-element.1232), kind=kOutput, calls=%fused_computation.10.clone.1.clone | convolution fusion | flops 812105728 | bytes 606688 | tf_op jit(solution)/shard_map/while/body/eval_jaxpr/qkb,bh->hqk/dot_general | solution.py:153
  92.0 18.4 %fusion.310 = f32[4,8,64,256]{3,1,2,0:T(8,128)} fusion(f32[4,8,64,256]{3,1,2,0:T(8,128)} %get-tuple-element.1226, s32[]{:T(128)} %get-tuple-element.1225, s32[64,256]{1,0:T(8,128)S(1)} %dynamic-slice_bitcast_fusion.18, f32[511,8]{0,1:T(8,128)S(1)} %get-tuple-element.1232), kind=kOutput, calls=%fused_computation.10.clone.1.clone | convolution fusion | flops 812105728 | bytes 606688 | tf_op jit(solution)/shard_map/while/body/eval_jaxpr/qkb,bh->hqk/dot_general | solution.py:153
  111.2 18.4 %fusion.310 = f32[4,8,64,256]{3,1,2,0:T(8,128)} fusion(f32[4,8,64,256]{3,1,2,0:T(8,128)} %get-tuple-element.1226, s32[]{:T(128)} %get-tuple-element.1225, s32[64,256]{1,0:T(8,128)S(1)} %dynamic-slice_bitcast_fusion.18, f32[511,8]{0,1:T(8,128)S(1)} %get-tuple-element.1232), kind=kOutput, calls=%fused_computation.10.clone.1.clone | convolution fusion | flops 812105728 | bytes 606688 | tf_op jit(solution)/shard_map/while/body/eval_jaxpr/qkb,bh->hqk/dot_general | solution.py:153
  145.6 37.2 %while.87 = (s32[]{:T(128)}, f32[8,4,256,64]{2,1,3,0:T(4,128)}, f32[8,4,256]{2,1,0:T(4,128)S(1)}, bf16[8,4,256,64]{2,3,1,0:T(8,128)(2,1)}, bf16[8,4,256,64]{2,3,...) while((s32[]{:T(128)}, f32[8,4,256,64]{2,1,3,0:T(4,128)}, ...), condition=%wide.region_7.8_spmd.clone.clone, body=%wide.region_4.7_spmd.clone.sunk.clone | while | flops 69467136 | bytes 5213285 | solution.py:165
  202.2 7.6 copy.149
  221.9 16.3 %all-to-all-done.1 = bf16[8,4,128,512]{3,2,1,0:T(8,128)(2,1)} async-done(((bf16[8,4,128,512]{3,2,1,0:T(8,128)(2,1)}), bf16[8,4,128,512]{3,2,1,0:T(8,128)(2,1)}, u32[]{:S(2)}, u32[]{:S(2)}) %all-to-all-start.1) | async-done | bytes 4194336 | tf_op jit(solution)/shard_map/all_to_all | solution.py:136
  238.3 7.6 copy.150
  258.0 46.8 %while.88 = (s32[]{:T(128)}, f32[8,4,256,64]{2,3,1,0:T(8,128)}, f32[8,4,256]{2,1,0:T(4,128)S(1)}, bf16[8,4,256,64]{2,3,1,0:T(8,128)(2,1)S(1)}, bf16[8,4,1024,64]...) while((s32[]{:T(128)}, f32[8,4,256,64]{2,3,1,0:T(8,128)}, ...), condition=%wide.region_13.14_spmd.clone.clone, body=%wide.region_10.13_spmd.clone.sunk.clone | while | flops 277875712 | bytes 14076001 | solution.py:180
  321.7 23.2 %fusion.182 = (f32[1024]{0:T(1024)S(1)}, f32[1024,2048]{1,0:T(8,128)S(1)}, f32[1024,2048]{1,0:T(8,128)}, f32[1024,2048]{1,0:T(8,128)}) fusion(f32[2048]{0:T(1024)S(1)} %copy-done.107, bf16[512,2048]{1,0:T(8,128)(2,1)S(1)} %copy-done, f32[1024,512]{1,0:T(8,128)S(1)} %get-tuple-element.785, f32[512]{0:T(512)S(1)} %copy-done.100, f32[512]{0:T(512)S(1)} %copy-done.91, ...), kind=kOutput, calls=%fused_computation.288 | convolution fusion | flops 2288516096 | bytes 29384704 | tf_op jit(solution)/shard_map/dot_general | solution.py:20
  353.9 13.5 %fusion.176 = (f32[2048]{0:T(1024)}, bf16[1024,2048]{1,0:T(8,128)(2,1)S(1)}, bf16[1024,2048]{1,0:T(8,128)(2,1)}) fusion(f32[1024,2048]{1,0:T(8,128)} %get-tuple-element.756, f32[1024]{0:T(1024)} %negate_multiply_fusion.5, f32[1024]{0:T(1024)S(1)} %get-tuple-element.776, f32[1024,2048]{1,0:T(8,128)S(1)} %get-tuple-element.755, ...), kind=kLoop, calls=%fused_computation.282 | loop fusion | flops 56621056 | bytes 41992192 | tf_op jit(solution)/shard_map/reduce_sum | solution.py:203
  384.1 89.8 %while.89 = (s32[]{:T(128)}, bf16[8,4,256,64]{2,3,1,0:T(8,128)(2,1)S(1)}, bf16[8,4,1024,64]{2,3,0,1:T(8,128)(2,1)}, bf16[8,4,1024,64]{2,3,0,1:T(8,128)(2,1)}, bf...) while((s32[]{:T(128)}, ...), condition=%wide.region_28.29_spmd.clone.clone, body=%wide.region_26.28_spmd.clone.sunk.clone | while | flops 683674624 | bytes 36225148 | solution.py:219
  473.9 8.2 copy.172
  506.0 7.8 copy.176
  518.5 61.0 %all-to-all-done.2 = bf16[1,4,1024,512]{3,1,0,2:T(4,128)(2,1)} async-done(((bf16[1,4,1024,512]{3,1,0,2:T(4,128)(2,1)}), bf16[1,4,1024,512]{3,1,0,2:T(4,128)(2,1)}, u32[]{:S(2)}, u32[]{:S(2)}) %all-to-all-start.2) | async-done | bytes 4194336 | tf_op jit(solution)/shard_map/all_to_all | solution.py:229
  584.2 138.2 %while.90 = (s32[]{:T(128)}, bf16[8,4,256,64]{2,3,1,0:T(8,128)(2,1)}, bf16[8,4,256,64]{2,3,1,0:T(8,128)(2,1)}, bf16[8,4,256,64]{2,3,1,0:T(8,128)(2,1)}, f32[8,25...) while((s32[]{:T(128)}, ...), condition=%wide.region_34.35_spmd.clone.clone, body=%wide.region_31.34_spmd.clone.sunk.clone | while | flops 170851328 | bytes 12018829 | solution.py:269
  782.6 49.1 %while.91 = (s32[]{:T(128)}, f32[511,8]{0,1:T(8,128)S(1)}, s32[4,64,256]{2,1,0:T(8,128)}, f32[4,8,64,256]{3,1,2,0:T(8,128)}) while((s32[]{:T(128)}, f32[511,8]{0,1:T(8,128)S(1)}, s32[4,64,256]{2,1,0:T(8,128)}, f32[4,8,64,256]{3,1,2,0:T(8,128)}) %tuple.234), condition=%wide.region_49.50_spmd.clone.clone, body=%wide.region_48.49_spmd.clone.sunk.clone | while | flops 812113920 | bytes 754179 | solution.py:284
  783.7 11.3 fusion.341
  795.9 11.3 fusion.341
  808.0 11.3 fusion.341
  820.2 11.3 fusion.341
  843.9 211.6 %all-reduce.7.cloned.1.call-done = (f32[512,512]{1,0:T(8,128)}, f32[512,512]{1,0:T(8,128)}, f32[512,512]{1,0:T(8,128)}, f32[512,512]{1,0:T(8,128)}, f32[512,512]...) async-done(((f32[512,512]{1,0:T(8,128)}, f32[512,512]{1,0:T(8,128)}, ...) | async-done | bytes 16777232 | tf_op jit(solution)/shard_map/psum | solution.py:304
  1059.5 155.4 %all-reduce.5.cloned.1.call-done = (f32[512]{0:T(512)}, f32[512]{0:T(512)}, f32[512]{0:T(512)}, f32[512]{0:T(512)}, f32[511,8]{0,1:T(8,128)}, /*index=5*/f32[8]{...) async-done(((f32[512]{0:T(512)}, f32[512]{0:T(512)}, ...) | async-done | bytes 71696 | tf_op jit(solution)/shard_map/psum | solution.py:304
  (712 shorter events, 597.6 us)
Async XLA Ops:
  7.2 314.1 %copy-start = (bf16[512,2048]{1,0:T(8,128)(2,1)S(1)}, bf16[512,2048]{1,0:T(8,128)(2,1)}, u32[]{:S(2)}) copy-start(bf16[512,2048]{1,0:T(8,128)(2,1)} %param.80) | copy-start | bytes 6291460
  14.0 7.4 copy-start.2
  14.0 125.3 %all-to-all-start = ((bf16[8,4,128,512]{3,2,1,0:T(8,128)(2,1)}), bf16[8,4,128,512]{3,2,1,0:T(8,128)(2,1)}, u32[]{:S(2)}, u32[]{:S(2)}) async-start(bf16[8,4,128,512]{3,2,1,0:T(8,128)(2,1)} %convolution_convert_fusion), calls=%async_computation | async-start | bytes 8388608 | tf_op jit(solution)/shard_map/all_to_all | solution.py:135
  139.4 98.9 %all-to-all-start.1 = ((bf16[8,4,128,512]{3,2,1,0:T(8,128)(2,1)}), bf16[8,4,128,512]{3,2,1,0:T(8,128)(2,1)}, u32[]{:S(2)}, u32[]{:S(2)}) async-start(bf16[8,4,128,512]{3,2,1,0:T(8,128)(2,1)} %add_convert_fusion.2), calls=%async_computation.1 | async-start | bytes 8388608 | tf_op jit(solution)/shard_map/all_to_all | solution.py:136
  145.6 37.3 %copy-start.123 = (f32[8]{0:T(128)S(1)}, f32[8]{0:T(128)}, u32[]{:S(2)}) copy-start(f32[8]{0:T(128)} %param.64) | copy-start | bytes 100
  320.8 24.0 %copy-start.9 = (f32[1024,512]{1,0:T(8,128)}, f32[1024,512]{1,0:T(8,128)S(1)}, u32[]{:S(2)}) copy-start(f32[1024,512]{1,0:T(8,128)S(1)} %get-tuple-element.785) | copy-start | bytes 6291460
  321.7 23.2 %copy-start.41 = (bf16[1024,512]{1,0:T(8,128)(2,1)S(1)}, bf16[1024,512]{1,0:T(8,128)(2,1)}, u32[]{:S(2)}) copy-start(bf16[1024,512]{1,0:T(8,128)(2,1)} %bitcast_convert_fusion) | copy-start | bytes 3145732
  321.7 23.2 %copy-start.90 = (f32[2048]{0:T(1024)S(1)}, f32[2048]{0:T(1024)}, u32[]{:S(2)}) copy-start(f32[2048]{0:T(1024)} %param.82) | copy-start | bytes 24580
  321.7 23.2 %copy-start.127 = (bf16[2048,512]{1,0:T(8,128)(2,1)S(1)}, bf16[2048,512]{1,0:T(8,128)(2,1)}, u32[]{:S(2)}) copy-start(bf16[2048,512]{1,0:T(8,128)(2,1)} %param.84) | copy-start | bytes 6291460
  367.4 6.6 copy-start.7
  367.4 6.6 copy-start.10
  367.4 6.6 copy-start.92
  473.9 19.2 %copy-start.23 = (bf16[8,4,256,64]{2,3,1,0:T(8,128)(2,1)}, bf16[8,4,256,64]{2,3,1,0:T(8,128)(2,1)S(1)}, u32[]{:S(2)}) copy-start(bf16[8,4,256,64]{2,3,1,0:T(8,128)(2,1)S(1)} %get-tuple-element.291) | copy-start | bytes 3145732
  482.1 97.4 %all-to-all-start.2 = ((bf16[1,4,1024,512]{3,1,0,2:T(4,128)(2,1)}), bf16[1,4,1024,512]{3,1,0,2:T(4,128)(2,1)}, u32[]{:S(2)}, u32[]{:S(2)}) async-start(bf16[1,4,1024,512]{3,1,0,2:T(4,128)(2,1)} %copy.172), calls=%async_computation.2 | async-start | bytes 8388608 | tf_op jit(solution)/shard_map/all_to_all | solution.py:229
  506.0 7.8 copy-start.124
  518.5 65.6 %copy-start.27 = (pred[256,256]{0,1:T(8,128)(4,1)S(1)}, pred[256,256]{0,1:T(8,128)(4,1)}, u32[]{:S(2)}) copy-start(pred[256,256]{0,1:T(8,128)(4,1)} %copy-done.26) | copy-start | bytes 196612
  518.5 65.6 %copy-start.70 = (pred[4,256]{1,0:T(4,128)(4,1)S(1)}, pred[4,256]{1,0:T(4,128)(4,1)}, u32[]{:S(2)}) copy-start(pred[4,256]{1,0:T(4,128)(4,1)} %copy-done.69) | copy-start | bytes 3076
  579.5 176.3 %all-to-all-start.3 = ((bf16[1,4,1024,512]{3,1,0,2:T(4,128)(2,1)}), bf16[1,4,1024,512]{3,1,0,2:T(4,128)(2,1)}, u32[]{:S(2)}, u32[]{:S(2)}) async-start(bf16[1,4,1024,512]{3,1,0,2:T(4,128)(2,1)} %copy.176), calls=%async_computation.3 | async-start | bytes 8388608 | tf_op jit(solution)/shard_map/all_to_all | solution.py:236
  584.1 471.5 %all-reduce.7.cloned.1.call-start = ((), (), s32[]{:S(2)}) async-start(), calls=%async_computation.5 | async-start | bytes 33554432 | tf_op jit(solution)/shard_map/psum | solution.py:304
  762.7 452.3 %all-reduce.5.cloned.1.call-start = ((), (), s32[]{:S(2)}) async-start(), calls=%async_computation.4 | async-start | bytes 144384 | tf_op jit(solution)/shard_map/psum | solution.py:304
  782.6 49.8 %copy-start.67 = (bf16[512,512]{1,0:T(8,128)(2,1)S(1)}, bf16[512,512]{1,0:T(8,128)(2,1)}, u32[]{:S(2)}) copy-start(bf16[512,512]{1,0:T(8,128)(2,1)} %param.72) | copy-start | bytes 1572868
  1055.5 161.9 %copy-start.51 = (f32[512,512]{1,0:T(8,128)S(1)}, f32[512,512]{1,0:T(8,128)}, u32[]{:S(2)}) copy-start(f32[512,512]{1,0:T(8,128)} %get-tuple-element.1367) | copy-start | bytes 3145732
  1058.2 160.7 %copy-start.50 = (f32[512,512]{1,0:T(8,128)S(1)}, f32[512,512]{1,0:T(8,128)}, u32[]{:S(2)}) copy-start(f32[512,512]{1,0:T(8,128)} %get-tuple-element.1369) | copy-start | bytes 3145732
  1222.7 6.1 copy-start.46
  (124 other events, 353.5 us)
Sparse Core Ops, SparseCore 0:
  762.8 292.6 all-reduce.6
  1064.8 150.0 all-reduce.4
where the time goes:
time: 1260 us; the launch traced here: 1250 us
  waiting for transfers between devices  444 us (35%)
  matrix products  425 us (34%)
  local copies, waits for them, and re-layouts  266 us (21%)
  other arithmetic  70.4 us (6%)
  starting transfers between devices  23 us (2%)
  between operations  15.7 us (1%)
    psum x2, waiting for transfers between devices, local(): lax.psum((sum_self_gain, sum_self_shift, sum_query_weight, sum_query_bias...  367 us
    unnamed x333, local copies, waits for them, and re-layouts  73.6 us
    dot_general x4, matrix products, bias_rows(): jnp.einsum('qkb,bh->hqk', one_hot, position_table, precision=lax.Precisio...  73.6 us
    all_to_all x1, waiting for transfers between devices, local(): lax.all_to_all(low_key_two.reshape(1, seq_count, mem_total, model_width),...  61 us
    dynamic_update_slice x16, local copies, waits for them, and re-layouts, local(): lax.map(self_backward, (heads_query, heads_key, heads_value, bias_heads,...  56.4 us
    dot_general x32, matrix products, scores_of(): jnp.einsum('sqd,skd->sqk', query_block, key_block, preferred_element_type...  53.1 us
    dot_general x10, matrix products, matmul(): return jnp.dot(left_side, right_side, preferred_element_type=jnp.float32)  50.7 us
    dot_general x4, matrix products, bucket_sums(): jnp.einsum('qkb,hqk->bh', one_hot, packed[1], precision=lax.Precision.HIG...  45.3 us
  transfers between devices with their start and end apart: 6, of which 4 were waited for; matrix products, arithmetic and copies ran while one was open for 37% of the time, Pallas kernels for 0%

commit v1 on v0

v1 whole, which is shorter than its diff:
```python
import functools

import jax
import jax.numpy as jnp
from jax import lax
from jax.experimental import pallas as pl
from jax.experimental.pallas import tpu as pltpu
from jax.sharding import PartitionSpec as P

NEG = -1e30
F32 = jnp.float32
BF16 = jnp.bfloat16
VMEM_LIMIT = 67043328

(
    SELF_GAIN,
    SELF_SHIFT,
    QUERY_BIAS,
    VALUE_BIAS,
    HEAD_SCALE,
    OUTPUT_BIAS,
    CROSS_GAIN,
    CROSS_SHIFT,
    CROSS_QUERY_BIAS,
    CROSS_VALUE_BIAS,
    POST_GAIN,
    POST_SHIFT,
    CROSS_OUTPUT_BIAS,
    FEED_GAIN,
    FEED_SHIFT,
    OUTER_BIAS,
) = range(16)


def mm(a, b):
    return jnp.dot(a, b, preferred_element_type=F32)


def mm_nt(a, b):
    return lax.dot_general(a, b, (((1,), (1,)), ((), ())), preferred_element_type=F32)


def mm_tn(a, b):
    return lax.dot_general(a, b, (((0,), (0,)), ((), ())), preferred_element_type=F32)


def normalize(x):
    center = x - jnp.mean(x, axis=-1, keepdims=True)
    spread = jnp.mean(center * center, axis=-1, keepdims=True)
    scale = lax.rsqrt(spread + 1e-05)
    return center * scale, scale


def norm_back(dy, hat, scale, gain):
    w = dy * gain
    first = jnp.mean(w, axis=-1, keepdims=True)
    second = jnp.mean(w * hat, axis=-1, keepdims=True)
    return (w - first - hat * second) * scale


def colsum(x):
    return jnp.sum(x, axis=0, keepdims=True)


def half_masks(rows):
    lane = lax.broadcasted_iota(jnp.int32, (rows, 128), 1)
    return (lane < 64, lane >= 64)


def pick(mask, x):
    return jnp.where(mask, x.astype(F32), 0.0).astype(BF16)


def pair_lanes(p):
    return pl.ds(pl.multiple_of(p * 128, 128), 128)


def head_rows(p, half):
    return pl.ds(pl.multiple_of(p * 128 + half * 64, 64), 64)


def bias_kernel(buckets_ref, table_ref, out_ref):
    length = buckets_ref.shape[0]
    chunks = table_ref.shape[2] // 128
    key_place = lax.broadcasted_iota(jnp.int32, (length, 128), 0)
    for tile in range(length // 128):
        lanes = pl.ds(tile * 128, 128)
        ids = buckets_ref[:, lanes]
        low, high = ids & 127, ids >> 7
        total = jnp.zeros((length, 128), F32)
        for c in range(chunks):
            row = jnp.broadcast_to(table_ref[0, :, pl.ds(c * 128, 128)], (length, 128))
            got = jnp.take_along_axis(row, low, axis=1, mode="promise_in_bounds")
            total = jnp.where(high == c, got, total)
        query_place = lax.broadcasted_iota(jnp.int32, (length, 128), 1) + tile * 128
        out_ref[0, :, lanes] = jnp.where(key_place <= query_place, total, NEG)


def position_bias(buckets_t, table_t):
    heads = table_t.shape[0]
    length = buckets_t.shape[0]
    return pl.pallas_call(
        bias_kernel,
        out_shape=jax.ShapeDtypeStruct((heads, length, length), F32),
        grid=(heads,),
        in_specs=[
            pl.BlockSpec(buckets_t.shape, lambda h: (0, 0)),
            pl.BlockSpec((1, 1, table_t.shape[2]), lambda h: (h, 0, 0)),
        ],
        out_specs=pl.BlockSpec((1, length, length), lambda h: (h, 0, 0)),
        name="position_bias",
    )(buckets_t, table_t)


def self_forward(s, tlen_ref, tok_ref, bias_ref, vec_ref, wq, wk, wv, wo, q_ref, k_ref, v_ref, lse_ref, ot_ref, x1_ref, vt_ref):
    length = tok_ref.shape[1]
    x0 = tok_ref[0].astype(F32)
    hat, _ = normalize(x0)
    h1 = (hat * vec_ref[SELF_GAIN : SELF_GAIN + 1] + vec_ref[SELF_SHIFT : SELF_SHIFT + 1]).astype(BF16)
    q_ref[0] = ((mm(h1, wq[...]) + vec_ref[QUERY_BIAS : QUERY_BIAS + 1]) * 0.125).astype(BF16)
    k_ref[0] = mm(h1, wk[...]).astype(BF16)
    value = (mm(h1, wv[...]) + vec_ref[VALUE_BIAS : VALUE_BIAS + 1]).astype(BF16)
    v_ref[0] = value
    vt_ref[:, pl.ds(0, length)] = value.T
    key_place = lax.broadcasted_iota(jnp.int32, (length, length), 0)
    outside = jnp.where(key_place < tlen_ref[s], 0.0, NEG)
    masks = half_masks(length)

    @pl.loop(0, q_ref.shape[2] // 128)
    def _(p):
        lanes = pair_lanes(p)
        kp, qp = k_ref[0, :, lanes], q_ref[0, :, lanes]
        for half in range(2):
            st = mm_nt(kp, pick(masks[half], qp)) + bias_ref[2 * p + half] + outside
            top = jnp.max(st, axis=0, keepdims=True)
            e = jnp.exp(st - top)
            total = colsum(e)
            ot = mm(vt_ref[head_rows(p, half), pl.ds(0, length)], e.astype(BF16))
            ot_ref[0, head_rows(p, half), :] = ot * (1.0 / total)
            lse_ref[0, 2 * p + half] = top + jnp.log(total)

    out = ot_ref[0].T
    c1 = (out * vec_ref[HEAD_SCALE : HEAD_SCALE + 1]).astype(BF16)
    x1_ref[...] = x0 + mm(c1, wo[...]) + vec_ref[OUTPUT_BIAS : OUTPUT_BIAS + 1]


def cross_forward(s, mlen_ref, mem_ref, vec_ref, x1, wcq, wck, wcv, q_ref, k_ref, v_ref, lse_ref, ot_ref, vt_ref, st_ref):
    length, mem_total = x1.shape[0], mem_ref.shape[0]
    hat, _ = normalize(x1)
    h2 = (hat * vec_ref[CROSS_GAIN : CROSS_GAIN + 1] + vec_ref[CROSS_SHIFT : CROSS_SHIFT + 1]).astype(BF16)
    q_ref[0] = ((mm(h2, wcq[...]) + vec_ref[CROSS_QUERY_BIAS : CROSS_QUERY_BIAS + 1]) * 0.125).astype(BF16)
    step = 256

    @pl.loop(0, mem_total // step)
    def _(c):
        rows = pl.ds(pl.multiple_of(c * step, step), step)
        part = mem_ref[rows, :]
        k_ref[0, rows, :] = mm(part, wck[...]).astype(BF16)
        v_ref[0, rows, :] = (mm(part, wcv[...]) + vec_ref[CROSS_VALUE_BIAS : CROSS_VALUE_BIAS + 1]).astype(BF16)

    for c in range(mem_total // step):
        vt_ref[:, pl.ds(c * step, step)] = v_ref[0, pl.ds(c * step, step), :].T
    masks = half_masks(length)
    place = lax.broadcasted_iota(jnp.int32, (step, length), 0)

    @pl.loop(0, q_ref.shape[2] // 128)
    def _(p):
        lanes = pair_lanes(p)
        qp = q_ref[0, :, lanes]
        for half in range(2):
            qm = pick(masks[half], qp)
            top = jnp.full((1, length), -jnp.inf, F32)
            for c in range(mem_total // step):
                rows = pl.ds(c * step, step)
                st = mm_nt(k_ref[0, rows, lanes], qm)
                st = st + jnp.where(place < mlen_ref[s] - c * step, 0.0, NEG)
                st_ref[half, rows, :] = st
                top = jnp.maximum(top, jnp.max(st, axis=0, keepdims=True))
            total = jnp.zeros((1, length), F32)
            ot = jnp.zeros((64, length), F32)
            for c in range(mem_total // step):
                e = jnp.exp(st_ref[half, pl.ds(c * step, step), :] - top)
                total = total + colsum(e)
                ot = ot + mm(vt_ref[head_rows(p, half), pl.ds(c * step, step)], e.astype(BF16))
            ot_ref[head_rows(p, half), :] = ot * (1.0 / total)
            lse_ref[0, 2 * p + half] = top + jnp.log(total)


def feed_both(x2, g3, vec_ref, wide_ref, w1, w2, out_ref, dw1_ref, dw2_ref, sums_ref, wide_sums_ref, u_ref, d_ref, df_ref, f_ref, eu_ref, r_ref):
    length, hidden = u_ref.shape
    hat3, scale3 = normalize(x2)
    gain3 = vec_ref[FEED_GAIN : FEED_GAIN + 1]
    h3 = (hat3 * gain3 + vec_ref[FEED_SHIFT : FEED_SHIFT + 1]).astype(BF16)
    u_ref[...] = mm(h3, w1[...])
    step = 16

    @pl.loop(0, length // step)
    def _(b):
        rows = pl.ds(pl.multiple_of(b * step, step), step)
        u = u_ref[rows, :] + wide_ref[0:1]
        below = 0.5 * (1.0 + lax.erf(u * 0.7071067811865476))
        d_ref[rows, :] = below + u * (jnp.exp(-0.5 * u * u) * 0.3989422804014327)
        hat, scale = normalize(u * below)
        u_ref[rows, :] = hat
        f_ref[rows, :] = (hat * wide_ref[1:2] + wide_ref[2:3]).astype(BF16)
        r_ref[rows, :] = jnp.broadcast_to(scale, (step, 128))

    x3 = x2 + mm(f_ref[...], w2[...]) + vec_ref[OUTER_BIAS : OUTER_BIAS + 1]
    out_ref[0] = x3.astype(BF16)
    sums_ref[0:1] += colsum(g3)
    e3 = g3.astype(BF16)
    dw2_ref[...] += mm_tn(f_ref[...], e3)
    df_ref[...] = mm_nt(e3, w2[...])

    @pl.loop(0, length // step)
    def _(b):
        rows = pl.ds(pl.multiple_of(b * step, step), step)
        dy, hat = df_ref[rows, :], u_ref[rows, :]
        part = dy * hat
        wide_sums_ref[0:8] += part[0:8] + part[8:16]
        wide_sums_ref[8:16] += dy[0:8] + dy[8:16]
        da = norm_back(dy, hat, r_ref[rows, 0:1], wide_ref[1:2])
        du = da * d_ref[rows, :]
        wide_sums_ref[16:24] += du[0:8] + du[8:16]
        eu_ref[rows, :] = du.astype(BF16)

    dw1_ref[...] += mm_tn(h3, eu_ref[...])
    dh3 = mm_nt(eu_ref[...], w1[...])
    sums_ref[1:2] += colsum(dh3 * hat3)
    sums_ref[2:3] += colsum(dh3)
    return g3 + norm_back(dh3, hat3, scale3, gain3)


def fwd_kernel(
    tlen_ref, mlen_ref,
    tok_ref, cot_ref, keep_ref, mem_ref, bias_ref, vec_ref, wide_ref,
    wq, wk, wv, wo, wcq, wck, wcv, wco, w1, w2,
    q1_ref, k1_ref, v1_ref, lse1_ref, ot1_ref,
    x1_ref, q2_ref, k2_ref, v2_ref, lse2_ref, delta2_ref, do2_ref, g2_ref, out_ref,
    dwco_ref, dw1_ref, dw2_ref, sums_ref, wide_out_ref,
    x1_scr, vt_scr, st_scr, ot_scr, u_scr, d_scr, df_scr, f_scr, eu_scr, r_scr, wide_scr,
):
    seqs = x1_scr.shape[0]
    t = pl.program_id(0)

    @pl.when(t == 0)
    def _():
        for ref in (dwco_ref, dw1_ref, dw2_ref, sums_ref, wide_scr):
            ref[...] = jnp.zeros_like(ref)

    @pl.when(t < seqs)
    def _():
        self_forward(
            t, tlen_ref, tok_ref, bias_ref, vec_ref, wq, wk, wv, wo,
            q1_ref, k1_ref, v1_ref, lse1_ref, ot1_ref, x1_scr.at[t], vt_scr,
        )

    @pl.when(t >= seqs)
    def _():
        s = t - seqs
        x1 = x1_scr[s]
        x1_ref[0] = x1
        cross_forward(
            s, mlen_ref, mem_ref.at[0], vec_ref, x1, wcq, wck, wcv,
            q2_ref, k2_ref, v2_ref, lse2_ref, ot_scr, vt_scr, st_scr,
        )
        hat, scale = normalize(ot_scr[...].T)
        gain = vec_ref[POST_GAIN : POST_GAIN + 1]
        c2 = (hat * gain + vec_ref[POST_SHIFT : POST_SHIFT + 1]).astype(BF16)
        x2 = x1 + mm(c2, wco[...]) + vec_ref[CROSS_OUTPUT_BIAS : CROSS_OUTPUT_BIAS + 1]
        g3 = cot_ref[0].astype(F32) * keep_ref[0]
        g2 = feed_both(
            x2, g3, vec_ref, wide_ref, w1, w2, out_ref, dw1_ref, dw2_ref, sums_ref, wide_scr,
            u_scr, d_scr, df_scr, f_scr, eu_scr, r_scr,
        )
        g2_ref[0] = g2
        sums_ref[3:4] += colsum(g2)
        e2 = g2.astype(BF16)
        dwco_ref[...] += mm_tn(c2, e2)
        dc2 = mm_nt(e2, wco[...])
        sums_ref[4:5] += colsum(dc2 * hat)
        sums_ref[5:6] += colsum(dc2)
        do2 = norm_back(dc2, hat, scale, gain)
        do2_ref[0] = do2.astype(BF16)
        prod = do2.astype(BF16).astype(F32).T * ot_scr[...]
        for h in range(lse2_ref.shape[1]):
            delta2_ref[0, h] = colsum(prod[h * 64 : (h + 1) * 64])

    @pl.when(t == 2 * seqs - 1)
    def _():
        for k in range(3):
            wide_out_ref[k : k + 1] = colsum(wide_scr[8 * k : 8 * k + 8])


def forward(tlen, mlen, tokens, cotangent, keep, mem, bias, vec, wide, weights):
    seqs, length, width = tokens.shape
    mem_total = mem.shape[1]
    heads = bias.shape[0]
    hidden = wide.shape[1]
    early = lambda t, *_: (jnp.minimum(t, seqs - 1), 0, 0)
    late = lambda t, *_: (jnp.maximum(t - seqs, 0), 0, 0)
    whole2 = lambda t, *_: (0, 0)
    const = lambda a: pl.BlockSpec(a.shape, lambda t, *_: (0,) * a.ndim, pipeline_mode=pl.Buffered(1))
    seq = lambda rows, cols, idx: pl.BlockSpec((1, rows, cols), idx)
    row = lambda idx: pl.BlockSpec((1, heads, 1, length), lambda t, *_: idx(t) + (0,))
    sds = jax.ShapeDtypeStruct
    outs = [
        (sds((seqs, length, width), BF16), seq(length, width, early)),
        (sds((seqs, length, width), BF16), seq(length, width, early)),
        (sds((seqs, length, width), BF16), seq(length, width, early)),
        (sds((seqs, heads, 1, length), F32), row(early)),
        (sds((seqs, width, length), F32), seq(width, length, early)),
        (sds((seqs, length, width), F32), seq(length, width, late)),
        (sds((seqs, length, width), BF16), seq(length, width, late)),
        (sds((seqs, mem_total, width), BF16), seq(mem_total, width, late)),
        (sds((seqs, mem_total, width), BF16), seq(mem_total, width, late)),
        (sds((seqs, heads, 1, length), F32), row(late)),
        (sds((seqs, heads, 1, length), F32), row(late)),
        (sds((seqs, length, width), BF16), seq(length, width, late)),
        (sds((seqs, length, width), F32), seq(length, width, late)),
        (sds((seqs, length, width), BF16), seq(length, width, late)),
        (sds((width, width), F32), pl.BlockSpec((width, width), whole2)),
        (sds((width, hidden), F32), pl.BlockSpec((width, hidden), whole2)),
        (sds((hidden, width), F32), pl.BlockSpec((hidden, width), whole2)),
        (sds((8, width), F32), pl.BlockSpec((8, width), whole2)),
        (sds((3, hidden), F32), pl.BlockSpec((3, hidden), whole2)),
    ]
    return pl.pallas_call(
        fwd_kernel,
        out_shape=[o[0] for o in outs],
        grid_spec=pltpu.PrefetchScalarGridSpec(
            num_scalar_prefetch=2,
            grid=(2 * seqs,),
            in_specs=[
                seq(length, width, early),
                seq(length, width, late),
                seq(length, 1, late),
                seq(mem_total, width, late),
                const(bias), const(vec), const(wide),
            ] + [const(w) for w in weights],
            out_specs=[o[1] for o in outs],
            scratch_shapes=[
                pltpu.VMEM((seqs, length, width), F32),
                pltpu.VMEM((width, mem_total), BF16),
                pltpu.VMEM((2, mem_total, length), F32),
                pltpu.VMEM((width, length), F32),
                pltpu.VMEM((length, hidden), F32),
                pltpu.VMEM((length, hidden), F32),
                pltpu.VMEM((length, hidden), F32),
                pltpu.VMEM((length, hidden), BF16),
                pltpu.VMEM((length, hidden), BF16),
                pltpu.VMEM((length, 128), F32),
                pltpu.VMEM((24, hidden), F32),
            ],
        ),
        compiler_params=pltpu.CompilerParams(vmem_limit_bytes=VMEM_LIMIT),
        name="forward",
    )(tlen, mlen, tokens, cotangent, keep, mem, bias, vec, wide, *weights)


def cross_backward(mlen, mem_ref, q_ref, k_ref, v_ref, lse_ref, delta_ref, do_ref, wck, wcv, dk_ref, dv_ref, dqt_ref, kt_ref, dmem_ref, dwck_ref, dwcv_ref, sums_ref):
    length, mem_total = q_ref.shape[0], mem_ref.shape[0]
    step = 256
    for c in range(mem_total // step):
        kt_ref[:, pl.ds(c * step, step)] = k_ref[pl.ds(c * step, step), :].T
    masks = half_masks(length)
    place = lax.broadcasted_iota(jnp.int32, (step, length), 0)

    @pl.loop(0, q_ref.shape[1] // 128)
    def _(p):
        lanes = pair_lanes(p)
        qp, dop = q_ref[:, lanes], do_ref[:, lanes]
        qms = [pick(masks[half], qp) for half in range(2)]
        doms = [pick(masks[half], dop) for half in range(2)]
        lse = [lse_ref[2 * p + half] for half in range(2)]
        delta = [delta_ref[2 * p + half] for half in range(2)]
        dqt = [jnp.zeros((64, length), F32) for half in range(2)]
        for c in range(mem_total // step):
            rows = pl.ds(c * step, step)
            kp, vp = k_ref[rows, lanes], v_ref[rows, lanes]
            outside = jnp.where(place < mlen - c * step, 0.0, NEG)
            dv = jnp.zeros((step, 128), F32)
            dk = jnp.zeros((step, 128), F32)
            for half in range(2):
                st = mm_nt(kp, qms[half]) + outside
                pt = jnp.exp(st - lse[half])
                dpt = mm_nt(vp, doms[half])
                dst = (pt * (dpt - delta[half])).astype(BF16)
                dqt[half] = dqt[half] + mm(kt_ref[head_rows(p, half), rows], dst)
                dv = dv + mm(pt.astype(BF16), doms[half])
                dk = dk + mm(dst, qms[half])
            dv_ref[rows, lanes] = dv.astype(BF16)
            dk_ref[rows, lanes] = dk.astype(BF16)
        for half in range(2):
            dqt_ref[head_rows(p, half), :] = dqt[half]

    @pl.loop(0, mem_total // step)
    def _(c):
        rows = pl.ds(pl.multiple_of(c * step, step), step)
        dk, dv = dk_ref[rows, :], dv_ref[rows, :]
        dmem_ref[rows, :] = (mm_nt(dk, wck[...]) + mm_nt(dv, wcv[...])).astype(BF16)
        sums_ref[8:9] += colsum(dv.astype(F32))

    dwck_ref[...] += mm_tn(mem_ref[...], dk_ref[...])
    dwcv_ref[...] += mm_tn(mem_ref[...], dv_ref[...])


def self_backward(tlen, bias_ref, q_ref, k_ref, v_ref, lse_ref, delta_ref, do_ref, dqt_ref, dk_ref, dv_ref, kt_ref, dbias_ref):
    length = q_ref.shape[0]
    kt_ref[:, pl.ds(0, length)] = k_ref[...].T
    key_place = lax.broadcasted_iota(jnp.int32, (length, length), 0)
    outside = jnp.where(key_place < tlen, 0.0, NEG)
    masks = half_masks(length)

    @pl.loop(0, q_ref.shape[1] // 128)
    def _(p):
        lanes = pair_lanes(p)
        qp, dop = q_ref[:, lanes], do_ref[:, lanes]
        kp, vp = k_ref[:, lanes], v_ref[:, lanes]
        dv = jnp.zeros((length, 128), F32)
        dk = jnp.zeros((length, 128), F32)
        for half in range(2):
            h = 2 * p + half
            qm, dom = pick(masks[half], qp), pick(masks[half], dop)
            st = mm_nt(kp, qm) + bias_ref[h] + outside
            pt = jnp.exp(st - lse_ref[h])
            dpt = mm_nt(vp, dom)
            dst = (pt * (dpt - delta_ref[h])).astype(BF16)
            rows = pl.ds(pl.multiple_of(h * length, length), length)
            wide_ds = dst.astype(F32)
            for tile in range(length // 128):
                dbias_ref[tile, rows, :] += wide_ds[:, tile * 128 : (tile + 1) * 128]
            dqt_ref[head_rows(p, half), :] = mm(kt_ref[head_rows(p, half), pl.ds(0, length)], dst)
            dv = dv + mm(pt.astype(BF16), dom)
            dk = dk + mm(dst, qm)
        dv_ref[:, lanes] = dv.astype(BF16)
        dk_ref[:, lanes] = dk.astype(BF16)


def bucket_totals(buckets_ref, dbias_ref, out_ref):
    length = buckets_ref.shape[0]
    heads = dbias_ref.shape[1] // length
    lo_places = lax.broadcasted_iota(jnp.int32, (32, length), 0)

    def body(b, acc):
        start = pl.multiple_of(b * 8, 8)
        rows = buckets_ref[pl.ds(start, 8), :]
        for k in range(8):
            ids = rows[k : k + 1]
            d = jnp.concatenate(
                [dbias_ref[tile, pl.ds(start + k, heads, stride=length), :] for tile in range(length // 128)], axis=1
            )
            rough = d.astype(BF16).astype(F32)
            fine = d - rough
            high = jnp.broadcast_to(ids >> 5, (heads, length))
            left = jnp.concatenate(
                [jnp.where(high == g, part, 0.0) for part in (rough, fine) for g in range(16)], axis=0
            ).astype(BF16)
            right = jnp.where(lo_places == (ids & 31), 1.0, 0.0).astype(BF16)
            acc = acc + mm_nt(left, right)
        return acc

    acc = lax.fori_loop(0, length // 8, body, jnp.zeros((2 * 16 * heads, 32), F32))
    acc = acc[: 16 * heads] + acc[16 * heads :]
    for g in range(16):
        out_ref[:, g * 32 : (g + 1) * 32] = acc[g * heads : (g + 1) * heads]


def bwd_kernel(
    tlen_ref, mlen_ref,
    tok_ref, mem_ref, bias_ref, buckets_ref, vec_ref, hs_ref,
    q1_ref, k1_ref, v1_ref, lse1_ref, ot1_ref,
    x1_ref, q2_ref, k2_ref, v2_ref, lse2_ref, delta2_ref, do2_ref, g2_ref,
    wq, wk, wv, wo, wcq, wck, wcv,
    dmem_ref, dtok_ref, dw_ref, sums_ref, table_ref,
    dk_scr, dv_scr, dqt_scr, kt_scr, dbias_scr, delta_scr, do_scr, hs_scr,
):
    t = pl.program_id(0)
    seqs = pl.num_programs(0)
    heads = lse1_ref.shape[1]
    length = tok_ref.shape[1]

    @pl.when(t == 0)
    def _():
        for ref in (dw_ref, sums_ref, dbias_scr, hs_scr):
            ref[...] = jnp.zeros_like(ref)

    cross_backward(
        mlen_ref[t], mem_ref.at[0], q2_ref.at[0], k2_ref.at[0], v2_ref.at[0], lse2_ref.at[0], delta2_ref.at[0],
        do2_ref.at[0], wck, wcv, dk_scr, dv_scr, dqt_scr, kt_scr, dmem_ref.at[0], dw_ref.at[5], dw_ref.at[6], sums_ref,
    )
    dq2 = (dqt_scr[...].T.astype(BF16).astype(F32) * 0.125).astype(BF16)
    hat2, scale2 = normalize(x1_ref[0])
    gain2 = vec_ref[CROSS_GAIN : CROSS_GAIN + 1]
    h2 = (hat2 * gain2 + vec_ref[CROSS_SHIFT : CROSS_SHIFT + 1]).astype(BF16)
    dw_ref[4] += mm_tn(h2, dq2)
    sums_ref[7:8] += colsum(dq2.astype(F32))
    dh2 = mm_nt(dq2, wcq[...])
    sums_ref[5:6] += colsum(dh2 * hat2)
    sums_ref[6:7] += colsum(dh2)
    g1 = g2_ref[0] + norm_back(dh2, hat2, scale2, gain2)
    sums_ref[4:5] += colsum(g1)
    e1 = g1.astype(BF16)
    c1t = (ot1_ref[0] * hs_ref[...]).astype(BF16)
    dw_ref[3] += mm(c1t, e1)
    dc1 = mm_nt(e1, wo[...])
    do_scr[...] = (dc1 * vec_ref[HEAD_SCALE : HEAD_SCALE + 1]).astype(BF16)
    dc1t = dc1.T
    do1t = (dc1t * hs_ref[...]).astype(BF16).astype(F32)
    for h in range(heads):
        rows = slice(h * 64, (h + 1) * 64)
        o = ot1_ref[0, rows, :]
        hs_scr[h : h + 1, :] += colsum(o * dc1t[rows])
        delta_scr[h] = colsum(o * do1t[rows])
    self_backward(
        tlen_ref[t], bias_ref, q1_ref.at[0], k1_ref.at[0], v1_ref.at[0], lse1_ref.at[0], delta_scr, do_scr,
        dqt_scr, dk_scr.at[pl.ds(0, length)], dv_scr.at[pl.ds(0, length)], kt_scr, dbias_scr,
    )
    dq1 = (dqt_scr[...].T.astype(BF16).astype(F32) * 0.125).astype(BF16)
    dk1 = dk_scr[pl.ds(0, length), :]
    dv1 = dv_scr[pl.ds(0, length), :]
    hat1, scale1 = normalize(tok_ref[0].astype(F32))
    gain1 = vec_ref[SELF_GAIN : SELF_GAIN + 1]
    h1 = (hat1 * gain1 + vec_ref[SELF_SHIFT : SELF_SHIFT + 1]).astype(BF16)
    dw_ref[0] += mm_tn(h1, dq1)
    dw_ref[1] += mm_tn(h1, dk1)
    dw_ref[2] += mm_tn(h1, dv1)
    sums_ref[2:3] += colsum(dq1.astype(F32))
    sums_ref[3:4] += colsum(dv1.astype(F32))
    dh1 = mm_nt(dq1, wq[...]) + mm_nt(dk1, wk[...]) + mm_nt(dv1, wv[...])
    sums_ref[0:1] += colsum(dh1 * hat1)
    sums_ref[1:2] += colsum(dh1)
    dtok_ref[0] = (g1 + norm_back(dh1, hat1, scale1, gain1)).astype(BF16)

    @pl.when(t == seqs - 1)
    def _():
        sums_ref[16 : 16 + heads] = jnp.broadcast_to(
            jnp.sum(hs_scr[...], axis=1, keepdims=True), (heads, sums_ref.shape[1])
        )
        bucket_totals(buckets_ref, dbias_scr, table_ref)


def backward(tlen, mlen, tokens, mem, bias, buckets_t, vec, hs_col, saved, weights):
    seqs, length, width = tokens.shape
    mem_total = mem.shape[1]
    heads = bias.shape[0]
    each = lambda t, *_: (t, 0, 0)
    const = lambda a: pl.BlockSpec(a.shape, lambda t, *_: (0,) * a.ndim, pipeline_mode=pl.Buffered(1))
    seq = lambda a: pl.BlockSpec((1,) + a.shape[1:], lambda t, *_: (t,) + (0,) * (a.ndim - 1))
    sds = jax.ShapeDtypeStruct
    whole = lambda shape: pl.BlockSpec(shape, lambda t, *_: (0,) * len(shape))
    return pl.pallas_call(
        bwd_kernel,
        out_shape=[
            sds((seqs, mem_total, width), BF16),
            sds((seqs, length, width), BF16),
            sds((7, width, width), F32),
            sds((24, width), F32),
            sds((heads, 512), F32),
        ],
        grid_spec=pltpu.PrefetchScalarGridSpec(
            num_scalar_prefetch=2,
            grid=(seqs,),
            in_specs=[seq(tokens), seq(mem), const(bias), const(buckets_t), const(vec), const(hs_col)]
            + [seq(a) for a in saved]
            + [const(w) for w in weights],
            out_specs=[
                pl.BlockSpec((1, mem_total, width), each),
                pl.BlockSpec((1, length, width), each),
                whole((7, width, width)),
                whole((24, width)),
                whole((heads, 512)),
            ],
            scratch_shapes=[
                pltpu.VMEM((mem_total, width), BF16),
                pltpu.VMEM((mem_total, width), BF16),
                pltpu.VMEM((width, length), F32),
                pltpu.VMEM((width, mem_total), BF16),
                pltpu.VMEM((length // 128, heads * length, 128), F32),
                pltpu.VMEM((heads, 1, length), F32),
                pltpu.VMEM((length, width), BF16),
                pltpu.VMEM((heads, length), F32),
            ],
        ),
        compiler_params=pltpu.CompilerParams(vmem_limit_bytes=VMEM_LIMIT),
        name="backward",
    )(tlen, mlen, tokens, mem, bias, buckets_t, vec, hs_col, *saved, *weights)


def local(
    tokens, cotangent, target_lengths, task_mask, memory_lengths, position_buckets, memory,
    self_gain, self_shift, query_weight, query_bias, key_weight, value_weight, value_bias, position_table, head_scale,
    output_weight, output_bias, cross_gain, cross_shift, cross_query, cross_query_bias, cross_key, cross_value,
    cross_value_bias, post_gain, post_shift, cross_output, cross_output_bias, feed_gain, feed_shift, inner_weight,
    inner_bias, inner_gain, inner_shift, outer_weight, outer_bias,
):
    seqs, length, width = tokens.shape
    heads = head_scale.shape[0]
    bucket_count = position_table.shape[0]
    buckets_t = position_buckets.T
    table_t = jnp.pad(position_table, ((0, 512 - bucket_count), (0, 0))).T[:, None, :]
    hs_lanes = jnp.repeat(head_scale, width // heads)
    vec = jnp.stack([
        self_gain, self_shift, query_bias, value_bias, hs_lanes, output_bias, cross_gain, cross_shift,
        cross_query_bias, cross_value_bias, post_gain, post_shift, cross_output_bias, feed_gain, feed_shift, outer_bias,
    ])
    wide = jnp.stack([inner_bias, inner_gain, inner_shift])
    keep = task_mask.astype(F32) * (jnp.arange(length)[None, :] < target_lengths[:, None]).astype(F32)
    bias = position_bias(buckets_t, table_t)
    mem = lax.all_to_all(memory, "dp", split_axis=0, concat_axis=2, tiled=True)[0]
    fwd = forward(
        target_lengths, memory_lengths, tokens, cotangent, keep[:, :, None], mem, bias, vec, wide,
        [query_weight, key_weight, value_weight, output_weight, cross_query, cross_key, cross_value, cross_output,
         inner_weight, outer_weight],
    )
    layer_output = fwd[13]
    dwco, dw1, dw2, sums_a, wide_sums = fwd[14:]
    dmem, dtok, dw, sums_b, table_sums = backward(
        target_lengths, memory_lengths, tokens, mem, bias, buckets_t, vec,
        jnp.broadcast_to(hs_lanes[:, None], (width, length)), fwd[:13],
        [query_weight, key_weight, value_weight, output_weight, cross_query, cross_key, cross_value],
    )
    memory_gradient = lax.all_to_all(dmem[None], "dp", split_axis=2, concat_axis=0, tiled=True)
    low = lambda a: a.astype(BF16)
    big = lax.psum((low(dw), low(dwco), low(dw1), low(dw2)), ("dp", "rep"))
    dw, dwco, dw1, dw2 = [a.astype(F32) for a in big]
    small = jnp.concatenate([sums_a, sums_b, table_sums, wide_sums.reshape(-1, width)], axis=0)
    small = lax.psum(small, ("dp", "rep"))
    a, b, tab, wid = small[:8], small[8:32], small[32:40], small[40:].reshape(3, -1)
    return (
        layer_output, dtok, memory_gradient,
        b[0], b[1], dw[0], b[2], dw[1], dw[2], b[3], tab[:, :bucket_count].T, b[16:24, 0],
        dw[3], b[4], b[5], b[6], dw[4], b[7], dw[5], dw[6], b[8],
        a[4], a[5], dwco, a[3], a[1], a[2], dw1, wid[2], wid[0], wid[1], dw2, a[0],
    )


def solution(mesh):
    per_seq3, per_seq2, per_seq1 = P(("dp", "rep"), None, None), P(("dp", "rep"), None), P(("dp", "rep"))
    spread = P(None, "rep", "dp", None)
    in_specs = (per_seq3, per_seq3, per_seq1, per_seq2, per_seq1, P(), spread) + (P(),) * 30
    out_specs = (per_seq3, per_seq3, spread) + (P(),) * 30
    return jax.shard_map(local, mesh=mesh, in_specs=in_specs, out_specs=out_specs, check_vma=False)
```

time: 1260 us -> 720 us (0.57); the launches traced: 1250 us -> 719 us
  matrix products: 425 us -> 0 us
  local copies, waits for them, and re-layouts: 266 us -> 33.7 us
  Pallas kernels: 0 us -> 212 us
  other arithmetic: 70.4 us -> 21.1 us
  waiting for transfers between devices: 444 us -> 425 us
    dot_general x150 -> x0, matrix products: 425 us -> none  [the longest x4 73.6 us: bias_rows(): jnp.einsum('qkb,bh->hqk', one_hot, position_table, precision=lax.Precisio...]
    pallas_call x0 -> x3, Pallas kernels: none -> 212 us  [the longest x1 107 us: forward(): pl.pallas_call(fwd_kernel, out_shape=[o[0] for o in outs], grid_spec=pltp...]
    unnamed x333 -> x71, local copies, waits for them, and re-layouts: 73.6 us -> 3.58 us
    dynamic_update_slice x24 -> x0, local copies, waits for them, and re-layouts: 63.5 us -> none  [the longest x16 56.4 us: local(): lax.map(self_backward, (heads_query, heads_key, heads_value, bias_heads,...]
    reduce_sum x44 -> x0, other arithmetic: 50.1 us -> none  [the longest x1 13.5 us: local(): sum_inner_bias = jnp.sum(grad_inner, axis=0)]
    convert_element_type x9 -> x0, local copies, waits for them, and re-layouts: 27.3 us -> none  [the longest x1 8.21 us: local(): low_key_two = merge_heads(dkey_two).astype(jnp.bfloat16)]
    reshape x8 -> x1, local copies, waits for them, and re-layouts: 24.4 us -> 0.02 us  [local(): wide_sums.reshape(-1, width)]
    psum x2, waiting for transfers between devices: 367 us -> 344 us  [the longest x1 181 us: local(): big = lax.psum((low(dw), low(dwco), low(dw1), low(dw2)), ('dp', 'rep'))]
  transfers between devices with their start and end apart: 6 -> 4, of which waited for: 4 -> 3; matrix products, arithmetic and copies ran while one was open for 37% -> 5% of each run, Pallas kernels for 0% -> 1%
where the time goes in v1:
time: 720 us; the launch traced here: 719 us
  waiting for transfers between devices  425 us (59%)
  Pallas kernels  212 us (29%)
  local copies, waits for them, and re-layouts  33.7 us (5%)
  other arithmetic  21.1 us (3%)
  between operations  14.5 us (2%)
  starting transfers between devices  12.4 us (2%)
    psum x1, waiting for transfers between devices, local(): big = lax.psum((low(dw), low(dwco), low(dw1), low(dw2)), ('dp', 'rep'))  181 us
    psum x1, waiting for transfers between devices, local(): small = lax.psum(small, ('dp', 'rep'))  163 us
    pallas_call x1, Pallas kernels, forward(): pl.pallas_call(fwd_kernel, out_shape=[o[0] for o in outs], grid_spec=pltp...  107 us
    pallas_call x1, Pallas kernels, backward(): pl.pallas_call(bwd_kernel, out_shape=[sds((seqs, mem_total, width), BF16)...  98.2 us
    all_to_all x1, waiting for transfers between devices, local(): lax.all_to_all(memory, 'dp', split_axis=0, concat_axis=2, tiled=True)[0]  80.9 us
  transfers between devices with their start and end apart: 4, of which 3 were waited for; matrix products, arithmetic and copies ran while one was open for 5% of the time, Pallas kernels for 1%

profile of v1, /device:TPU:0, one launch (start us, length us, event | category | flops | bytes accessed | tf_op | source)
XLA Modules:
  0.0 718.6 jit_solution(5652600215366569370)
XLA Ops:
  7.5 7.4 %all-to-all-start = ((bf16[8,4,128,512]{3,2,1,0:T(8,128)(2,1)}), bf16[8,4,128,512]{3,2,1,0:T(8,128)(2,1)}, u32[]{:S(2)}, u32[]{:S(2)}) async-start(bf16[8,4,128,512]{3,2,1,0:T(8,128)(2,1)} %param.43), calls=%async_computation | async-start | bytes 8388608 | tf_op jit(solution)/shard_map/all_to_all | solution.py:610
  18.2 6.9 position_bias.1.bias_ref
  25.3 1.3 stack.75.vec_ref
  27.2 80.9 %all-to-all-done = bf16[8,4,128,512]{3,2,1,0:T(8,128)(2,1)} async-done(((bf16[8,4,128,512]{3,2,1,0:T(8,128)(2,1)}), bf16[8,4,128,512]{3,2,1,0:T(8,128)(2,1)}, u32[]{:S(2)}, u32[]{:S(2)}) %all-to-all-start) | async-done | bytes 4194336 | tf_op jit(solution)/shard_map/all_to_all | solution.py:610
  108.1 4.6 copy.77
  112.8 107.1 %forward.1 = (bf16[4,256,512]{2,1,0:T(8,128)(2,1)}, bf16[4,256,512]{2,1,0:T(8,128)(2,1)}, bf16[4,256,512]{2,1,0:T(8,128)(2,1)}, f32[4,8,1,256]{3,2,1,0:T(1,128)}...) custom-call(s32[4]{0:T(128)} %tlen_ref.3, ...), custom_call_target="tpu_custom_call" | custom-call | tf_op jit(solution)/shard_map/forward/pallas_call | solution.py:328
  219.9 1.6 broadcast_in_dim.25.hs_ref
  221.5 98.2 %backward.1 = (bf16[4,1024,512]{2,1,0:T(8,128)(2,1)}, bf16[4,256,512]{2,1,0:T(8,128)(2,1)}, f32[7,512,512]{2,1,0:T(8,128)}, f32[24,512]{1,0:T(8,128)}, f32[8,512]{1,0:T(8,128)}) custom-call(s32[4]{0:T(128)} %tlen_ref.3, s32[4]{0:T(128)} %mlen_ref.3, bf16[4,256,512]{2,1,0:T(8,128)(2,1)} %tok_ref.3, bf16[4,1024,512]{2,1,0:T(8,128)(2,1)} %bitcast.75, ...), custom_call_target="tpu_custom_call" | custom-call | tf_op jit(solution)/shard_map/backward/pallas_call | solution.py:552
  319.7 7.4 %copy.80 = bf16[1,4,1024,512]{3,1,0,2:T(4,128)(2,1)} copy(bf16[1,4,1024,512]{3,2,1,0:T(8,128)(2,1)} %bitcast.79) | data formatting | bytes 8388608 | tf_op jit(solution)/shard_map/broadcast_in_dim | solution.py:623
  327.1 4.7 all-to-all-start.1
  333.8 4.5 convert_element_type.35
  338.2 1.6 convert_element_type.37
  339.9 2.3 convert_element_type.31
  342.2 162.9 %all-reduce.5.cloned.1.call-done = f32[52,512]{1,0:T(8,128)} async-done(((f32[52,512]{1,0:T(8,128)}), f32[52,512]{1,0:T(8,128)}) %all-reduce.5.cloned.1.call-update) | async-done | bytes 106512 | tf_op jit(solution)/shard_map/psum | solution.py:628
  507.8 1.3 slice_reduce_fusion
  509.1 1.3 slice_bitcast_fusion.7
  510.4 1.7 fusion
  512.1 180.8 %all-reduce.7.cloned.1.call-done = (bf16[7,512,512]{2,1,0:T(8,128)(2,1)}, bf16[512,512]{1,0:T(8,128)(2,1)}, bf16[512,2048]{1,0:T(8,128)(2,1)}, bf16[2048,512]{1,0:T(8,128)(2,1)}) async-done(((bf16[7,512,512]{2,1,0:T(8,128)(2,1)}, bf16[512,512]{1,0:T(8,128)(2,1)}, bf16[512,2048]{1,0:T(8,128)(2,1)}, bf16[2048,512]{1,0:T(8,128)(2,1)}), (bf16[7,512,512]{2,1,0:T(8,128)(2,1)}, bf16[512,512]{1,0:T(8,128)(2,1)}, ...) | async-done | bytes 8388624 | tf_op jit(solution)/shard_map/psum | solution.py:625
  692.9 2.1 convert_element_type.34
  695.1 3.2 convert_element_type.32
  698.3 2.5 convert_element_type.36
  700.8 2.6 convert_element_type.38
  703.4 3.1 slice_bitcast_fusion
  706.5 5.3 copy.86
  (88 shorter events, 8.6 us)
Async XLA Ops:
  7.3 9.9 %copy-start.13 = (s32[4]{0:T(128)S(1)}, s32[4]{0:T(128)}, u32[]{:S(2)}) copy-start(s32[4]{0:T(128)} %tlen_ref.3) | copy-start | bytes 52
  7.3 9.9 %copy-start.14 = (s32[4,256]{1,0:T(4,128)S(1)}, s32[4,256]{1,0:T(4,128)}, u32[]{:S(2)}) copy-start(s32[4,256]{1,0:T(4,128)} %param.40) | copy-start | bytes 12292
  7.3 17.9 %copy-start.29 = (f32[512]{0:T(512)S(1)}, f32[512]{0:T(512)}, u32[]{:S(2)}) copy-start(f32[512]{0:T(512)} %param.73) | copy-start | bytes 6148
  7.3 17.9 %copy-start.28 = (f32[512]{0:T(512)S(1)}, f32[512]{0:T(512)}, u32[]{:S(2)}) copy-start(f32[512]{0:T(512)} %param.67) | copy-start | bytes 6148
  7.3 17.9 %copy-start.27 = (f32[512]{0:T(512)S(1)}, f32[512]{0:T(512)}, u32[]{:S(2)}) copy-start(f32[512]{0:T(512)} %param.66) | copy-start | bytes 6148
  7.3 17.9 %copy-start.26 = (f32[512]{0:T(512)S(1)}, f32[512]{0:T(512)}, u32[]{:S(2)}) copy-start(f32[512]{0:T(512)} %param.65) | copy-start | bytes 6148
  7.3 17.9 %copy-start.25 = (f32[512]{0:T(512)S(1)}, f32[512]{0:T(512)}, u32[]{:S(2)}) copy-start(f32[512]{0:T(512)} %param.63) | copy-start | bytes 6148
  7.3 17.9 %copy-start.24 = (f32[512]{0:T(512)S(1)}, f32[512]{0:T(512)}, u32[]{:S(2)}) copy-start(f32[512]{0:T(512)} %param.62) | copy-start | bytes 6148
  7.3 17.9 %copy-start.23 = (f32[512]{0:T(512)S(1)}, f32[512]{0:T(512)}, u32[]{:S(2)}) copy-start(f32[512]{0:T(512)} %param.61) | copy-start | bytes 6148
  7.3 17.9 %copy-start.22 = (f32[512]{0:T(512)S(1)}, f32[512]{0:T(512)}, u32[]{:S(2)}) copy-start(f32[512]{0:T(512)} %param.58) | copy-start | bytes 6148
  7.4 17.9 %copy-start.21 = (f32[512]{0:T(512)S(1)}, f32[512]{0:T(512)}, u32[]{:S(2)}) copy-start(f32[512]{0:T(512)} %param.56) | copy-start | bytes 6148
  7.4 17.9 %copy-start.20 = (f32[512]{0:T(512)S(1)}, f32[512]{0:T(512)}, u32[]{:S(2)}) copy-start(f32[512]{0:T(512)} %param.55) | copy-start | bytes 6148
  7.4 17.9 %copy-start.19 = (f32[512]{0:T(512)S(1)}, f32[512]{0:T(512)}, u32[]{:S(2)}) copy-start(f32[512]{0:T(512)} %param.54) | copy-start | bytes 6148
  7.4 17.9 %copy-start.18 = (f32[512]{0:T(512)S(1)}, f32[512]{0:T(512)}, u32[]{:S(2)}) copy-start(f32[512]{0:T(512)} %param.50) | copy-start | bytes 6148
  7.4 17.9 %copy-start.17 = (f32[512]{0:T(512)S(1)}, f32[512]{0:T(512)}, u32[]{:S(2)}) copy-start(f32[512]{0:T(512)} %param.47) | copy-start | bytes 6148
  7.4 17.9 %copy-start.16 = (f32[512]{0:T(512)S(1)}, f32[512]{0:T(512)}, u32[]{:S(2)}) copy-start(f32[512]{0:T(512)} %param.45) | copy-start | bytes 6148
  7.4 17.9 %copy-start.15 = (f32[512]{0:T(512)S(1)}, f32[512]{0:T(512)}, u32[]{:S(2)}) copy-start(f32[512]{0:T(512)} %param.44) | copy-start | bytes 6148
  7.4 19.1 %copy-start.10 = (f32[2048]{0:T(1024)S(1)}, f32[2048]{0:T(1024)}, u32[]{:S(2)}) copy-start(f32[2048]{0:T(1024)} %param.71) | copy-start | bytes 24580
  7.4 19.1 %copy-start.11 = (f32[2048]{0:T(1024)S(1)}, f32[2048]{0:T(1024)}, u32[]{:S(2)}) copy-start(f32[2048]{0:T(1024)} %param.70) | copy-start | bytes 24580
  7.4 19.1 %copy-start.12 = (f32[2048]{0:T(1024)S(1)}, f32[2048]{0:T(1024)}, u32[]{:S(2)}) copy-start(f32[2048]{0:T(1024)} %param.69) | copy-start | bytes 24580
  7.5 100.7 %all-to-all-start = ((bf16[8,4,128,512]{3,2,1,0:T(8,128)(2,1)}), bf16[8,4,128,512]{3,2,1,0:T(8,128)(2,1)}, u32[]{:S(2)}, u32[]{:S(2)}) async-start(bf16[8,4,128,512]{3,2,1,0:T(8,128)(2,1)} %param.43), calls=%async_computation | async-start | bytes 8388608 | tf_op jit(solution)/shard_map/all_to_all | solution.py:610
  327.1 379.4 %all-to-all-start.1 = ((bf16[1,4,1024,512]{3,1,0,2:T(4,128)(2,1)}), bf16[1,4,1024,512]{3,1,0,2:T(4,128)(2,1)}, u32[]{:S(2)}, u32[]{:S(2)}) async-start(bf16[1,4,1024,512]{3,1,0,2:T(4,128)(2,1)} %copy.80), calls=%async_computation.1 | async-start | bytes 8388608 | tf_op jit(solution)/shard_map/all_to_all | solution.py:623
  331.8 173.3 %all-reduce.5.cloned.1.call-start = ((), (), s32[]{:S(2)}) async-start(), calls=%async_computation.2 | async-start | bytes 229376 | tf_op jit(solution)/shard_map/psum | solution.py:628
  332.6 360.3 %all-reduce.7.cloned.1.call-start = ((), (), s32[]{:S(2)}) async-start(), calls=%async_computation.3 | async-start | bytes 16777216 | tf_op jit(solution)/shard_map/psum | solution.py:625
  (13 other events, 74.4 us)
Sparse Core Ops, SparseCore 0:
  338.8 166.3 all-reduce.4
  512.4 180.4 all-reduce.6

commit v2 on v1

v2 whole, which is shorter than its diff:
```python
import functools

import jax
import jax.numpy as jnp
from jax import lax
from jax.experimental import pallas as pl
from jax.experimental.pallas import tpu as pltpu
from jax.sharding import PartitionSpec as P

NEG = -1e30
F32 = jnp.float32
BF16 = jnp.bfloat16
VMEM_LIMIT = 67043328

(
    SELF_GAIN,
    SELF_SHIFT,
    QUERY_BIAS,
    VALUE_BIAS,
    HEAD_SCALE,
    OUTPUT_BIAS,
    CROSS_GAIN,
    CROSS_SHIFT,
    CROSS_QUERY_BIAS,
    CROSS_VALUE_BIAS,
    POST_GAIN,
    POST_SHIFT,
    CROSS_OUTPUT_BIAS,
    FEED_GAIN,
    FEED_SHIFT,
    OUTER_BIAS,
) = range(16)


def mm(a, b):
    return jnp.dot(a, b, preferred_element_type=F32)


def mm_nt(a, b):
    return lax.dot_general(a, b, (((1,), (1,)), ((), ())), preferred_element_type=F32)


def mm_tn(a, b):
    return lax.dot_general(a, b, (((0,), (0,)), ((), ())), preferred_element_type=F32)


def normalize(x):
    center = x - jnp.mean(x, axis=-1, keepdims=True)
    spread = jnp.mean(center * center, axis=-1, keepdims=True)
    scale = lax.rsqrt(spread + 1e-05)
    return center * scale, scale


def norm_back(dy, hat, scale, gain):
    w = dy * gain
    first = jnp.mean(w, axis=-1, keepdims=True)
    second = jnp.mean(w * hat, axis=-1, keepdims=True)
    return (w - first - hat * second) * scale


def colsum(x):
    return jnp.sum(x, axis=0, keepdims=True)


def half_masks(rows):
    lane = lax.broadcasted_iota(jnp.int32, (rows, 128), 1)
    return (lane < 64, lane >= 64)


def pick(mask, x):
    return jnp.where(mask, x.astype(F32), 0.0).astype(BF16)


def pair_lanes(p):
    return pl.ds(pl.multiple_of(p * 128, 128), 128)


def head_rows(p, half):
    return pl.ds(pl.multiple_of(p * 128 + half * 64, 64), 64)


def fill_bias(buckets, table_rows, out_ref):
    length = buckets.shape[0]
    chunks = table_rows.shape[2] // 128
    ids_t = buckets.T
    low, high = ids_t & 127, ids_t >> 7
    key_place = lax.broadcasted_iota(jnp.int32, (length, 128), 0)
    lane = lax.broadcasted_iota(jnp.int32, (length, 128), 1)

    @pl.loop(0, out_ref.shape[0])
    def _(h):
        rows = [jnp.broadcast_to(table_rows[h, :, pl.ds(c * 128, 128)], (length, 128)) for c in range(chunks)]
        for tile in range(length // 128):
            cols = slice(tile * 128, (tile + 1) * 128)
            total = jnp.zeros((length, 128), F32)
            for c in range(chunks):
                got = jnp.take_along_axis(rows[c], low[:, cols], axis=1, mode="promise_in_bounds")
                total = jnp.where(high[:, cols] == c, got, total)
            out_ref[h, :, pl.ds(tile * 128, 128)] = jnp.where(key_place <= lane + tile * 128, total, NEG)


def axis_bits(sizes):
    return [(axis, bit) for axis in ("rep", "dp") for bit in range(sizes[axis].bit_length() - 1)]


def stage_orders(sizes):
    plain = axis_bits(sizes)
    reps = sizes["rep"].bit_length() - 1
    swapped = list(plain)
    if reps >= 2 and len(plain) > reps:
        swapped = plain[: reps - 1] + [plain[reps], plain[reps - 1]] + plain[reps + 1 :]
    return plain, swapped


class Reduction:
    def __init__(self, buf, land, start, rows, land_start, stages, tile, send, recv, free):
        self.buf, self.land, self.tile, self.send, self.recv, self.free = buf, land, tile, send, recv, free
        self.plan = []
        base, span, at = start, rows, land_start
        for axis, bit in stages:
            place = lax.axis_index(axis)
            mine = (place // 2**bit) % 2
            peer = {axis: place + (1 - 2 * mine) * 2**bit}
            halve = span % (2 * tile) == 0
            size = span // 2 if halve else span
            keep = base + mine * size if halve else base
            give = base + (1 - mine) * size if halve else base
            mark = len(self.plan)
            self.plan.append(("fold", peer, give, keep, size, at, mark if halve else None))
            at += size
            if halve:
                self.plan.append(("spread", peer, keep, base, size, None, mark))
            base, span = keep, size
        folds = [p for p in self.plan if p[0] == "fold"]
        spreads = [p for p in self.plan if p[0] == "spread"]
        self.plan = folds + spreads[::-1]
        self.land_rows = at - land_start

    def __len__(self):
        return len(self.plan)

    def rows(self, start, size):
        return pl.ds(start if isinstance(start, int) else pl.multiple_of(start, self.tile), size)

    def copy(self, k):
        kind, peer, give, keep, size, at, mark = self.plan[k]
        source = self.buf.at[self.rows(give, size)]
        target = self.land.at[self.rows(at, size)] if kind == "fold" else source
        return pltpu.make_async_remote_copy(
            src_ref=source, dst_ref=target, send_sem=self.send.at[k], recv_sem=self.recv.at[k],
            device_id=peer, device_id_type=pl.DeviceIdType.MESH,
        )

    def start(self, k):
        if k < len(self):
            if self.plan[k][0] == "spread":
                pl.semaphore_wait(self.free.at[self.plan[k][6]], 1)
            self.copy(k).start()

    def finish(self, k):
        if k >= len(self):
            return
        kind, peer, give, keep, size, at, mark = self.plan[k]
        self.copy(k).wait()
        if kind == "fold":
            if mark is not None:
                pl.semaphore_signal(
                    self.free.at[mark], inc=1, device_id=peer, device_id_type=pl.DeviceIdType.MESH
                )
            step = next(c for c in (128, 64, 48, 32, 16, 8) if size % c == 0)

            @pl.loop(0, size // step)
            def _(b):
                kept = pl.ds(pl.multiple_of(keep + b * step, self.tile), step)
                came = pl.ds(pl.multiple_of(at + b * step, self.tile), step)
                total = self.buf[kept, :].astype(F32) + self.land[came, :].astype(F32)
                self.buf[kept, :] = total.astype(self.buf.dtype)

    def advance(self, k):
        if 0 < k <= len(self):
            self.finish(k - 1)
        self.start(k)


def land_rows(rows, stages, tile):
    span, total = rows, 0
    for _ in stages:
        span = span // 2 if span % (2 * tile) == 0 else span
        total += span
    return total


def meet(peers):
    barrier = pltpu.get_barrier_semaphore()
    for peer in peers:
        pl.semaphore_signal(barrier, inc=1, device_id=peer, device_id_type=pl.DeviceIdType.MESH)
    pl.semaphore_wait(barrier, len(peers))


def scaled_heads(value_t, hs_ref):
    return jnp.concatenate([value_t[h * 64 : (h + 1) * 64] * hs_ref[h] for h in range(value_t.shape[0] // 64)], axis=0)


def self_forward(s, tlen_ref, hs_ref, tok_ref, bias_ref, vec_ref, wq, wk, wv, wo, q_ref, k_ref, v_ref, lse_ref, ot_ref, x1_ref, vt_ref):
    length = tok_ref.shape[1]
    x0 = tok_ref[0].astype(F32)
    hat, _ = normalize(x0)
    h1 = (hat * vec_ref[SELF_GAIN][...] + vec_ref[SELF_SHIFT][...]).astype(BF16)
    q_ref[0] = ((mm(h1, wq[...]) + vec_ref[QUERY_BIAS][...]) * 0.125).astype(BF16)
    k_ref[0] = mm(h1, wk[...]).astype(BF16)
    value = (mm(h1, wv[...]) + vec_ref[VALUE_BIAS][...]).astype(BF16)
    v_ref[0] = value
    vt_ref[:, pl.ds(0, length)] = value.T
    key_place = lax.broadcasted_iota(jnp.int32, (length, length), 0)
    outside = jnp.where(key_place < tlen_ref[s], 0.0, NEG)
    masks = half_masks(length)

    @pl.loop(0, q_ref.shape[2] // 128)
    def _(p):
        lanes = pair_lanes(p)
        kp, qp = k_ref[0, :, lanes], q_ref[0, :, lanes]
        for half in range(2):
            st = mm_nt(kp, pick(masks[half], qp)) + bias_ref[2 * p + half] + outside
            top = jnp.max(st, axis=0, keepdims=True)
            e = jnp.exp(st - top)
            total = colsum(e)
            ot = mm(vt_ref[head_rows(p, half), pl.ds(0, length)], e.astype(BF16))
            ot_ref[0, head_rows(p, half), :] = ot * (1.0 / total)
            lse_ref[0, 2 * p + half] = top + jnp.log(total)

    c1 = scaled_heads(ot_ref[0], hs_ref).T.astype(BF16)
    x1_ref[...] = x0 + mm(c1, wo[...]) + vec_ref[OUTPUT_BIAS][...]


def cross_forward(s, mlen_ref, mem_ref, vec_ref, x1, wcq, wck, wcv, q_ref, k_ref, v_ref, lse_ref, ot_ref, vt_ref, st_ref):
    length, mem_total = x1.shape[0], mem_ref.shape[0]
    hat, _ = normalize(x1)
    h2 = (hat * vec_ref[CROSS_GAIN][...] + vec_ref[CROSS_SHIFT][...]).astype(BF16)
    q_ref[0] = ((mm(h2, wcq[...]) + vec_ref[CROSS_QUERY_BIAS][...]) * 0.125).astype(BF16)
    step = 256

    @pl.loop(0, mem_total // step)
    def _(c):
        rows = pl.ds(pl.multiple_of(c * step, step), step)
        part = mem_ref[rows, :]
        k_ref[0, rows, :] = mm(part, wck[...]).astype(BF16)
        v_ref[0, rows, :] = (mm(part, wcv[...]) + vec_ref[CROSS_VALUE_BIAS][...]).astype(BF16)

    for c in range(mem_total // step):
        vt_ref[:, pl.ds(c * step, step)] = v_ref[0, pl.ds(c * step, step), :].T
    masks = half_masks(length)
    place = lax.broadcasted_iota(jnp.int32, (step, length), 0)

    @pl.loop(0, q_ref.shape[2] // 128)
    def _(p):
        lanes = pair_lanes(p)
        qp = q_ref[0, :, lanes]
        for half in range(2):
            qm = pick(masks[half], qp)
            top = jnp.full((1, length), -jnp.inf, F32)
            for c in range(mem_total // step):
                rows = pl.ds(c * step, step)
                st = mm_nt(k_ref[0, rows, lanes], qm)
                st = st + jnp.where(place < mlen_ref[s] - c * step, 0.0, NEG)
                st_ref[half, rows, :] = st
                top = jnp.maximum(top, jnp.max(st, axis=0, keepdims=True))
            total = jnp.zeros((1, length), F32)
            ot = jnp.zeros((64, length), F32)
            for c in range(mem_total // step):
                e = jnp.exp(st_ref[half, pl.ds(c * step, step), :] - top)
                total = total + colsum(e)
                ot = ot + mm(vt_ref[head_rows(p, half), pl.ds(c * step, step)], e.astype(BF16))
            ot_ref[head_rows(p, half), :] = ot * (1.0 / total)
            lse_ref[0, 2 * p + half] = top + jnp.log(total)


def feed_both(x2, g3, vec_ref, wide_ref, w1, w2, out_ref, dw1_ref, dw2_ref, sums_ref, wide_sums_ref, u_ref, d_ref, df_ref, f_ref, eu_ref, r_ref):
    length, hidden = u_ref.shape
    hat3, scale3 = normalize(x2)
    gain3 = vec_ref[FEED_GAIN][...]
    h3 = (hat3 * gain3 + vec_ref[FEED_SHIFT][...]).astype(BF16)
    u_ref[...] = mm(h3, w1[...])
    step = 16

    @pl.loop(0, length // step)
    def _(b):
        rows = pl.ds(pl.multiple_of(b * step, step), step)
        u = u_ref[rows, :] + wide_ref[0][...]
        below = 0.5 * (1.0 + lax.erf(u * 0.7071067811865476))
        d_ref[rows, :] = below + u * (jnp.exp(-0.5 * u * u) * 0.3989422804014327)
        hat, scale = normalize(u * below)
        u_ref[rows, :] = hat
        f_ref[rows, :] = (hat * wide_ref[1][...] + wide_ref[2][...]).astype(BF16)
        r_ref[rows, :] = jnp.broadcast_to(scale, (step, 128))

    x3 = x2 + mm(f_ref[...], w2[...]) + vec_ref[OUTER_BIAS][...]
    out_ref[0] = x3.astype(BF16)
    sums_ref[0:1] += colsum(g3)
    e3 = g3.astype(BF16)
    dw2_ref[...] += mm_tn(f_ref[...], e3)
    df_ref[...] = mm_nt(e3, w2[...])

    @pl.loop(0, length // step)
    def _(b):
        rows = pl.ds(pl.multiple_of(b * step, step), step)
        dy, hat = df_ref[rows, :], u_ref[rows, :]
        part = dy * hat
        wide_sums_ref[0:8] += part[0:8] + part[8:16]
        wide_sums_ref[8:16] += dy[0:8] + dy[8:16]
        da = norm_back(dy, hat, r_ref[rows, 0:1], wide_ref[1][...])
        du = da * d_ref[rows, :]
        wide_sums_ref[16:24] += du[0:8] + du[8:16]
        eu_ref[rows, :] = du.astype(BF16)

    dw1_ref[...] += mm_tn(h3, eu_ref[...])
    dh3 = mm_nt(eu_ref[...], w1[...])
    sums_ref[1:2] += colsum(dh3 * hat3)
    sums_ref[2:3] += colsum(dh3)
    return g3 + norm_back(dh3, hat3, scale3, gain3)


def fwd_kernel(
    tlen_ref, mlen_ref, hs_ref,
    tok_ref, cot_ref, mask_ref, buckets_ref, table_ref, mem_hbm, *rest,
):
    vec_ref, wide_ref, rest = rest[:16], rest[16:19], rest[19:]
    wq, wk, wv, wo, wcq, wck, wcv, wco, w1, w2 = rest[:10]
    (
    q1_ref, k1_ref, v1_ref, lse1_ref, ot1_ref,
    x1_ref, q2_ref, k2_ref, v2_ref, lse2_ref, delta2_ref, do2_ref, g2_ref, out_ref,
    gathered_hbm, packed_hbm, bias_hbm, sums_ref, wide_out_ref,
    mem_scr, packed_scr, dwco_ref, dw1_ref, dw2_ref, bias_ref, table_scr,
    x1_scr, vt_scr, st_scr, ot_scr, u_scr, d_scr, df_scr, f_scr, eu_scr, r_scr, wide_scr,
    send_sem, recv_sem, own_sem, out_sem,
    ) = rest[10:]
    seqs = x1_scr.shape[0]
    t = pl.program_id(0)
    places, _, piece, _ = mem_hbm.shape[0], mem_hbm.shape[1], mem_hbm.shape[2], mem_hbm.shape[3]
    me = lax.axis_index("dp")
    mine = pl.ds(pl.multiple_of(me * piece, piece), piece)
    others = pl.ds(0, (places - 1) * piece)

    def own(s):
        return pltpu.make_async_copy(mem_hbm.at[me, s], mem_scr.at[s, mine], own_sem.at[s])

    def save(s):
        return pltpu.make_async_copy(mem_scr.at[s], gathered_hbm.at[s], out_sem.at[s])

    def pack():
        return pltpu.make_async_copy(packed_scr, packed_hbm, out_sem.at[seqs])

    def keep_bias():
        return pltpu.make_async_copy(bias_ref, bias_hbm, out_sem.at[seqs + 1])

    def to_peer(k, s):
        peer = lax.rem(me + k, places)
        return pltpu.make_async_remote_copy(
            src_ref=mem_hbm.at[peer, s], dst_ref=mem_scr.at[s, mine], send_sem=send_sem.at[s], recv_sem=recv_sem.at[s],
            device_id={"dp": peer}, device_id_type=pl.DeviceIdType.MESH,
        )

    def all_peers(s):
        return pltpu.make_async_remote_copy(
            src_ref=mem_scr.at[s, others], dst_ref=mem_scr.at[s, others], send_sem=send_sem.at[s],
            recv_sem=recv_sem.at[s], device_id={"dp": lax.rem(me + 1, places)}, device_id_type=pl.DeviceIdType.MESH,
        )

    @pl.when(t == 0)
    def _():
        for s in range(seqs):
            own(s).start()
        if places > 1:
            meet([{"dp": lax.rem(me + k, places)} for k in range(1, places)])
            for s in range(seqs):

                @pl.loop(1, places)
                def _(k):
                    to_peer(k, s).start()

    @pl.when(t == 0)
    def _():
        for ref in (dwco_ref, dw1_ref, dw2_ref, sums_ref, wide_scr):
            ref[...] = jnp.zeros_like(ref)
        for h in range(table_scr.shape[0]):
            table_scr[h] = table_ref[h : h + 1, :]
        fill_bias(buckets_ref[...], table_scr, bias_ref)
        keep_bias().start()

    @pl.when(t < seqs)
    def _():
        self_forward(
            t, tlen_ref, hs_ref, tok_ref, bias_ref, vec_ref, wq, wk, wv, wo,
            q1_ref, k1_ref, v1_ref, lse1_ref, ot1_ref, x1_scr.at[t], vt_scr,
        )

    @pl.when(t >= seqs)
    def _():
        s = t - seqs
        own(s).wait()
        if places > 1:
            all_peers(s).wait_recv()
        save(s).start()
        x1 = x1_scr[s]
        x1_ref[0] = x1
        cross_forward(
            s, mlen_ref, mem_scr.at[s], vec_ref, x1, wcq, wck, wcv,
            q2_ref, k2_ref, v2_ref, lse2_ref, ot_scr, vt_scr, st_scr,
        )
        hat, scale = normalize(ot_scr[...].T)
        gain = vec_ref[POST_GAIN][...]
        c2 = (hat * gain + vec_ref[POST_SHIFT][...]).astype(BF16)
        x2 = x1 + mm(c2, wco[...]) + vec_ref[CROSS_OUTPUT_BIAS][...]
        length = cot_ref.shape[1]
        here = lax.broadcasted_iota(jnp.int32, mask_ref.shape, 0) == s
        row = jnp.sum(jnp.where(here, mask_ref[...], 0), axis=0, keepdims=True).astype(F32)
        row = jnp.where(lax.broadcasted_iota(jnp.int32, (1, length), 1) < tlen_ref[s], row, 0.0)
        keep = jnp.broadcast_to(row, (8, length)).T[:, 0:1]
        g3 = cot_ref[0].astype(F32) * keep
        g2 = feed_both(
            x2, g3, vec_ref, wide_ref, w1, w2, out_ref, dw1_ref, dw2_ref, sums_ref, wide_scr,
            u_scr, d_scr, df_scr, f_scr, eu_scr, r_scr,
        )
        g2_ref[0] = g2
        sums_ref[3:4] += colsum(g2)
        e2 = g2.astype(BF16)
        dwco_ref[...] += mm_tn(c2, e2)
        dc2 = mm_nt(e2, wco[...])
        sums_ref[4:5] += colsum(dc2 * hat)
        sums_ref[5:6] += colsum(dc2)
        do2 = norm_back(dc2, hat, scale, gain)
        do2_ref[0] = do2.astype(BF16)
        prod = do2.astype(BF16).astype(F32).T * ot_scr[...]
        for h in range(lse2_ref.shape[1]):
            delta2_ref[0, h] = colsum(prod[h * 64 : (h + 1) * 64])

    @pl.when(t == 2 * seqs - 1)
    def _():
        width, hidden = dw1_ref.shape
        for k in range(3):
            wide_out_ref[k : k + 1] = colsum(wide_scr[8 * k : 8 * k + 8])
        for c in range(hidden // width):
            packed_scr[pl.ds(c * width, width), :] = dw1_ref[:, pl.ds(c * width, width)].astype(BF16)
        packed_scr[pl.ds(hidden, hidden), :] = dw2_ref[...].astype(BF16)
        packed_scr[pl.ds(2 * hidden, width), :] = dwco_ref[...].astype(BF16)
        pack().start()
        for s in range(seqs):
            if places > 1:
                all_peers(s).wait_send()
            save(s).wait()
        pack().wait()
        keep_bias().wait()


def forward(tlen, mlen, head_scale, tokens, cotangent, mask, buckets, table, mem, vecs, wides, weights):
    seqs, length, width = tokens.shape
    mem_total = mem.shape[0] * mem.shape[2]
    heads = head_scale.shape[0]
    hidden = wides[0].shape[1]
    early = lambda t, *_: (jnp.minimum(t, seqs - 1), 0, 0)
    late = lambda t, *_: (jnp.maximum(t - seqs, 0), 0, 0)
    whole2 = lambda t, *_: (0, 0)
    const = lambda a: pl.BlockSpec(a.shape, lambda t, *_: (0,) * a.ndim, pipeline_mode=pl.Buffered(1))
    seq = lambda rows, cols, idx: pl.BlockSpec((1, rows, cols), idx)
    row = lambda idx: pl.BlockSpec((1, heads, 1, length), lambda t, *_: idx(t) + (0,))
    sds = jax.ShapeDtypeStruct
    outs = [
        (sds((seqs, length, width), BF16), seq(length, width, early)),
        (sds((seqs, length, width), BF16), seq(length, width, early)),
        (sds((seqs, length, width), BF16), seq(length, width, early)),
        (sds((seqs, heads, 1, length), F32), row(early)),
        (sds((seqs, width, length), F32), seq(width, length, early)),
        (sds((seqs, length, width), F32), seq(length, width, late)),
        (sds((seqs, length, width), BF16), seq(length, width, late)),
        (sds((seqs, mem_total, width), BF16), seq(mem_total, width, late)),
        (sds((seqs, mem_total, width), BF16), seq(mem_total, width, late)),
        (sds((seqs, heads, 1, length), F32), row(late)),
        (sds((seqs, heads, 1, length), F32), row(late)),
        (sds((seqs, length, width), BF16), seq(length, width, late)),
        (sds((seqs, length, width), F32), seq(length, width, late)),
        (sds((seqs, length, width), BF16), seq(length, width, late)),
        (sds((seqs, mem_total, width), BF16), pl.BlockSpec(memory_space=pl.ANY)),
        (sds((2 * hidden + width, width), BF16), pl.BlockSpec(memory_space=pl.ANY)),
        (sds((heads, length, length), F32), pl.BlockSpec(memory_space=pl.ANY)),
        (sds((8, width), F32), pl.BlockSpec((8, width), whole2)),
        (sds((3, hidden), F32), pl.BlockSpec((3, hidden), whole2)),
    ]
    return pl.pallas_call(
        fwd_kernel,
        out_shape=[o[0] for o in outs],
        grid_spec=pltpu.PrefetchScalarGridSpec(
            num_scalar_prefetch=3,
            grid=(2 * seqs,),
            in_specs=[
                seq(length, width, early),
                seq(length, width, late),
                const(mask), const(buckets), const(table),
                pl.BlockSpec(memory_space=pl.ANY),
            ] + [const(a) for a in vecs + wides + weights],
            out_specs=[o[1] for o in outs],
            scratch_shapes=[
                pltpu.VMEM((seqs, mem_total, width), BF16),
                pltpu.VMEM((2 * hidden + width, width), BF16),
                pltpu.VMEM((width, width), F32),
                pltpu.VMEM((width, hidden), F32),
                pltpu.VMEM((hidden, width), F32),
                pltpu.VMEM((heads, length, length), F32),
                pltpu.VMEM((heads, 1, table.shape[1]), F32),
                pltpu.VMEM((seqs, length, width), F32),
                pltpu.VMEM((width, mem_total), BF16),
                pltpu.VMEM((2, mem_total, length), F32),
                pltpu.VMEM((width, length), F32),
                pltpu.VMEM((length, hidden), F32),
                pltpu.VMEM((length, hidden), F32),
                pltpu.VMEM((length, hidden), F32),
                pltpu.VMEM((length, hidden), BF16),
                pltpu.VMEM((length, hidden), BF16),
                pltpu.VMEM((length, 128), F32),
                pltpu.VMEM((24, hidden), F32),
                pltpu.SemaphoreType.DMA((seqs,)),
                pltpu.SemaphoreType.DMA((seqs,)),
                pltpu.SemaphoreType.DMA((seqs,)),
                pltpu.SemaphoreType.DMA((seqs + 2,)),
            ],
        ),
        compiler_params=pltpu.CompilerParams(
            vmem_limit_bytes=VMEM_LIMIT, collective_id=0 if mem.shape[0] > 1 else None, has_side_effects=True
        ),
        name="forward",
    )(tlen, mlen, head_scale, tokens, cotangent, mask, buckets, table, mem, *vecs, *wides, *weights)


def cross_backward(mlen, mem_ref, q_ref, k_ref, v_ref, lse_ref, delta_ref, do_ref, wck, wcv, dk_ref, dv_ref, dqt_ref, kt_ref, dmem_ref, dwck_ref, dwcv_ref, sums_ref, middle):
    length, mem_total = q_ref.shape[0], mem_ref.shape[0]
    step = 256
    for c in range(mem_total // step):
        kt_ref[:, pl.ds(c * step, step)] = k_ref[pl.ds(c * step, step), :].T
    masks = half_masks(length)
    place = lax.broadcasted_iota(jnp.int32, (step, length), 0)

    @pl.loop(0, q_ref.shape[1] // 128)
    def _(p):
        lanes = pair_lanes(p)
        qp, dop = q_ref[:, lanes], do_ref[:, lanes]
        qms = [pick(masks[half], qp) for half in range(2)]
        doms = [pick(masks[half], dop) for half in range(2)]
        lse = [lse_ref[2 * p + half] for half in range(2)]
        delta = [delta_ref[2 * p + half] for half in range(2)]
        dqt = [jnp.zeros((64, length), F32) for half in range(2)]
        for c in range(mem_total // step):
            rows = pl.ds(c * step, step)
            kp, vp = k_ref[rows, lanes], v_ref[rows, lanes]
            outside = jnp.where(place < mlen - c * step, 0.0, NEG)
            dv = jnp.zeros((step, 128), F32)
            dk = jnp.zeros((step, 128), F32)
            for half in range(2):
                st = mm_nt(kp, qms[half]) + outside
                pt = jnp.exp(st - lse[half])
                dpt = mm_nt(vp, doms[half])
                dst = (pt * (dpt - delta[half])).astype(BF16)
                dqt[half] = dqt[half] + mm(kt_ref[head_rows(p, half), rows], dst)
                dv = dv + mm(pt.astype(BF16), doms[half])
                dk = dk + mm(dst, qms[half])
            dv_ref[rows, lanes] = dv.astype(BF16)
            dk_ref[rows, lanes] = dk.astype(BF16)
        for half in range(2):
            dqt_ref[head_rows(p, half), :] = dqt[half]

    middle()

    @pl.loop(0, mem_total // step)
    def _(c):
        rows = pl.ds(pl.multiple_of(c * step, step), step)
        dk, dv = dk_ref[rows, :], dv_ref[rows, :]
        dmem_ref[rows, :] = (mm_nt(dk, wck[...]) + mm_nt(dv, wcv[...])).astype(BF16)
        sums_ref[8:9] += colsum(dv.astype(F32))

    dwck_ref[...] += mm_tn(mem_ref[...], dk_ref[...])
    dwcv_ref[...] += mm_tn(mem_ref[...], dv_ref[...])


def self_backward(tlen, bias_ref, q_ref, k_ref, v_ref, lse_ref, delta_ref, do_ref, dqt_ref, dk_ref, dv_ref, kt_ref, dbias_ref):
    length = q_ref.shape[0]
    kt_ref[:, pl.ds(0, length)] = k_ref[...].T
    key_place = lax.broadcasted_iota(jnp.int32, (length, length), 0)
    outside = jnp.where(key_place < tlen, 0.0, NEG)
    masks = half_masks(length)

    @pl.loop(0, q_ref.shape[1] // 128)
    def _(p):
        lanes = pair_lanes(p)
        qp, dop = q_ref[:, lanes], do_ref[:, lanes]
        kp, vp = k_ref[:, lanes], v_ref[:, lanes]
        dv = jnp.zeros((length, 128), F32)
        dk = jnp.zeros((length, 128), F32)
        for half in range(2):
            h = 2 * p + half
            qm, dom = pick(masks[half], qp), pick(masks[half], dop)
            st = mm_nt(kp, qm) + bias_ref[h] + outside
            pt = jnp.exp(st - lse_ref[h])
            dpt = mm_nt(vp, dom)
            dst = (pt * (dpt - delta_ref[h])).astype(BF16)
            rows = pl.ds(pl.multiple_of(h * length, length), length)
            wide_ds = dst.astype(F32)
            for tile in range(length // 128):
                dbias_ref[tile, rows, :] += wide_ds[:, tile * 128 : (tile + 1) * 128]
            dqt_ref[head_rows(p, half), :] = mm(kt_ref[head_rows(p, half), pl.ds(0, length)], dst)
            dv = dv + mm(pt.astype(BF16), dom)
            dk = dk + mm(dst, qm)
        dv_ref[:, lanes] = dv.astype(BF16)
        dk_ref[:, lanes] = dk.astype(BF16)


def bucket_totals(buckets_t, dbias_ref, out_ref):
    length = buckets_t.shape[0]
    heads = dbias_ref.shape[1] // length
    lo_places = lax.broadcasted_iota(jnp.int32, (32, 128), 0)
    group = 8

    def block(start, tiles, acc):
        rows = buckets_t[pl.ds(start, group), :]
        lefts, rights = [], []
        for k in range(group):
            for tile in tiles:
                ids = rows[k : k + 1, tile * 128 : (tile + 1) * 128]
                d = dbias_ref[tile, pl.ds(start + k, heads, stride=length), :]
                high = jnp.broadcast_to(ids >> 5, (heads, 128))
                lefts.append(jnp.concatenate([jnp.where(high == g, d, 0.0) for g in range(16)], axis=0).astype(BF16))
                rights.append(jnp.where(lo_places == (ids & 31), 1.0, 0.0).astype(BF16))
        return acc + mm_nt(jnp.concatenate(lefts, axis=1), jnp.concatenate(rights, axis=1))

    acc = jnp.zeros((16 * heads, 32), F32)
    tiles = length // 128
    for band in range(tiles):
        live = range(band, tiles)

        def body(b, acc):
            return block(pl.multiple_of(band * 128 + b * group, group), live, acc)

        acc = lax.fori_loop(0, 128 // group, body, acc)
    for g in range(16):
        out_ref[:, g * 32 : (g + 1) * 32] = acc[g * heads : (g + 1) * heads]


FIRST_POINTS = (0, 1, 2, 3, 5, 7, 9, 11, 12, 14, 15)
SECOND_POINTS = (1, 2, 4, 5, 7, 9, 11, 13, 14)
THIRD_POINTS = (8, 9, 11, 13, 15)


def bwd_kernel(
    sizes, groups,
    tlen_ref, mlen_ref,
    hs_ref, tok_ref, mem_ref, bias_ref, buckets_ref, sg_ref, ss_ref, cg_ref, cs_ref, packed_hbm, sums_a_ref, wide_a_ref,
    q1_ref, k1_ref, v1_ref, lse1_ref, ot1_ref,
    x1_ref, q2_ref, k2_ref, v2_ref, lse2_ref, delta2_ref, do2_ref, g2_ref,
    wq, wk, wv, wo, wcq, wck, wcv,
    dtok_ref, dmem_hbm, grads_hbm, small_hbm,
    dmem_scr, g1_scr, grads, land, small, small_land, dw_ref,
    dk_scr, dv_scr, dqt_scr, kt_scr, dbias_scr, delta_scr, do_scr, hs_scr,
    send_sem, recv_sem, own_sem, io_sem, group_send, group_recv, free_sem, buckets_t_scr,
):
    t = pl.program_id(0)
    seqs, heads, length, width = dmem_scr.shape[0], lse1_ref.shape[1], tok_ref.shape[1], tok_ref.shape[2]
    sums_ref = small.at[pl.ds(24, 24)]
    places, piece = dmem_hbm.shape[0], dmem_hbm.shape[2]
    me = lax.axis_index("dp")
    rows_mine = pl.ds(pl.multiple_of(me * piece, piece), piece)

    plain, swapped = stage_orders(sizes)
    reductions = []
    at = 0
    for k, (start, rows) in enumerate(groups):
        order = swapped if k % 2 else plain
        reductions.append(Reduction(grads, land, start, rows, at, order, 16, group_send.at[k], group_recv.at[k], free_sem.at[k]))
        at += reductions[-1].land_rows
    last = len(groups)
    reductions.append(
        Reduction(small, small_land, 0, small.shape[0], 0, plain, 8, group_send.at[last], group_recv.at[last], free_sem.at[last])
    )
    def own(s):
        return pltpu.make_async_copy(dmem_scr.at[s, rows_mine], dmem_hbm.at[me, s], own_sem.at[s])

    def to_peer(k, s):
        peer = lax.rem(me + k, places)
        rows = pl.ds(pl.multiple_of(peer * piece, piece), piece)
        return pltpu.make_async_remote_copy(
            src_ref=dmem_scr.at[s, rows], dst_ref=dmem_hbm.at[me, s], send_sem=send_sem.at[s], recv_sem=recv_sem.at[s],
            device_id={"dp": peer}, device_id_type=pl.DeviceIdType.MESH,
        )

    def all_peers(s):
        some = dmem_hbm.at[pl.ds(0, places - 1), s]
        return pltpu.make_async_remote_copy(
            src_ref=some, dst_ref=some, send_sem=send_sem.at[s], recv_sem=recv_sem.at[s],
            device_id={"dp": lax.rem(me + 1, places)}, device_id_type=pl.DeviceIdType.MESH,
        )

    points = 4 * seqs
    timing = [FIRST_POINTS, FIRST_POINTS, SECOND_POINTS, SECOND_POINTS, THIRD_POINTS, THIRD_POINTS]
    acts = {p: [] for p in range(points)}
    moved = [0] * len(reductions)
    for r, when in enumerate(timing):
        for p in when:
            if p < points and moved[r] <= len(reductions[r]):
                acts[p].append((r, moved[r]))
                moved[r] += 1
    pieces = [(s, k) for s in range(seqs) for k in range(1, places)]
    quota = -(-len(pieces) // (points - 2))
    sends = {p: [] for p in range(points)}
    for p in range(2, points):
        for _ in range(quota):
            if pieces and 2 * (pieces[0][0] + 1) <= p:
                s, k = pieces.pop(0)
                if sends[p] and sends[p][-1][0] == s:
                    sends[p][-1][2] = k + 1
                else:
                    sends[p].append([s, k, k + 1])

    def send(s, first, end):
        @pl.loop(first, end)
        def _(k):
            to_peer(k, s).start()

    def point(half):
        for step in range(2 * seqs):
            p = 2 * step + half
            if acts[p] or sends[p]:

                @pl.when(t == step)
                def _():
                    for r, k in acts[p]:
                        reductions[r].advance(k)
                    for s, first, end in sends[p]:
                        send(s, first, end)

    @pl.when(t == 0)
    def _():
        early = packed_hbm.shape[0]
        load = pltpu.make_async_copy(packed_hbm, grads.at[pl.ds(0, early)], io_sem.at[0])
        load.start()
        for ref in (dw_ref, dbias_scr, hs_scr, small):
            ref[...] = jnp.zeros_like(ref)
        buckets_t_scr[...] = buckets_ref[...].T
        small[0:8] = sums_a_ref[...]
        hidden = wide_a_ref.shape[1]
        for k in range(3):
            for c in range(hidden // width):
                row = 8 + k * (hidden // width) + c
                small[row : row + 1] = wide_a_ref[k : k + 1, c * width : (c + 1) * width]
        peers = [{"dp": lax.rem(me + k, places)} for k in range(1, places)]
        rep = lax.axis_index("rep")
        for bit in range(sizes["rep"].bit_length() - 1):
            peers.append({"rep": rep + (1 - 2 * ((rep // 2**bit) % 2)) * 2**bit})
        if peers:
            meet(peers)
        load.wait()

    point(0)

    @pl.when(t < seqs)
    def _():
        cross_backward(
            mlen_ref[t], mem_ref.at[0], q2_ref.at[0], k2_ref.at[0], v2_ref.at[0], lse2_ref.at[0], delta2_ref.at[0],
            do2_ref.at[0], wck, wcv, dk_scr, dv_scr, dqt_scr, kt_scr, dmem_scr.at[t], dw_ref.at[5], dw_ref.at[6],
            sums_ref, lambda: point(1),
        )
        own(t).start()
        dq2 = (dqt_scr[...].T.astype(BF16).astype(F32) * 0.125).astype(BF16)
        hat2, scale2 = normalize(x1_ref[0])
        gain2 = cg_ref[...]
        h2 = (hat2 * gain2 + cs_ref[...]).astype(BF16)
        dw_ref[4] += mm_tn(h2, dq2)
        sums_ref[7:8] += colsum(dq2.astype(F32))
        dh2 = mm_nt(dq2, wcq[...])
        sums_ref[5:6] += colsum(dh2 * hat2)
        sums_ref[6:7] += colsum(dh2)
        g1 = g2_ref[0] + norm_back(dh2, hat2, scale2, gain2)
        g1_scr[t] = g1
        sums_ref[4:5] += colsum(g1)
        e1 = g1.astype(BF16)
        c1t = scaled_heads(ot1_ref[0], hs_ref).astype(BF16)
        dw_ref[3] += mm(c1t, e1)

    @pl.when(t == seqs - 1)
    def _():
        for k in range(4):
            grads[pl.ds(groups[4][0] + k * width, width), :] = dw_ref[3 + k].astype(BF16)

    @pl.when(t >= seqs)
    def _():
        s = t - seqs
        g1 = g1_scr[s]
        dc1 = mm_nt(g1.astype(BF16), wo[...])
        dc1t = dc1.T
        do1t = scaled_heads(dc1t, hs_ref).astype(BF16)
        do_scr[...] = do1t.T
        for h in range(heads):
            rows = slice(h * 64, (h + 1) * 64)
            o = ot1_ref[0, rows, :]
            hs_scr[h : h + 1, :] += colsum(o * dc1t[rows])
            delta_scr[h] = colsum(o * do1t[rows].astype(F32))
        self_backward(
            tlen_ref[s], bias_ref, q1_ref.at[0], k1_ref.at[0], v1_ref.at[0], lse1_ref.at[0], delta_scr, do_scr,
            dqt_scr, dk_scr.at[pl.ds(0, length)], dv_scr.at[pl.ds(0, length)], kt_scr, dbias_scr,
        )
        point(1)
        dq1 = (dqt_scr[...].T.astype(BF16).astype(F32) * 0.125).astype(BF16)
        dk1 = dk_scr[pl.ds(0, length), :]
        dv1 = dv_scr[pl.ds(0, length), :]
        hat1, scale1 = normalize(tok_ref[0].astype(F32))
        gain1 = sg_ref[...]
        h1 = (hat1 * gain1 + ss_ref[...]).astype(BF16)
        dw_ref[0] += mm_tn(h1, dq1)
        dw_ref[1] += mm_tn(h1, dk1)
        dw_ref[2] += mm_tn(h1, dv1)
        sums_ref[2:3] += colsum(dq1.astype(F32))
        sums_ref[3:4] += colsum(dv1.astype(F32))
        dh1 = mm_nt(dq1, wq[...]) + mm_nt(dk1, wk[...]) + mm_nt(dv1, wv[...])
        sums_ref[0:1] += colsum(dh1 * hat1)
        sums_ref[1:2] += colsum(dh1)
        dtok_ref[0] = (g1 + norm_back(dh1, hat1, scale1, gain1)).astype(BF16)

    @pl.when(t == 2 * seqs - 1)
    def _():
        for k in range(3):
            grads[pl.ds(groups[6][0] + k * width, width), :] = dw_ref[k].astype(BF16)
        sums_ref[16 : 16 + heads] = jnp.broadcast_to(jnp.sum(hs_scr[...], axis=1, keepdims=True), (heads, width))
        late = [6, 7] + [r for r in range(6)]
        for r in (6, 7):
            reductions[r].advance(0)
            moved[r] = 1
        bucket_totals(buckets_t_scr, dbias_scr, small.at[pl.ds(48, 8)])
        late.append(last)
        while any(moved[r] <= len(reductions[r]) for r in late):
            for r in late:
                reductions[r].advance(moved[r])
                moved[r] += 1
        for s, k in pieces:
            send(s, k, k + 1)
        stores = [pltpu.make_async_copy(grads, grads_hbm, io_sem.at[0]), pltpu.make_async_copy(small, small_hbm, io_sem.at[1])]
        for c in stores:
            c.start()
        for s in range(seqs):
            own(s).wait()
            if places > 1:
                all_peers(s).wait_send()
                all_peers(s).wait_recv()
        for c in stores:
            c.wait()


def backward(sizes, tlen, mlen, head_scale, tokens, mem, bias, buckets, vecs, packed, sums_a, wide_a, saved, weights):
    seqs, length, width = tokens.shape
    mem_total = mem.shape[1]
    heads = bias.shape[0]
    places = sizes["dp"]
    early = packed.shape[0]
    quarter = early // (9 * width) * 2 * width
    groups = [(k * quarter, quarter) for k in range(2)]
    groups += [(2 * quarter, early - 3 * quarter), (early - quarter, quarter)]
    groups += [(early, 2 * width), (early + 2 * width, 2 * width)]
    groups += [(early + 4 * width, 2 * width), (early + 6 * width, width)]
    total = early + 7 * width
    plain, _ = stage_orders(sizes)
    land = max(sum(land_rows(rows, plain, 16) for _, rows in groups), 16)
    small_rows = 64
    small_land = max(land_rows(small_rows, plain, 8), 8)
    late = lambda t, *_: jnp.maximum(t - seqs, 0)
    soon = lambda t, *_: jnp.minimum(t, seqs - 1)
    both = lambda t, *_: jnp.where(t < seqs, t, t - seqs)
    const = lambda a: pl.BlockSpec(a.shape, lambda t, *_: (0,) * a.ndim, pipeline_mode=pl.Buffered(1))
    seq = lambda a, idx: pl.BlockSpec((1,) + a.shape[1:], lambda t, *_: (idx(t),) + (0,) * (a.ndim - 1))
    sds = jax.ShapeDtypeStruct
    anywhere = pl.BlockSpec(memory_space=pl.ANY)
    when = [late, late, late, late, both] + [soon] * 8
    slots = max(2 * len(plain), 1)
    several = places > 1 or sizes["rep"] > 1
    return pl.pallas_call(
        functools.partial(bwd_kernel, sizes, groups),
        out_shape=[
            sds((seqs, length, width), BF16),
            sds((places, seqs, mem_total // places, width), BF16),
            sds((total, width), BF16),
            sds((small_rows, width), F32),
        ],
        grid_spec=pltpu.PrefetchScalarGridSpec(
            num_scalar_prefetch=3,
            grid=(2 * seqs,),
            in_specs=[seq(tokens, late), seq(mem, soon), const(bias), const(buckets)] + [const(v) for v in vecs]
            + [anywhere, const(sums_a), const(wide_a)]
            + [seq(a, idx) for a, idx in zip(saved, when)]
            + [const(w) for w in weights],
            out_specs=[seq(tokens, late), anywhere, anywhere, anywhere],
            scratch_shapes=[
                pltpu.VMEM((seqs, mem_total, width), BF16),
                pltpu.VMEM((seqs, length, width), F32),
                pltpu.VMEM((total, width), BF16),
                pltpu.VMEM((land, width), BF16),
                pltpu.VMEM((small_rows, width), F32),
                pltpu.VMEM((small_land, width), F32),
                pltpu.VMEM((7, width, width), F32),
                pltpu.VMEM((mem_total, width), BF16),
                pltpu.VMEM((mem_total, width), BF16),
                pltpu.VMEM((width, length), F32),
                pltpu.VMEM((width, mem_total), BF16),
                pltpu.VMEM((length // 128, heads * length, 128), F32),
                pltpu.VMEM((heads, 1, length), F32),
                pltpu.VMEM((length, width), BF16),
                pltpu.VMEM((heads, length), F32),
                pltpu.SemaphoreType.DMA((seqs,)),
                pltpu.SemaphoreType.DMA((seqs,)),
                pltpu.SemaphoreType.DMA((seqs,)),
                pltpu.SemaphoreType.DMA((2,)),
                pltpu.SemaphoreType.DMA((len(groups) + 1, slots)),
                pltpu.SemaphoreType.DMA((len(groups) + 1, slots)),
                pltpu.SemaphoreType.REGULAR((len(groups) + 1, slots)),
                pltpu.VMEM((length, length), jnp.int32),
            ],
        ),
        compiler_params=pltpu.CompilerParams(
            vmem_limit_bytes=VMEM_LIMIT, collective_id=1 if several else None, has_side_effects=True
        ),
        name="backward",
    )(tlen, mlen, head_scale, tokens, mem, bias, buckets, *vecs, packed, sums_a, wide_a, *saved, *weights)


def unpack_kernel(grads_ref, small_ref, *refs):
    big, vectors, (table_ref, scale_ref, slots, sem) = refs[:10], refs[10:-4], refs[-4:]
    dw1, dw2, rest = big[0], big[1], big[2:]
    width = grads_ref.shape[0]
    parts = dw1.shape[1] // width
    targets = [dw1.at[:, pl.ds(c * width, width)] for c in range(parts)]
    targets += [dw2.at[pl.ds(c * width, width)] for c in range(parts)] + list(rest)
    t = pl.program_id(0)
    depth = slots.shape[0]
    slot = lax.rem(t, depth)

    def settle(k):
        pltpu.make_async_copy(slots.at[k], rest[0], sem.at[k]).wait()

    @pl.when(t >= depth)
    def _():
        settle(slot)

    slots[slot] = grads_ref[...].astype(F32)
    for k, target in enumerate(targets):

        @pl.when(t == k)
        def _():
            pltpu.make_async_copy(slots.at[k % depth], target, sem.at[k % depth]).start()

    @pl.when(t == 0)
    def _():
        for row, ref in zip(VECTOR_ROWS, vectors):
            for c in range(ref.shape[1] // width):
                ref[:, c * width : (c + 1) * width] = small_ref[row + c : row + c + 1]
        heads = scale_ref.shape[1]
        buckets = table_ref.shape[0]
        table_ref[...] = small_ref[48 : 48 + heads].T[:buckets]
        block = small_ref[40 : 40 + heads]
        diagonal = lax.broadcasted_iota(jnp.int32, block.shape, 0) == lax.broadcasted_iota(jnp.int32, block.shape, 1)
        scale_ref[...] = colsum(jnp.where(diagonal, block, 0.0))[:, :heads]

    @pl.when(t == len(targets) - 1)
    def _():
        for k in range(depth):
            settle(k)


VECTOR_ROWS = (24, 25, 26, 27, 28, 29, 30, 31, 32, 4, 5, 3, 1, 2, 0, 16, 8, 12)


def unpack(grads, small, hidden, heads, buckets):
    width = grads.shape[1]
    sds = jax.ShapeDtypeStruct
    big = [sds((width, hidden), F32), sds((hidden, width), F32)] + [sds((width, width), F32)] * 8
    vectors = [sds((1, width), F32)] * 15 + [sds((1, hidden), F32)] * 3
    tail = [sds((buckets, heads), F32), sds((1, heads), F32)]
    whole = lambda a: pl.BlockSpec(a.shape, lambda t: (0,) * len(a.shape))
    steps = grads.shape[0] // width
    return pl.pallas_call(
        unpack_kernel,
        out_shape=big + vectors + tail,
        grid=(steps,),
        in_specs=[pl.BlockSpec((width, width), lambda t: (t, 0)), whole(small)],
        out_specs=[pl.BlockSpec(memory_space=pl.ANY)] * 10 + [whole(a) for a in vectors + tail],
        scratch_shapes=[pltpu.VMEM((4, width, width), F32), pltpu.SemaphoreType.DMA((4,))],
        name="unpack",
    )(grads, small)


def local(
    tokens, cotangent, target_lengths, task_mask, memory_lengths, position_buckets, memory,
    self_gain, self_shift, query_weight, query_bias, key_weight, value_weight, value_bias, position_table, head_scale,
    output_weight, output_bias, cross_gain, cross_shift, cross_query, cross_query_bias, cross_key, cross_value,
    cross_value_bias, post_gain, post_shift, cross_output, cross_output_bias, feed_gain, feed_shift, inner_weight,
    inner_bias, inner_gain, inner_shift, outer_weight, outer_bias,
):
    heads = head_scale.shape[0]
    bucket_count = position_table.shape[0]
    hidden = inner_weight.shape[1]
    table_t = jnp.pad(position_table.T, ((0, 0), (0, 512 - bucket_count)))
    row = lambda v: v.reshape(1, -1)
    vecs = [row(v) for v in (
        self_gain, self_shift, query_bias, value_bias, output_bias, output_bias, cross_gain, cross_shift,
        cross_query_bias, cross_value_bias, post_gain, post_shift, cross_output_bias, feed_gain, feed_shift, outer_bias,
    )]
    wides = [row(v) for v in (inner_bias, inner_gain, inner_shift)]
    sizes = {"dp": lax.axis_size("dp"), "rep": lax.axis_size("rep")}
    fwd = forward(
        target_lengths, memory_lengths, head_scale, tokens, cotangent, task_mask, position_buckets, table_t, memory,
        vecs, wides,
        [query_weight, key_weight, value_weight, output_weight, cross_query, cross_key, cross_value, cross_output,
         inner_weight, outer_weight],
    )
    layer_output, gathered, packed, bias, sums_a, wide_a = fwd[13:]
    dtok, memory_gradient, grads, small = backward(
        sizes, target_lengths, memory_lengths, head_scale, tokens, gathered, bias, position_buckets,
        [vecs[k] for k in (SELF_GAIN, SELF_SHIFT, CROSS_GAIN, CROSS_SHIFT)], packed, sums_a, wide_a, fwd[:13],
        [query_weight, key_weight, value_weight, output_weight, cross_query, cross_key, cross_value],
    )
    outs = unpack(grads, small, hidden, heads, bucket_count)
    dw1, dw2, dwco, dwo, dwcq, dwck, dwcv, dwq, dwk, dwv = outs[:10]
    (
        d_self_gain, d_self_shift, d_query_bias, d_value_bias, d_output_bias, d_cross_gain, d_cross_shift,
        d_cross_query_bias, d_cross_value_bias, d_post_gain, d_post_shift, d_cross_output_bias, d_feed_gain,
        d_feed_shift, d_outer_bias, d_inner_bias, d_inner_gain, d_inner_shift,
    ) = [v.reshape(-1) for v in outs[10:28]]
    d_table, d_scale = outs[28], outs[29].reshape(-1)
    return (
        layer_output, dtok, memory_gradient,
        d_self_gain, d_self_shift, dwq, d_query_bias, dwk, dwv, d_value_bias, d_table, d_scale,
        dwo, d_output_bias, d_cross_gain, d_cross_shift, dwcq, d_cross_query_bias, dwck, dwcv, d_cross_value_bias,
        d_post_gain, d_post_shift, dwco, d_cross_output_bias, d_feed_gain, d_feed_shift, dw1, d_inner_bias,
        d_inner_gain, d_inner_shift, dw2, d_outer_bias,
    )


def solution(mesh):
    per_seq3, per_seq2, per_seq1 = P(("dp", "rep"), None, None), P(("dp", "rep"), None), P(("dp", "rep"))
    spread = P(None, "rep", "dp", None)
    in_specs = (per_seq3, per_seq3, per_seq1, per_seq2, per_seq1, P(), spread) + (P(),) * 30
    out_specs = (per_seq3, per_seq3, spread) + (P(),) * 30
    return jax.shard_map(local, mesh=mesh, in_specs=in_specs, out_specs=out_specs, check_vma=False)
```

time: 720 us -> 357 us (0.50)
  waiting for transfers between devices: 425 us -> 0 us
  Pallas kernels: 212 us -> 346 us
  local copies, waits for them, and re-layouts: 33.7 us -> 9.57 us
  other arithmetic: 21.1 us -> 0 us
  between operations: 14.5 us -> 0.72 us
  starting transfers between devices: 12.4 us -> 0 us
    psum x2 -> x0, waiting for transfers between devices: 344 us -> none  [the longest x1 181 us: local(): big = lax.psum((low(dw), low(dwco), low(dw1), low(dw2)), ('dp', 'rep'))]
    pallas_call x2, Pallas kernels: 105 us -> 219 us  [the longest x1 204 us: backward(): pl.pallas_call(functools.partial(bwd_kernel, sizes, groups), out_shape=[s...]
    all_to_all x2 -> x0, waiting for transfers between devices: 80.9 us -> none  [the longest x1 80.9 us: local(): lax.all_to_all(memory, 'dp', split_axis=0, concat_axis=2, tiled=True)[0]]
    pallas_call x1, Pallas kernels: 107 us -> 127 us  [forward(): pl.pallas_call(fwd_kernel, out_shape=[o[0] for o in outs], grid_spec=pltp...]
    convert_element_type x8 -> x0, other arithmetic: 19.7 us -> none  [the longest x4 10.5 us: local(): dw, dwco, dw1, dw2 = [a.astype(F32) for a in big]]
    all_to_all x2 -> x0, starting transfers between devices: 12.1 us -> none  [the longest x1 7.4 us: local(): lax.all_to_all(memory, 'dp', split_axis=0, concat_axis=2, tiled=True)[0]]
    broadcast_in_dim x6 -> x0, local copies, waits for them, and re-layouts: 11.4 us -> none  [the longest x1 7.44 us: local(): dmem[None]]
    all_to_all x2 -> x0, local copies, waits for them, and re-layouts: 9.94 us -> none  [the longest x1 5.3 us: local(): lax.all_to_all(dmem[None], 'dp', split_axis=2, concat_axis=0, tiled=True)]
  transfers between devices with their start and end apart: 4 -> 0, of which waited for: 3 -> 0; matrix products, arithmetic and copies ran while one was open for 5% -> 0% of each run, Pallas kernels for 1% -> 0%
where the time goes in v2:
time: 357 us; the launch traced here: 356 us
  Pallas kernels  346 us (97%)
  local copies, waits for them, and re-layouts  9.57 us (3%)
    pallas_call x1, Pallas kernels, backward(): pl.pallas_call(functools.partial(bwd_kernel, sizes, groups), out_shape=[s...  204 us
    pallas_call x1, Pallas kernels, forward(): pl.pallas_call(fwd_kernel, out_shape=[o[0] for o in outs], grid_spec=pltp...  127 us
    pallas_call x1, Pallas kernels, unpack(): pl.pallas_call(unpack_kernel, out_shape=big + vectors + tail, grid=(steps...  14.9 us
    unnamed x8, local copies, waits for them, and re-layouts  8.25 us

profile of v2, /device:TPU:0, one launch (start us, length us, event | category | flops | bytes accessed | tf_op | source)
XLA Modules:
  0.0 356.4 jit_solution(3760152233929041620)
XLA Ops:
  0.7 1.3 pad.4.table_ref
  2.0 126.9 %forward.1 = (bf16[4,256,512]{2,1,0:T(8,128)(2,1)}, bf16[4,256,512]{2,1,0:T(8,128)(2,1)}, bf16[4,256,512]{2,1,0:T(8,128)(2,1)}, f32[4,8,1,256]{3,2,1,0:T(1,128)}...) custom-call(s32[4]{0:T(128)} %tlen_ref.3, ...), custom_call_target="tpu_custom_call" | custom-call | tf_op jit(solution)/shard_map/forward/pallas_call | solution.py:487
  128.9 204.3 %backward.1 = (bf16[4,256,512]{2,1,0:T(8,128)(2,1)}, bf16[8,4,128,512]{3,2,1,0:T(8,128)(2,1)}, bf16[8192,512]{1,0:T(8,128)(2,1)}, f32[64,512]{1,0:T(8,128)}) custom-call(s32[4]{0:T(128)} %tlen_ref.3, s32[4]{0:T(128)} %mlen_ref.3, f32[8]{0:T(128)} %hs_ref.3, bf16[4,256,512]{2,1,0:T(8,128)(2,1)} %tok_ref.3, bf16[4,1024,512]{2,1,0:T(8,128)(2,1)} %get-tuple-element.87.mem_ref, ...), custom_call_target="tpu_custom_call" | custom-call | tf_op jit(solution)/shard_map/backward/pallas_call | solution.py:877
  333.2 0.0 copy-start
  333.3 0.0 copy-start.1
  333.3 14.9 %unpack.1 = (f32[512,2048]{1,0:T(8,128)}, f32[2048,512]{1,0:T(8,128)}, f32[512,512]{1,0:T(8,128)}, f32[512,512]{1,0:T(8,128)}, f32[512,512]{1,0:T(8,128)}, /*ind...) custom-call(bf16[8192,512]{1,0:T(8,128)(2,1)} %get-tuple-element.107, ...), custom_call_target="tpu_custom_call" | custom-call | tf_op jit(solution)/shard_map/unpack/pallas_call | solution.py:980
  348.2 1.7 copy.70
  349.9 0.0 copy-done
  349.9 1.0 copy.74
  350.8 0.0 copy-done.1
  350.8 1.0 copy.75
  351.8 4.6 %copy.76 = bf16[8,4,128,512]{3,2,1,0:T(8,128)(2,1)} copy(bf16[8,4,128,512]{3,2,1,0:T(8,128)(2,1)} %get-tuple-element.207) | data formatting | bytes 8388608
Async XLA Ops:
  333.2 16.6 %copy-start = (bf16[4,256,512]{2,1,0:T(8,128)(2,1)S(1)}, bf16[4,256,512]{2,1,0:T(8,128)(2,1)}, u32[]{:S(2)}) copy-start(bf16[4,256,512]{2,1,0:T(8,128)(2,1)} %get-tuple-element.205) | copy-start | bytes 3145732
  333.3 17.6 %copy-start.1 = (bf16[4,256,512]{2,1,0:T(8,128)(2,1)S(1)}, bf16[4,256,512]{2,1,0:T(8,128)(2,1)}, u32[]{:S(2)}) copy-start(bf16[4,256,512]{2,1,0:T(8,128)(2,1)} %get-tuple-element.206) | copy-start | bytes 3145732

commit v3 on v2

v3 whole, which is shorter than its diff:
```python
import functools

import jax
import jax.numpy as jnp
from jax import lax
from jax.experimental import pallas as pl
from jax.experimental.pallas import tpu as pltpu
from jax.sharding import PartitionSpec as P

NEG = -1e30
F32 = jnp.float32
BF16 = jnp.bfloat16
VMEM_LIMIT = 67043328

(
    SELF_GAIN,
    SELF_SHIFT,
    QUERY_BIAS,
    VALUE_BIAS,
    HEAD_SCALE,
    OUTPUT_BIAS,
    CROSS_GAIN,
    CROSS_SHIFT,
    CROSS_QUERY_BIAS,
    CROSS_VALUE_BIAS,
    POST_GAIN,
    POST_SHIFT,
    CROSS_OUTPUT_BIAS,
    FEED_GAIN,
    FEED_SHIFT,
    OUTER_BIAS,
) = range(16)


def mm(a, b):
    return jnp.dot(a, b, preferred_element_type=F32)


def mm_nt(a, b):
    return lax.dot_general(a, b, (((1,), (1,)), ((), ())), preferred_element_type=F32)


def mm_tn(a, b):
    return lax.dot_general(a, b, (((0,), (0,)), ((), ())), preferred_element_type=F32)


def normalize(x):
    center = x - jnp.mean(x, axis=-1, keepdims=True)
    spread = jnp.mean(center * center, axis=-1, keepdims=True)
    scale = lax.rsqrt(spread + 1e-05)
    return center * scale, scale


def norm_back(dy, hat, scale, gain):
    w = dy * gain
    first = jnp.mean(w, axis=-1, keepdims=True)
    second = jnp.mean(w * hat, axis=-1, keepdims=True)
    return (w - first - hat * second) * scale


def colsum(x):
    return jnp.sum(x, axis=0, keepdims=True)


def half_masks(rows):
    lane = lax.broadcasted_iota(jnp.int32, (rows, 128), 1)
    return (lane < 64, lane >= 64)


def pick(mask, x):
    return jnp.where(mask, x.astype(F32), 0.0).astype(BF16)


def pair_lanes(p):
    return pl.ds(pl.multiple_of(p * 128, 128), 128)


def head_rows(p, half):
    return pl.ds(pl.multiple_of(p * 128 + half * 64, 64), 64)


def fill_bias(buckets, table_rows, out_ref):
    length = buckets.shape[0]
    chunks = table_rows.shape[2] // 128
    low, high = buckets & 127, buckets >> 7
    key_place = lax.broadcasted_iota(jnp.int32, (length, 128), 0)
    lane = lax.broadcasted_iota(jnp.int32, (length, 128), 1)

    @pl.loop(0, out_ref.shape[0])
    def _(h):
        rows = [jnp.broadcast_to(table_rows[h, :, pl.ds(c * 128, 128)], (length, 128)) for c in range(chunks)]
        for tile in range(length // 128):
            cols = slice(tile * 128, (tile + 1) * 128)
            total = jnp.zeros((length, 128), F32)
            for c in range(chunks):
                got = jnp.take_along_axis(rows[c], low[:, cols], axis=1, mode="promise_in_bounds")
                total = jnp.where(high[:, cols] == c, got, total)
            out_ref[h, :, pl.ds(tile * 128, 128)] = jnp.where(key_place <= lane + tile * 128, total, NEG)


def axis_bits(sizes):
    return [(axis, bit) for axis in ("rep", "dp") for bit in range(sizes[axis].bit_length() - 1)]


def stage_orders(sizes):
    plain = axis_bits(sizes)
    reps = sizes["rep"].bit_length() - 1
    swapped = list(plain)
    if reps >= 2 and len(plain) > reps:
        swapped = plain[: reps - 1] + [plain[reps], plain[reps - 1]] + plain[reps + 1 :]
    return plain, swapped


def flip(axis, bit):
    place = lax.axis_index(axis)
    return {axis: place + (1 - 2 * ((place // 2**bit) % 2)) * 2**bit}


def fold_sizes(rows, stages, tile):
    sizes, span = [], rows
    for _ in stages:
        span = span // 2 if span % (2 * tile) == 0 else span
        sizes.append(span)
    return sizes


class Reduction:
    def __init__(self, buf, start, rows, out, out_start, stages, tile, lands, send, recv, store):
        self.buf, self.out, self.tile, self.lands = buf, out, tile, lands
        self.send, self.recv, self.shift = send, recv, out_start - start
        folds, spreads = [], []
        base, span = start, rows
        for (axis, bit), size in zip(stages, fold_sizes(rows, stages, tile)):
            mine = (lax.axis_index(axis) // 2**bit) % 2
            peer = flip(axis, bit)
            halve = size < span
            keep = base + mine * size if halve else base
            give = base + (1 - mine) * size if halve else base
            folds.append((peer, give, keep, size))
            if halve:
                spreads.insert(0, (peer, keep, size))
            base, span = keep, size
        self.folds, self.spreads, self.own = folds, spreads, (base, span)
        self.store = pltpu.make_async_copy(self.part(buf, base, span), self.part(out, base + self.shift, span), store)

    def __len__(self):
        return len(self.folds) + len(self.spreads)

    def part(self, ref, start, size):
        return ref.at[pl.ds(start if isinstance(start, int) else pl.multiple_of(start, self.tile), size)]

    def copy(self, k):
        n = len(self.folds)
        if k < n:
            peer, give, keep, size = self.folds[k]
            land, at = self.lands[k]
            source, target = self.part(self.buf, give, size), land.at[pl.ds(at, size)]
        else:
            peer, base, size = self.spreads[k - n]
            target = self.part(self.out, base + self.shift, size)
            source = self.part(self.buf, base, size) if k == n else target
        return pltpu.make_async_remote_copy(
            src_ref=source, dst_ref=target, send_sem=self.send.at[k], recv_sem=self.recv.at[k],
            device_id=peer, device_id_type=pl.DeviceIdType.MESH,
        )

    def start(self, k):
        if k == len(self.folds):
            self.store.start()
        if k == min(len(self.folds) + 1, len(self)):
            self.store.wait()
        if k < len(self):
            self.copy(k).start()

    def finish(self, k):
        self.copy(k).wait()
        if k < len(self.folds):
            peer, give, keep, size = self.folds[k]
            land, at = self.lands[k]
            step = next(c for c in (128, 64, 48, 32, 16, 8) if size % c == 0)

            @pl.loop(0, size // step)
            def _(b):
                kept = pl.ds(pl.multiple_of(keep + b * step, self.tile), step)
                came = pl.ds(pl.multiple_of(at + b * step, self.tile), step)
                total = self.buf[kept, :].astype(F32) + land[came, :].astype(F32)
                self.buf[kept, :] = total.astype(self.buf.dtype)

    def advance(self, k):
        if 0 < k <= len(self):
            self.finish(k - 1)
        if k <= len(self):
            self.start(k)


def signal_all(sem, peers):
    for peer in peers:
        pl.semaphore_signal(sem, inc=1, device_id=peer, device_id_type=pl.DeviceIdType.MESH)


def scaled_heads(value_t, hs_ref):
    return jnp.concatenate([value_t[h * 64 : (h + 1) * 64] * hs_ref[h] for h in range(value_t.shape[0] // 64)], axis=0)


def self_forward(
    tlen, hs_ref, tok, bias_ref, vec_ref, wq, wk, wv, wo, q_ref, k_ref, v_ref, lse_ref, ot_ref, x1_ref, vt_ref
):
    length = tok.shape[0]
    x0 = tok.astype(F32)
    hat, _ = normalize(x0)
    h1 = (hat * vec_ref[SELF_GAIN][...] + vec_ref[SELF_SHIFT][...]).astype(BF16)
    q_ref[...] = ((mm(h1, wq[...]) + vec_ref[QUERY_BIAS][...]) * 0.125).astype(BF16)
    k_ref[...] = mm(h1, wk[...]).astype(BF16)
    value = (mm(h1, wv[...]) + vec_ref[VALUE_BIAS][...]).astype(BF16)
    v_ref[...] = value
    vt_ref[:, pl.ds(0, length)] = value.T
    key_place = lax.broadcasted_iota(jnp.int32, (length, length), 0)
    outside = jnp.where(key_place < tlen, 0.0, NEG)
    masks = half_masks(length)

    @pl.loop(0, q_ref.shape[1] // 128)
    def _(p):
        lanes = pair_lanes(p)
        kp, qp = k_ref[:, lanes], q_ref[:, lanes]
        for half in range(2):
            st = mm_nt(kp, pick(masks[half], qp)) + bias_ref[2 * p + half] + outside
            top = jnp.max(st, axis=0, keepdims=True)
            e = jnp.exp(st - top)
            total = colsum(e)
            ot = mm(vt_ref[head_rows(p, half), pl.ds(0, length)], e.astype(BF16))
            ot_ref[head_rows(p, half), :] = ot * (1.0 / total)
            lse_ref[2 * p + half] = top + jnp.log(total)

    c1 = scaled_heads(ot_ref[...], hs_ref).T.astype(BF16)
    x1_ref[...] = x0 + mm(c1, wo[...]) + vec_ref[OUTPUT_BIAS][...]


def cross_forward(mlen, mem_ref, vec_ref, x1, wcq, wck, wcv, q_ref, k_ref, v_ref, lse_ref, ot_ref, vt_ref, st_ref):
    length, mem_total = x1.shape[0], mem_ref.shape[0]
    hat, _ = normalize(x1)
    h2 = (hat * vec_ref[CROSS_GAIN][...] + vec_ref[CROSS_SHIFT][...]).astype(BF16)
    q_ref[...] = ((mm(h2, wcq[...]) + vec_ref[CROSS_QUERY_BIAS][...]) * 0.125).astype(BF16)
    step = 256

    @pl.loop(0, mem_total // step)
    def _(c):
        rows = pl.ds(pl.multiple_of(c * step, step), step)
        part = mem_ref[rows, :]
        k_ref[rows, :] = mm(part, wck[...]).astype(BF16)
        v_ref[rows, :] = (mm(part, wcv[...]) + vec_ref[CROSS_VALUE_BIAS][...]).astype(BF16)

    for c in range(mem_total // step):
        vt_ref[:, pl.ds(c * step, step)] = v_ref[pl.ds(c * step, step), :].T
    masks = half_masks(length)
    place = lax.broadcasted_iota(jnp.int32, (step, length), 0)
    tiles = length // 128

    @pl.loop(0, q_ref.shape[1] // 128)
    def _(p):
        lanes = pair_lanes(p)
        qp = q_ref[:, lanes]
        for half in range(2):
            qm = pick(masks[half], qp)
            top = jnp.full((1, length), -jnp.inf, F32)
            for c in range(mem_total // step):
                st = mm_nt(k_ref[pl.ds(c * step, step), lanes], qm)
                st = st + jnp.where(place < mlen - c * step, 0.0, NEG)
                for tile in range(tiles):
                    st_ref[tile, pl.ds(half * mem_total + c * step, step), :] = st[:, tile * 128 : (tile + 1) * 128]
                top = jnp.maximum(top, jnp.max(st, axis=0, keepdims=True))
            total = jnp.zeros((1, length), F32)
            ot = jnp.zeros((64, length), F32)
            for c in range(mem_total // step):
                rows = pl.ds(half * mem_total + c * step, step)
                st = jnp.concatenate([st_ref[tile, rows, :] for tile in range(tiles)], axis=1)
                e = jnp.exp(st - top)
                total = total + colsum(e)
                ot = ot + mm(vt_ref[head_rows(p, half), pl.ds(c * step, step)], e.astype(BF16))
            ot_ref[head_rows(p, half), :] = ot * (1.0 / total)
            lse_ref[2 * p + half] = top + jnp.log(total)


def feed_both(x2, g3, vec_ref, wide_ref, w1, w2, out_ref, acc, sums_ref, wide_sums_ref, u_ref, d_ref, df_ref, f_ref, r_ref, middle):
    length, hidden = u_ref.shape
    width = x2.shape[1]
    parts = hidden // width
    hat3, scale3 = normalize(x2)
    gain3 = vec_ref[FEED_GAIN][...]
    h3 = (hat3 * gain3 + vec_ref[FEED_SHIFT][...]).astype(BF16)
    cols = [pl.ds(c * width, width) for c in range(parts)]
    chunk = [pl.ds(c * length, length) for c in range(parts)]
    for c in range(parts):
        u_ref[:, cols[c]] = mm(h3, w1[cols[c], :])
    step = 16
    tiles = hidden // 128
    halves = d_ref.shape[0]

    def d_place(b, k):
        return k % halves, pl.ds(pl.multiple_of((k // halves) * length + b * step, step), step)

    @pl.loop(0, length // step)
    def _(b):
        rows = pl.ds(pl.multiple_of(b * step, step), step)
        u = u_ref[rows, :] + wide_ref[0][...]
        below = 0.5 * (1.0 + lax.erf(u * 0.7071067811865476))
        d = below + u * (jnp.exp(-0.5 * u * u) * 0.3989422804014327)
        for k in range(tiles):
            tile, place = d_place(b, k)
            d_ref[tile, place, :] = d[:, k * 128 : (k + 1) * 128]
        hat, scale = normalize(u * below)
        u_ref[rows, :] = hat
        f = (hat * wide_ref[1][...] + wide_ref[2][...]).astype(BF16)
        for c in range(parts):
            f_ref[pl.ds(pl.multiple_of(c * length + b * step, step), step), :] = f[:, c * width : (c + 1) * width]
        r_ref[rows, :] = jnp.broadcast_to(scale, (step, 128))

    x3 = x2 + vec_ref[OUTER_BIAS][...]
    for c in range(parts):
        x3 = x3 + mm(f_ref[chunk[c], :], w2[cols[c], :])
    out_ref[0] = x3.astype(BF16)
    sums_ref[0:1] += colsum(g3)
    e3 = g3.astype(BF16)
    for c in range(parts):
        acc[pl.ds(hidden + c * width, width), :] += mm_tn(f_ref[chunk[c], :], e3)
        df_ref[:, cols[c]] = mm_nt(e3, w2[cols[c], :])
    middle()

    @pl.loop(0, length // step)
    def _(b):
        rows = pl.ds(pl.multiple_of(b * step, step), step)
        dy, hat = df_ref[rows, :], u_ref[rows, :]
        part = dy * hat
        wide_sums_ref[0:8] += part[0:8] + part[8:16]
        wide_sums_ref[8:16] += dy[0:8] + dy[8:16]
        da = norm_back(dy, hat, r_ref[rows, 0:1], wide_ref[1][...])
        pieces = []
        for k in range(tiles):
            tile, place = d_place(b, k)
            pieces.append(d_ref[tile, place, :])
        du = da * jnp.concatenate(pieces, axis=1)
        wide_sums_ref[16:24] += du[0:8] + du[8:16]
        eu = du.astype(BF16)
        for c in range(parts):
            f_ref[pl.ds(pl.multiple_of(c * length + b * step, step), step), :] = eu[:, c * width : (c + 1) * width]

    dh3 = jnp.zeros(x2.shape, F32)
    h3t = h3.T
    for c in range(parts):
        acc[cols[c], :] += mm(h3t, f_ref[chunk[c], :])
        dh3 = dh3 + mm_nt(f_ref[chunk[c], :], w1[cols[c], :])
    sums_ref[1:2] += colsum(dh3 * hat3)
    sums_ref[2:3] += colsum(dh3)
    return g3 + norm_back(dh3, hat3, scale3, gain3)


def cross_backward(
    mlen, mem_ref, q_ref, k_ref, v_ref, lse_ref, delta_ref, do_ref, wck, wcv, dk_ref, dv_ref, dqt_ref, kt_ref,
    acc_key, acc_value, sums_ref, points,
):
    length, mem_total = q_ref.shape[0], mem_ref.shape[0]
    step = 256
    for c in range(mem_total // step):
        kt_ref[:, pl.ds(c * step, step)] = k_ref[pl.ds(c * step, step), :].T
    masks = half_masks(length)
    place = lax.broadcasted_iota(jnp.int32, (step, length), 0)
    pairs = q_ref.shape[1] // 128

    @pl.loop(0, pairs)
    def _(p):
        @pl.when(p == pairs // 2)
        def _():
            points[0]()

        lanes = pair_lanes(p)
        qp, dop = q_ref[:, lanes], do_ref[:, lanes]
        qms = [pick(masks[half], qp) for half in range(2)]
        doms = [pick(masks[half], dop) for half in range(2)]
        lse = [lse_ref[2 * p + half] for half in range(2)]
        delta = [delta_ref[2 * p + half] for half in range(2)]
        dqt = [jnp.zeros((64, length), F32) for half in range(2)]
        for c in range(mem_total // step):
            rows = pl.ds(c * step, step)
            kp, vp = k_ref[rows, lanes], v_ref[rows, lanes]
            outside = jnp.where(place < mlen - c * step, 0.0, NEG)
            dv = jnp.zeros((step, 128), F32)
            dk = jnp.zeros((step, 128), F32)
            for half in range(2):
                st = mm_nt(kp, qms[half]) + outside
                pt = jnp.exp(st - lse[half])
                dpt = mm_nt(vp, doms[half])
                dst = (pt * (dpt - delta[half])).astype(BF16)
                dqt[half] = dqt[half] + mm(kt_ref[head_rows(p, half), rows], dst)
                dv = dv + mm(pt.astype(BF16), doms[half])
                dk = dk + mm(dst, qms[half])
            dv_ref[rows, lanes] = dv.astype(BF16)
            dk_ref[rows, lanes] = dk.astype(BF16)
        for half in range(2):
            dqt_ref[head_rows(p, half), :] = dqt[half]

    points[1]()
    acc_key[...] += mm_tn(mem_ref[...], dk_ref[...])
    acc_value[...] += mm_tn(mem_ref[...], dv_ref[...])

    @pl.loop(0, mem_total // step)
    def _(c):
        rows = pl.ds(pl.multiple_of(c * step, step), step)
        dk, dv = dk_ref[rows, :], dv_ref[rows, :]
        mem_ref[rows, :] = (mm_nt(dk, wck[...]) + mm_nt(dv, wcv[...])).astype(BF16)
        sums_ref[8:9] += colsum(dv.astype(F32))


def self_backward(tlen, bias_ref, q_ref, k_ref, v_ref, lse_ref, delta_ref, do_ref, dqt_ref, dk_ref, dv_ref, kt_ref, dbias_ref):
    length = q_ref.shape[0]
    kt_ref[:, pl.ds(0, length)] = k_ref[...].T
    key_place = lax.broadcasted_iota(jnp.int32, (length, length), 0)
    outside = jnp.where(key_place < tlen, 0.0, NEG)
    masks = half_masks(length)

    @pl.loop(0, q_ref.shape[1] // 128)
    def _(p):
        lanes = pair_lanes(p)
        qp, dop = q_ref[:, lanes], do_ref[:, lanes]
        kp, vp = k_ref[:, lanes], v_ref[:, lanes]
        dv = jnp.zeros((length, 128), F32)
        dk = jnp.zeros((length, 128), F32)
        for half in range(2):
            h = 2 * p + half
            qm, dom = pick(masks[half], qp), pick(masks[half], dop)
            st = mm_nt(kp, qm) + bias_ref[h] + outside
            pt = jnp.exp(st - lse_ref[h])
            dpt = mm_nt(vp, dom)
            dst = (pt * (dpt - delta_ref[h])).astype(BF16)
            rows = pl.ds(pl.multiple_of(h * length, length), length)
            wide_ds = dst.astype(F32)
            for tile in range(length // 128):
                dbias_ref[tile, rows, :] += wide_ds[:, tile * 128 : (tile + 1) * 128]
            dqt_ref[head_rows(p, half), :] = mm(kt_ref[head_rows(p, half), pl.ds(0, length)], dst)
            dv = dv + mm(pt.astype(BF16), dom)
            dk = dk + mm(dst, qm)
        dv_ref[:, lanes] = dv.astype(BF16)
        dk_ref[:, lanes] = dk.astype(BF16)


def bucket_totals(buckets_t, dbias_ref, out_ref):
    length = buckets_t.shape[0]
    heads = dbias_ref.shape[1] // length
    lo_places = lax.broadcasted_iota(jnp.int32, (32, 128), 0)
    group = 8

    def block(start, tiles, acc):
        rows = buckets_t[pl.ds(start, group), :]
        lefts, rights = [], []
        for k in range(group):
            for tile in tiles:
                ids = rows[k : k + 1, tile * 128 : (tile + 1) * 128]
                d = dbias_ref[tile, pl.ds(start + k, heads, stride=length), :]
                high = jnp.broadcast_to(ids >> 5, (heads, 128))
                lefts.append(jnp.concatenate([jnp.where(high == g, d, 0.0) for g in range(16)], axis=0).astype(BF16))
                rights.append(jnp.where(lo_places == (ids & 31), 1.0, 0.0).astype(BF16))
        return acc + mm_nt(jnp.concatenate(lefts, axis=1), jnp.concatenate(rights, axis=1))

    acc = jnp.zeros((16 * heads, 32), F32)
    tiles = length // 128
    for band in range(tiles):
        live = range(band, tiles)

        def body(b, acc):
            return block(pl.multiple_of(band * 128 + b * group, group), live, acc)

        acc = lax.fori_loop(0, 128 // group, body, acc)
    for g in range(16):
        out_ref[:, g * 32 : (g + 1) * 32] = acc[g * heads : (g + 1) * heads]


SMALL_ROWS = 64
SUMS_B = 24
HEAD_ROWS = 40
TABLE_ROWS = 48


def piece_order(places):
    far, near = list(range(max(places // 2, 1), places)), list(range(1, places // 2))
    order = []
    for k in range(len(far)):
        order.append(far[k])
        if k < len(near):
            order.append(near[k])
    return order


def partner(me, places, k):
    if places & (places - 1):
        return lax.rem(me + k, places)
    for bit in range(places.bit_length() - 1):
        if (k >> bit) & 1:
            me = me + (1 - 2 * ((me // 2**bit) % 2)) * 2**bit
    return me


def layer_kernel(sizes, layout, tlen_ref, mlen_ref, hs_ref, tok_ref, cot_ref, mask_ref, buckets_ref, table_ref, *rest):
    mem_hbm, w1_hbm, w2_hbm = rest[:3]
    vec_ref, wide_ref = rest[3:19], rest[19:22]
    wq, wk, wv, wo, wcq, wck, wcv, wco = rest[22:30]
    out_ref, dtok_ref, dmem_hbm, grads_hbm, small_hbm = rest[30:35]
    (
        mem_scr, w1s, w2s, acc, bias_ref, st_scr,
        q1_scr, k1_scr, v1_scr, lse1_scr, ot1_scr, x1_scr,
        kv_scr, q2_scr, do_scr, lse2_scr, delta_scr,
        vt_scr, ot_scr, u_scr, df_scr, r_scr, dk_scr, dv_scr,
        grads, land, small, small_land, wide_scr, hs_scr, table_scr, buckets_t_scr,
        load_sem, send_sem, recv_sem, own_sem, back_send, back_recv, back_own, group_send, group_recv, store_sem, ready_sem,
    ) = rest[35:]
    seqs, mem_total, width = mem_scr.shape
    length, hidden, heads = tok_ref.shape[1], u_scr.shape[1], bias_ref.shape[0]
    places, piece = mem_hbm.shape[0], mem_hbm.shape[2]
    t = pl.program_id(0)
    me = lax.axis_index("dp")
    mine = pl.ds(pl.multiple_of(me * piece, piece), piece)
    k2_scr, v2_scr = kv_scr.at[pl.ds(0, mem_total)], kv_scr.at[pl.ds(mem_total, mem_total)]
    sums_a, sums_b = small.at[pl.ds(0, 8)], small.at[pl.ds(SUMS_B, 24)]
    base = 2 * hidden
    acc_at = lambda k: acc.at[pl.ds(base + k * width, width)]
    CROSS_OUT, OUT, QUERY, KEY, VALUE = range(5)
    order = piece_order(places)

    def own_in(s):
        return pltpu.make_async_copy(mem_hbm.at[me, s], mem_scr.at[s, mine], own_sem.at[s])

    def own_back(s):
        return pltpu.make_async_copy(mem_scr.at[s, mine], dmem_hbm.at[me, s], back_own.at[s])

    def loads():
        copies = []
        for c in range(hidden // width):
            cols = pl.ds(c * width, width)
            copies.append(pltpu.make_async_copy(w1_hbm.at[:, cols], w1s.at[cols], load_sem.at[c]))
        copies.append(pltpu.make_async_copy(w2_hbm, w2s, load_sem.at[hidden // width]))
        return copies

    def remote(source, target, send, recv, peer):
        return pltpu.make_async_remote_copy(
            src_ref=source, dst_ref=target, send_sem=send, recv_sem=recv, device_id={"dp": peer},
            device_id_type=pl.DeviceIdType.MESH,
        )

    def send_in(s, k):
        peer = partner(me, places, k)
        remote(mem_hbm.at[peer, s], mem_scr.at[s, mine], send_sem.at[s], recv_sem.at[s], peer).start()

    def send_back(s, k):
        peer = partner(me, places, k)
        rows = pl.ds(pl.multiple_of(peer * piece, piece), piece)
        remote(mem_scr.at[s, rows], dmem_hbm.at[me, s], back_send.at[s], back_recv.at[s], peer).start()

    def all_in(s):
        some = mem_scr.at[s, pl.ds(0, (places - 1) * piece)]
        return remote(some, some, send_sem.at[s], recv_sem.at[s], partner(me, places, 1))

    def all_back(s):
        some = dmem_hbm.at[pl.ds(0, places - 1), s]
        return remote(some, some, back_send.at[s], back_recv.at[s], partner(me, places, 1))

    plain, swapped = stage_orders(sizes)
    pools = {"first": w2s, "second": w1s, "land": land}
    buffers = {"grads": grads, "kv": kv_scr}
    reductions = []
    for r, (buf, start, rows, out_start, lands) in enumerate(layout):
        reductions.append(Reduction(
            buffers[buf], start, rows, grads_hbm, out_start, swapped if r % 2 else plain, 16,
            [(pools[name], at) for name, at in lands], group_send.at[r], group_recv.at[r], store_sem.at[r],
        ))
    last = len(layout)
    at, lands = 0, []
    for size in fold_sizes(SMALL_ROWS, plain, 8):
        lands.append((small_land, at))
        at += size
    reductions.append(Reduction(
        small, 0, SMALL_ROWS, small_hbm, 0, plain, 8, lands, group_send.at[last], group_recv.at[last], store_sem.at[last],
    ))
    first = [r for r, item in enumerate(layout) if item[0] == "grads" and item[1] < base]
    second = [r for r, item in enumerate(layout) if item[0] == "grads" and item[1] >= base]
    third = [r for r, item in enumerate(layout) if item[0] == "kv"]
    flips = [flip(axis, bit) for axis, bit in plain]

    steps = 4 * seqs
    begin_first, begin_second = 3 * (3 * seqs - 1), 3 * 3 * seqs
    acts = {p: [] for p in range(3 * steps)}
    moved = [0] * len(reductions)
    for group, begin, table in ((first, begin_first, FIRST_POINTS), (second, begin_second, SECOND_POINTS)):
        for n, r in enumerate(group):
            for p in table[n % len(table)]:
                if begin + p < 3 * steps and moved[r] <= len(reductions[r]):
                    acts[begin + p].append((r, moved[r]))
                    moved[r] += 1
    queue = [(s, k) for s in range(seqs) for k in order]
    sends = {p: [] for p in range(3 * steps)}
    for p in range(3 * steps):
        quota = -(-len(order) * PIECES[p % len(PIECES)] // 7)
        while quota and queue and p >= 3 * (seqs + 2 * queue[0][0] + 2):
            sends[p].append(queue.pop(0))
            quota -= 1

    def point(part, low, high):
        for step in range(low, high):
            p = 3 * step + part
            if acts[p] or sends[p] or (p == begin_first and flips):

                @pl.when(t == step)
                def _():
                    if p == begin_first and flips:
                        pl.semaphore_wait(ready_sem, len(flips))
                    for r, k in acts[p]:
                        reductions[r].advance(k)
                    for s, k in sends[p]:
                        send_back(s, k)

    @pl.when(t == 0)
    def _():
        bucket_load = pltpu.make_async_copy(buckets_ref, buckets_t_scr, load_sem.at[hidden // width + 1])
        bucket_load.start()
        for s in range(seqs):
            own_in(s).start()
        peers = [{"dp": partner(me, places, k)} for k in range(1, places)]
        peers += [flip(axis, bit) for axis, bit in plain if axis == "rep"]
        if peers:
            barrier = pltpu.get_barrier_semaphore()
            signal_all(barrier, peers)
            pl.semaphore_wait(barrier, len(peers))
        for s in range(seqs):
            for k in order:
                send_in(s, k)
        for c in loads():
            c.start()
        for ref in (acc, small, wide_scr, hs_scr):
            ref[...] = jnp.zeros_like(ref)
        for h in range(heads):
            table_scr[h] = table_ref[h : h + 1, :]
        bucket_load.wait()
        buckets_t_scr[...] = buckets_t_scr[...].T
        fill_bias(buckets_t_scr[...], table_scr, bias_ref)

    @pl.when(t < seqs)
    def _():
        self_forward(
            tlen_ref[t], hs_ref, tok_ref[0], bias_ref, vec_ref, wq, wk, wv, wo,
            q1_scr.at[t], k1_scr.at[t], v1_scr.at[t], lse1_scr.at[t], ot1_scr.at[t], x1_scr.at[t], vt_scr,
        )

    @pl.when(t == seqs)
    def _():
        for c in loads():
            c.wait()

    inner = t - seqs
    s = inner // 2

    @pl.when((t >= seqs) & (t < 3 * seqs) & (inner % 2 == 0))
    def _():
        own_in(s).wait()
        if places > 1:
            all_in(s).wait_recv()
        point(0, seqs, 3 * seqs)
        x1 = x1_scr[s]
        cross_forward(
            mlen_ref[s], mem_scr.at[s], vec_ref, x1, wcq, wck, wcv,
            q2_scr, k2_scr, v2_scr, lse2_scr, ot_scr, vt_scr, st_scr,
        )
        point(1, seqs, 3 * seqs)
        hat, scale = normalize(ot_scr[...].T)
        gain = vec_ref[POST_GAIN][...]
        c2 = (hat * gain + vec_ref[POST_SHIFT][...]).astype(BF16)
        x2 = x1 + mm(c2, wco[...]) + vec_ref[CROSS_OUTPUT_BIAS][...]
        here = lax.broadcasted_iota(jnp.int32, mask_ref.shape, 0) == s
        row = jnp.sum(jnp.where(here, mask_ref[...], 0), axis=0, keepdims=True).astype(F32)
        row = jnp.where(lax.broadcasted_iota(jnp.int32, (1, length), 1) < tlen_ref[s], row, 0.0)
        g3 = cot_ref[0].astype(F32) * jnp.broadcast_to(row, (8, length)).T[:, 0:1]
        g2 = feed_both(
            x2, g3, vec_ref, wide_ref, w1s, w2s, out_ref, acc, sums_a, wide_scr,
            u_scr, st_scr, df_scr, dk_scr, r_scr, lambda: point(2, seqs, 3 * seqs),
        )
        df_scr[:, pl.ds(0, width)] = g2
        sums_a[3:4] += colsum(g2)
        e2 = g2.astype(BF16)
        acc_at(CROSS_OUT)[...] += mm_tn(c2, e2)
        dc2 = mm_nt(e2, wco[...])
        sums_a[4:5] += colsum(dc2 * hat)
        sums_a[5:6] += colsum(dc2)
        do2 = norm_back(dc2, hat, scale, gain).astype(BF16)
        do_scr[...] = do2
        prod = do2.astype(F32).T * ot_scr[...]
        for h in range(heads):
            delta_scr[h] = colsum(prod[h * 64 : (h + 1) * 64])

    @pl.when(t == 3 * seqs - 2)
    def _():
        signal_all(ready_sem, flips)
        for k in range(3):
            total = colsum(wide_scr[8 * k : 8 * k + 8])
            for c in range(hidden // width):
                row = 8 + k * (hidden // width) + c
                small[row : row + 1] = total[:, c * width : (c + 1) * width]

        @pl.loop(0, base // 256)
        def _(b):
            rows = pl.ds(pl.multiple_of(b * 256, 256), 256)
            grads[rows, :] = acc[rows, :].astype(BF16)

    @pl.when((t >= seqs) & (t < 3 * seqs) & (inner % 2 == 1))
    def _():
        point(0, seqs, 3 * seqs)
        cross_backward(
            mlen_ref[s], mem_scr.at[s], q2_scr, k2_scr, v2_scr, lse2_scr, delta_scr, do_scr, wck, wcv,
            dk_scr, dv_scr, ot_scr, vt_scr, acc_at(KEY), acc_at(VALUE), sums_b,
            [lambda: point(1, seqs, 3 * seqs), lambda: point(2, seqs, 3 * seqs)],
        )
        own_back(s).start()
        dq2 = (ot_scr[...].T.astype(BF16).astype(F32) * 0.125).astype(BF16)
        hat2, scale2 = normalize(x1_scr[s])
        gain2 = vec_ref[CROSS_GAIN][...]
        h2 = (hat2 * gain2 + vec_ref[CROSS_SHIFT][...]).astype(BF16)
        acc_at(QUERY)[...] += mm_tn(h2, dq2)
        sums_b[7:8] += colsum(dq2.astype(F32))
        dh2 = mm_nt(dq2, wcq[...])
        sums_b[5:6] += colsum(dh2 * hat2)
        sums_b[6:7] += colsum(dh2)
        g1 = df_scr[:, pl.ds(0, width)] + norm_back(dh2, hat2, scale2, gain2)
        x1_scr[s] = g1
        sums_b[4:5] += colsum(g1)
        c1t = scaled_heads(ot1_scr[s], hs_ref).astype(BF16)
        acc_at(OUT)[...] += mm(c1t, g1.astype(BF16))

    @pl.when(t == 3 * seqs - 1)
    def _():
        @pl.loop(0, 5 * width // 256)
        def _(b):
            rows = pl.ds(pl.multiple_of(base + b * 256, 256), 256)
            grads[rows, :] = acc[rows, :].astype(BF16)

        st_scr[...] = jnp.zeros_like(st_scr)
        acc[pl.ds(0, 3 * width), :] = jnp.zeros((3 * width, width), F32)

    @pl.when(t >= 3 * seqs)
    def _():
        point(0, 3 * seqs, steps)
        s = t - 3 * seqs
        g1 = x1_scr[s]
        dc1t = mm_nt(g1.astype(BF16), wo[...]).T
        do1t = scaled_heads(dc1t, hs_ref).astype(BF16)
        do_scr[...] = do1t.T
        for h in range(heads):
            rows = slice(h * 64, (h + 1) * 64)
            o = ot1_scr[s, rows, :]
            hs_scr[h : h + 1, :] += colsum(o * dc1t[rows])
            delta_scr[h] = colsum(o * do1t[rows].astype(F32))
        dk_ref, dv_ref = dk_scr.at[pl.ds(0, length)], dv_scr.at[pl.ds(0, length)]
        self_backward(
            tlen_ref[s], bias_ref, q1_scr.at[s], k1_scr.at[s], v1_scr.at[s], lse1_scr.at[s], delta_scr, do_scr,
            ot_scr, dk_ref, dv_ref, vt_scr, st_scr,
        )
        point(1, 3 * seqs, steps)
        dq1 = (ot_scr[...].T.astype(BF16).astype(F32) * 0.125).astype(BF16)
        dk1, dv1 = dk_ref[...], dv_ref[...]
        hat1, scale1 = normalize(tok_ref[0].astype(F32))
        gain1 = vec_ref[SELF_GAIN][...]
        h1t = (hat1 * gain1 + vec_ref[SELF_SHIFT][...]).astype(BF16).T
        for k, d in enumerate((dq1, dk1, dv1)):
            acc[pl.ds(k * width, width), :] += mm(h1t, d)
        point(2, 3 * seqs, steps)
        sums_b[2:3] += colsum(dq1.astype(F32))
        sums_b[3:4] += colsum(dv1.astype(F32))
        dh1 = mm_nt(dq1, wq[...]) + mm_nt(dk1, wk[...]) + mm_nt(dv1, wv[...])
        sums_b[0:1] += colsum(dh1 * hat1)
        sums_b[1:2] += colsum(dh1)
        dtok_ref[0] = (g1 + norm_back(dh1, hat1, scale1, gain1)).astype(BF16)

    @pl.when(t == steps - 1)
    def _():
        @pl.loop(0, 3 * width // 256)
        def _(b):
            rows = pl.ds(pl.multiple_of(b * 256, 256), 256)
            kv_scr[rows, :] = acc[rows, :].astype(BF16)

        small[HEAD_ROWS : HEAD_ROWS + heads] = jnp.broadcast_to(
            jnp.sum(hs_scr[...], axis=1, keepdims=True), (heads, width)
        )
        for r in third:
            reductions[r].advance(0)
            moved[r] = 1
        for r in first + second:
            reductions[r].advance(moved[r])
            moved[r] += 1
        bucket_totals(buckets_t_scr, st_scr, small.at[pl.ds(TABLE_ROWS, heads)])
        left = third + [last] + second + first
        while any(moved[r] <= len(reductions[r]) for r in left):
            for r in left:
                reductions[r].advance(moved[r])
                moved[r] += 1
            for _ in range(-(-len(order) * 2 // 7)):
                if queue:
                    send_back(*queue.pop(0))
        for s, k in queue:
            send_back(s, k)
        for s in range(seqs):
            own_back(s).wait()
            if places > 1:
                all_in(s).wait_send()
                all_back(s).wait_send()
                all_back(s).wait_recv()


FIRST_POINTS = ((0, 1, 2, 4, 6, 8, 10, 12), (0, 1, 2, 4, 6, 8, 10, 12), (1, 2, 3, 5, 7, 9, 11, 13), (1, 2, 3, 5, 7, 9, 11, 13))
SECOND_POINTS = ((1, 3, 5, 7, 9), (1, 3, 5, 7, 9), (2, 4, 6, 8, 10), (2, 4, 6, 8, 10))
PIECES = (2, 2, 2)


def reduction_layout(sizes, width, hidden):
    plain, _ = stage_orders(sizes)
    base = 2 * hidden
    members = [("grads", k * hidden // 2, hidden // 2, k * hidden // 2) for k in range(4)]
    members += [("grads", base, 2 * width, base), ("grads", base + 2 * width, 2 * width, base + 2 * width)]
    members += [("grads", base + 4 * width, width, base + 4 * width)]
    members += [("kv", 0, width, base + 5 * width), ("kv", width, width, base + 6 * width)]
    members += [("kv", 2 * width, width, base + 7 * width)]
    used = {"first": 0, "second": 0, "land": 0}
    layout = []
    for buf, start, rows, out_start in members:
        lands = []
        for size in fold_sizes(rows, plain, 16):
            name = "land"
            if buf == "grads":
                name = next((n for n in ("first", "second") if used[n] + size <= hidden), "land")
            lands.append((name, used[name]))
            used[name] += size
        layout.append((buf, start, rows, out_start, lands))
    return layout, max(used["land"], 16)


def whole_layer(sizes, tlen, mlen, head_scale, tokens, cotangent, mask, buckets, table, memory, w1, w2, vecs, wides, weights):
    seqs, length, width = tokens.shape
    places, _, piece, _ = memory.shape
    mem_total = places * piece
    heads, hidden = head_scale.shape[0], w1.shape[1]
    layout, land = reduction_layout(sizes, width, hidden)
    plain, _ = stage_orders(sizes)
    small_land = max(sum(fold_sizes(SMALL_ROWS, plain, 8)), 8)
    slots = max(2 * len(plain), 1)
    several = places > 1 or sizes["rep"] > 1
    sds = jax.ShapeDtypeStruct
    anywhere = pl.BlockSpec(memory_space=pl.ANY)
    const = lambda a: pl.BlockSpec(a.shape, lambda t, *_: (0,) * a.ndim, pipeline_mode=pl.Buffered(1))
    seq = lambda idx: pl.BlockSpec((1, length, width), lambda t, *_: (idx(t), 0, 0))
    ends = lambda t: jnp.where(t < 3 * seqs, jnp.minimum(t, seqs - 1), t - 3 * seqs)
    middle = lambda t: jnp.clip((t - seqs) // 2, 0, seqs - 1)
    late = lambda t: jnp.maximum(t - 3 * seqs, 0)
    tall = heads * length
    scratch = [
        ((seqs, mem_total, width), BF16), ((hidden, width), BF16), ((hidden, width), BF16),
        ((2 * hidden + 5 * width, width), F32), ((heads, length, length), F32),
        ((length // 128, max(tall, 2 * mem_total, hidden * length * 128 // (length * 128)), 128), F32),
        ((seqs, length, width), BF16), ((seqs, length, width), BF16), ((seqs, length, width), BF16),
        ((seqs, heads, 1, length), F32), ((seqs, width, length), F32), ((seqs, length, width), F32),
        ((2 * mem_total, width), BF16), ((length, width), BF16), ((length, width), BF16),
        ((heads, 1, length), F32), ((heads, 1, length), F32),
        ((width, mem_total), BF16), ((width, length), F32), ((length, hidden), F32), ((length, hidden), F32),
        ((length, 128), F32), ((max(mem_total, hidden // width * length), width), BF16), ((mem_total, width), BF16),
        ((2 * hidden + 5 * width, width), BF16), ((land, width), BF16), ((SMALL_ROWS, width), F32), ((small_land, width), F32),
        ((24, hidden), F32), ((heads, length), F32), ((heads, 1, table.shape[1]), F32), ((length, length), jnp.int32),
    ]
    dma = pltpu.SemaphoreType.DMA
    groups = len(layout) + 1
    return pl.pallas_call(
        functools.partial(layer_kernel, sizes, layout),
        out_shape=[
            sds(tokens.shape, BF16), sds(tokens.shape, BF16), sds(memory.shape, BF16),
            sds((2 * hidden + 8 * width, width), BF16), sds((SMALL_ROWS, width), F32),
        ],
        grid_spec=pltpu.PrefetchScalarGridSpec(
            num_scalar_prefetch=3,
            grid=(4 * seqs,),
            in_specs=[seq(ends), seq(middle), const(mask), anywhere, const(table), anywhere, anywhere, anywhere]
            + [const(a) for a in vecs + wides + weights],
            out_specs=[seq(middle), seq(late), anywhere, anywhere, anywhere],
            scratch_shapes=[pltpu.VMEM(shape, dtype) for shape, dtype in scratch] + [
                dma((hidden // width + 2,)), dma((seqs,)), dma((seqs,)), dma((seqs,)), dma((seqs,)), dma((seqs,)),
                dma((seqs,)), dma((groups, slots)), dma((groups, slots)), dma((groups,)), pltpu.SemaphoreType.REGULAR,
            ],
        ),
        compiler_params=pltpu.CompilerParams(
            vmem_limit_bytes=VMEM_LIMIT, collective_id=0 if several else None, has_side_effects=True
        ),
        name="layer",
    )(tlen, mlen, head_scale, tokens, cotangent, mask, buckets, table, memory, w1, w2, *vecs, *wides, *weights)


def unpack_kernel(grads_ref, small_ref, *refs):
    big, vectors, (table_ref, scale_ref, slots, sem) = refs[:10], refs[10:-4], refs[-4:]
    dw1, dw2, rest = big[0], big[1], big[2:]
    width = grads_ref.shape[0]
    parts = dw1.shape[1] // width
    targets = [dw1.at[:, pl.ds(c * width, width)] for c in range(parts)]
    targets += [dw2.at[pl.ds(c * width, width)] for c in range(parts)] + list(rest)
    t = pl.program_id(0)
    depth = slots.shape[0]
    slot = lax.rem(t, depth)

    def settle(k):
        pltpu.make_async_copy(slots.at[k], rest[0], sem.at[k]).wait()

    @pl.when(t >= depth)
    def _():
        settle(slot)

    slots[slot] = grads_ref[...].astype(F32)
    for k, target in enumerate(targets):

        @pl.when(t == k)
        def _():
            pltpu.make_async_copy(slots.at[k % depth], target, sem.at[k % depth]).start()

    @pl.when(t == 0)
    def _():
        for row, ref in zip(VECTOR_ROWS, vectors):
            for c in range(ref.shape[1] // width):
                ref[:, c * width : (c + 1) * width] = small_ref[row + c : row + c + 1]
        heads = scale_ref.shape[1]
        buckets = table_ref.shape[0]
        table_ref[...] = small_ref[48 : 48 + heads].T[:buckets]
        block = small_ref[40 : 40 + heads]
        diagonal = lax.broadcasted_iota(jnp.int32, block.shape, 0) == lax.broadcasted_iota(jnp.int32, block.shape, 1)
        scale_ref[...] = colsum(jnp.where(diagonal, block, 0.0))[:, :heads]

    @pl.when(t == len(targets) - 1)
    def _():
        for k in range(depth):
            settle(k)


VECTOR_ROWS = (24, 25, 26, 27, 28, 29, 30, 31, 32, 4, 5, 3, 1, 2, 0, 16, 8, 12)


def unpack(grads, small, hidden, heads, buckets):
    width = grads.shape[1]
    sds = jax.ShapeDtypeStruct
    big = [sds((width, hidden), F32), sds((hidden, width), F32)] + [sds((width, width), F32)] * 8
    vectors = [sds((1, width), F32)] * 15 + [sds((1, hidden), F32)] * 3
    tail = [sds((buckets, heads), F32), sds((1, heads), F32)]
    whole = lambda a: pl.BlockSpec(a.shape, lambda t: (0,) * len(a.shape))
    steps = grads.shape[0] // width
    return pl.pallas_call(
        unpack_kernel,
        out_shape=big + vectors + tail,
        grid=(steps,),
        in_specs=[pl.BlockSpec((width, width), lambda t: (t, 0)), whole(small)],
        out_specs=[pl.BlockSpec(memory_space=pl.ANY)] * 10 + [whole(a) for a in vectors + tail],
        scratch_shapes=[pltpu.VMEM((4, width, width), F32), pltpu.SemaphoreType.DMA((4,))],
        name="unpack",
    )(grads, small)


def local(
    tokens, cotangent, target_lengths, task_mask, memory_lengths, position_buckets, memory,
    self_gain, self_shift, query_weight, query_bias, key_weight, value_weight, value_bias, position_table, head_scale,
    output_weight, output_bias, cross_gain, cross_shift, cross_query, cross_query_bias, cross_key, cross_value,
    cross_value_bias, post_gain, post_shift, cross_output, cross_output_bias, feed_gain, feed_shift, inner_weight,
    inner_bias, inner_gain, inner_shift, outer_weight, outer_bias,
):
    heads = head_scale.shape[0]
    bucket_count = position_table.shape[0]
    hidden = inner_weight.shape[1]
    table_t = jnp.pad(position_table.T, ((0, 0), (0, 512 - bucket_count)))
    row = lambda v: v.reshape(1, -1)
    vecs = [row(v) for v in (
        self_gain, self_shift, query_bias, value_bias, output_bias, output_bias, cross_gain, cross_shift,
        cross_query_bias, cross_value_bias, post_gain, post_shift, cross_output_bias, feed_gain, feed_shift, outer_bias,
    )]
    wides = [row(v) for v in (inner_bias, inner_gain, inner_shift)]
    sizes = {"dp": lax.axis_size("dp"), "rep": lax.axis_size("rep")}
    layer_output, dtok, memory_gradient, grads, small = whole_layer(
        sizes, target_lengths, memory_lengths, head_scale, tokens, cotangent, task_mask, position_buckets, table_t,
        memory, inner_weight, outer_weight, vecs, wides,
        [query_weight, key_weight, value_weight, output_weight, cross_query, cross_key, cross_value, cross_output],
    )
    outs = unpack(grads, small, hidden, heads, bucket_count)
    dw1, dw2, dwco, dwo, dwcq, dwck, dwcv, dwq, dwk, dwv = outs[:10]
    (
        d_self_gain, d_self_shift, d_query_bias, d_value_bias, d_output_bias, d_cross_gain, d_cross_shift,
        d_cross_query_bias, d_cross_value_bias, d_post_gain, d_post_shift, d_cross_output_bias, d_feed_gain,
        d_feed_shift, d_outer_bias, d_inner_bias, d_inner_gain, d_inner_shift,
    ) = [v.reshape(-1) for v in outs[10:28]]
    d_table, d_scale = outs[28], outs[29].reshape(-1)
    return (
        layer_output, dtok, memory_gradient,
        d_self_gain, d_self_shift, dwq, d_query_bias, dwk, dwv, d_value_bias, d_table, d_scale,
        dwo, d_output_bias, d_cross_gain, d_cross_shift, dwcq, d_cross_query_bias, dwck, dwcv, d_cross_value_bias,
        d_post_gain, d_post_shift, dwco, d_cross_output_bias, d_feed_gain, d_feed_shift, dw1, d_inner_bias,
        d_inner_gain, d_inner_shift, dw2, d_outer_bias,
    )


def solution(mesh):
    per_seq3, per_seq2, per_seq1 = P(("dp", "rep"), None, None), P(("dp", "rep"), None), P(("dp", "rep"))
    spread = P(None, "rep", "dp", None)
    in_specs = (per_seq3, per_seq3, per_seq1, per_seq2, per_seq1, P(), spread) + (P(),) * 30
    out_specs = (per_seq3, per_seq3, spread) + (P(),) * 30
    return jax.shard_map(local, mesh=mesh, in_specs=in_specs, out_specs=out_specs, check_vma=False)
```

time: 357 us -> 319 us (0.89)
  Pallas kernels: 346 us -> 308 us
    pallas_call x2 -> x1, Pallas kernels: 331 us -> 293 us  [whole_layer(): pl.pallas_call(functools.partial(layer_kernel, sizes, layout), out_shape=...]
where the time goes in v3:
time: 319 us
  Pallas kernels  308 us (97%)
  local copies, waits for them, and re-layouts  9.57 us (3%)
    pallas_call x1, Pallas kernels, whole_layer(): pl.pallas_call(functools.partial(layer_kernel, sizes, layout), out_shape=...  293 us
    pallas_call x1, Pallas kernels, unpack(): pl.pallas_call(unpack_kernel, out_shape=big + vectors + tail, grid=(steps...  14.9 us
    unnamed x8, local copies, waits for them, and re-layouts  8.25 us

profile of v3, /device:TPU:0, one launch (start us, length us, event | category | flops | bytes accessed | tf_op | source)
XLA Modules:
  0.0 318.6 jit_solution(6261976362017084553)
XLA Ops:
  0.7 1.3 pad.4.table_ref
  2.0 293.4 %layer.1 = (bf16[4,256,512]{2,1,0:T(8,128)(2,1)}, bf16[4,256,512]{2,1,0:T(8,128)(2,1)}, bf16[8,4,128,512]{3,2,1,0:T(8,128)(2,1)}, bf16[8192,512]{1,0:T(8,128)(2,1)}, f32[64,512]{1,0:T(8,128)}) custom-call(s32[4]{0:T(128)} %tlen_ref.1, s32[4]{0:T(128)} %mlen_ref.1, f32[8]{0:T(128)} %hs_ref.1, bf16[4,256,512]{2,1,0:T(8,128)(2,1)} %tok_ref.1, ...), custom_call_target="tpu_custom_call" | custom-call | tf_op jit(solution)/shard_map/layer/pallas_call | solution.py:871
  295.4 0.0 copy-start.1
  295.4 0.0 copy-start
  295.4 14.9 %unpack.1 = (f32[512,2048]{1,0:T(8,128)}, f32[2048,512]{1,0:T(8,128)}, f32[512,512]{1,0:T(8,128)}, f32[512,512]{1,0:T(8,128)}, f32[512,512]{1,0:T(8,128)}, /*ind...) custom-call(bf16[8192,512]{1,0:T(8,128)(2,1)} %get-tuple-element.71., ...), custom_call_target="tpu_custom_call" | custom-call | tf_op jit(solution)/shard_map/unpack/pallas_call | solution.py:949
  310.3 1.7 copy.70
  312.0 0.0 copy-done.1
  312.0 1.0 copy.74
  313.0 0.0 copy-done
  313.0 1.0 copy.75
  313.9 4.6 %copy.76 = bf16[8,4,128,512]{3,2,1,0:T(8,128)(2,1)} copy(bf16[8,4,128,512]{3,2,1,0:T(8,128)(2,1)} %get-tuple-element.171) | data formatting | bytes 8388608
Async XLA Ops:
  295.4 16.6 %copy-start.1 = (bf16[4,256,512]{2,1,0:T(8,128)(2,1)S(1)}, bf16[4,256,512]{2,1,0:T(8,128)(2,1)}, u32[]{:S(2)}) copy-start(bf16[4,256,512]{2,1,0:T(8,128)(2,1)} %get-tuple-element.169) | copy-start | bytes 3145732
  295.4 17.6 %copy-start = (bf16[4,256,512]{2,1,0:T(8,128)(2,1)S(1)}, bf16[4,256,512]{2,1,0:T(8,128)(2,1)}, u32[]{:S(2)}) copy-start(bf16[4,256,512]{2,1,0:T(8,128)(2,1)} %get-tuple-element.170) | copy-start | bytes 3145732

commit v4 on v3

--- a/solution.py
+++ b/solution.py
@@ -62,6 +62,13 @@
     return jnp.sum(x, axis=0, keepdims=True)
 
 
+def eight_rows(x):
+    total = x[0:8]
+    for k in range(8, x.shape[0], 8):
+        total = total + x[k : k + 8]
+    return total
+
+
 def half_masks(rows):
     lane = lax.broadcasted_iota(jnp.int32, (rows, 128), 1)
     return (lane < 64, lane >= 64)
@@ -90,12 +97,15 @@
     def _(h):
         rows = [jnp.broadcast_to(table_rows[h, :, pl.ds(c * 128, 128)], (length, 128)) for c in range(chunks)]
         for tile in range(length // 128):
-            cols = slice(tile * 128, (tile + 1) * 128)
-            total = jnp.zeros((length, 128), F32)
+            cols, live = slice(tile * 128, (tile + 1) * 128), (tile + 1) * 128
+            total = jnp.zeros((live, 128), F32)
             for c in range(chunks):
-                got = jnp.take_along_axis(rows[c], low[:, cols], axis=1, mode="promise_in_bounds")
-                total = jnp.where(high[:, cols] == c, got, total)
-            out_ref[h, :, pl.ds(tile * 128, 128)] = jnp.where(key_place <= lane + tile * 128, total, NEG)
+                got = jnp.take_along_axis(rows[c][:live], low[:live, cols], axis=1, mode="promise_in_bounds")
+                total = jnp.where(high[:live, cols] == c, got, total)
+            seen = jnp.where(key_place[:live] <= lane[:live] + tile * 128, total, NEG)
+            out_ref[h, pl.ds(0, live), pl.ds(tile * 128, 128)] = seen
+            if live < length:
+                out_ref[h, pl.ds(live, length - live), pl.ds(tile * 128, 128)] = jnp.full((length - live, 128), NEG, F32)
 
 
 def axis_bits(sizes):
@@ -218,7 +228,7 @@
     outside = jnp.where(key_place < tlen, 0.0, NEG)
     masks = half_masks(length)
 
-    @pl.loop(0, q_ref.shape[1] // 128)
+    @pl.loop(0, q_ref.shape[1] // 128, unroll=4)
     def _(p):
         lanes = pair_lanes(p)
         kp, qp = k_ref[:, lanes], q_ref[:, lanes]
@@ -242,7 +252,7 @@
     q_ref[...] = ((mm(h2, wcq[...]) + vec_ref[CROSS_QUERY_BIAS][...]) * 0.125).astype(BF16)
     step = 256
 
-    @pl.loop(0, mem_total // step)
+    @pl.loop(0, mem_total // step, unroll=4)
     def _(c):
         rows = pl.ds(pl.multiple_of(c * step, step), step)
         part = mem_ref[rows, :]
@@ -255,7 +265,7 @@
     place = lax.broadcasted_iota(jnp.int32, (step, length), 0)
     tiles = length // 128
 
-    @pl.loop(0, q_ref.shape[1] // 128)
+    @pl.loop(0, q_ref.shape[1] // 128, unroll=2)
     def _(p):
         lanes = pair_lanes(p)
         qp = q_ref[:, lanes]
@@ -291,7 +301,7 @@
     chunk = [pl.ds(c * length, length) for c in range(parts)]
     for c in range(parts):
         u_ref[:, cols[c]] = mm(h3, w1[cols[c], :])
-    step = 16
+    step = 64
     tiles = hidden // 128
     halves = d_ref.shape[0]
 
@@ -330,15 +340,15 @@
         rows = pl.ds(pl.multiple_of(b * step, step), step)
         dy, hat = df_ref[rows, :], u_ref[rows, :]
         part = dy * hat
-        wide_sums_ref[0:8] += part[0:8] + part[8:16]
-        wide_sums_ref[8:16] += dy[0:8] + dy[8:16]
+        wide_sums_ref[0:8] += eight_rows(part)
+        wide_sums_ref[8:16] += eight_rows(dy)
         da = norm_back(dy, hat, r_ref[rows, 0:1], wide_ref[1][...])
         pieces = []
         for k in range(tiles):
             tile, place = d_place(b, k)
             pieces.append(d_ref[tile, place, :])
         du = da * jnp.concatenate(pieces, axis=1)
-        wide_sums_ref[16:24] += du[0:8] + du[8:16]
+        wide_sums_ref[16:24] += eight_rows(du)
         eu = du.astype(BF16)
         for c in range(parts):
             f_ref[pl.ds(pl.multiple_of(c * length + b * step, step), step), :] = eu[:, c * width : (c + 1) * width]
@@ -355,7 +365,7 @@
 
 def cross_backward(
     mlen, mem_ref, q_ref, k_ref, v_ref, lse_ref, delta_ref, do_ref, wck, wcv, dk_ref, dv_ref, dqt_ref, kt_ref,
-    acc_key, acc_value, sums_ref, points,
+    acc_key, acc_value, sums_ref, stage_ref, points,
 ):
     length, mem_total = q_ref.shape[0], mem_ref.shape[0]
     step = 256
@@ -363,7 +373,7 @@
         kt_ref[:, pl.ds(c * step, step)] = k_ref[pl.ds(c * step, step), :].T
     masks = half_masks(length)
     place = lax.broadcasted_iota(jnp.int32, (step, length), 0)
-    pairs = q_ref.shape[1] // 128
+    pairs, chunks = q_ref.shape[1] // 128, mem_total // step
 
     @pl.loop(0, pairs)
     def _(p):
@@ -377,7 +387,6 @@
         doms = [pick(masks[half], dop) for half in range(2)]
         lse = [lse_ref[2 * p + half] for half in range(2)]
         delta = [delta_ref[2 * p + half] for half in range(2)]
-        dqt = [jnp.zeros((64, length), F32) for half in range(2)]
         for c in range(mem_total // step):
             rows = pl.ds(c * step, step)
             kp, vp = k_ref[rows, lanes], v_ref[rows, lanes]
@@ -389,19 +398,21 @@
                 pt = jnp.exp(st - lse[half])
                 dpt = mm_nt(vp, doms[half])
                 dst = (pt * (dpt - delta[half])).astype(BF16)
-                dqt[half] = dqt[half] + mm(kt_ref[head_rows(p, half), rows], dst)
+                stage_ref[:, pl.ds((half * chunks + c) * length, length)] = dst.astype(F32)
                 dv = dv + mm(pt.astype(BF16), doms[half])
                 dk = dk + mm(dst, qms[half])
             dv_ref[rows, lanes] = dv.astype(BF16)
             dk_ref[rows, lanes] = dk.astype(BF16)
         for half in range(2):
-            dqt_ref[head_rows(p, half), :] = dqt[half]
+            staged = [stage_ref[:, pl.ds((half * chunks + c) * length, length)] for c in range(chunks)]
+            dst = jnp.concatenate(staged, axis=0).astype(BF16)
+            dqt_ref[head_rows(p, half), :] = mm(kt_ref[head_rows(p, half), :], dst)
 
     points[1]()
     acc_key[...] += mm_tn(mem_ref[...], dk_ref[...])
     acc_value[...] += mm_tn(mem_ref[...], dv_ref[...])
 
-    @pl.loop(0, mem_total // step)
+    @pl.loop(0, mem_total // step, unroll=4)
     def _(c):
         rows = pl.ds(pl.multiple_of(c * step, step), step)
         dk, dv = dk_ref[rows, :], dv_ref[rows, :]
@@ -416,7 +427,7 @@
     outside = jnp.where(key_place < tlen, 0.0, NEG)
     masks = half_masks(length)
 
-    @pl.loop(0, q_ref.shape[1] // 128)
+    @pl.loop(0, q_ref.shape[1] // 128, unroll=4)
     def _(p):
         lanes = pair_lanes(p)
         qp, dop = q_ref[:, lanes], do_ref[:, lanes]
@@ -441,7 +452,7 @@
         dk_ref[:, lanes] = dk.astype(BF16)
 
 
-def bucket_totals(buckets_t, dbias_ref, out_ref):
+def bucket_totals(buckets_t, dbias_ref, out_ref, between):
     length = buckets_t.shape[0]
     heads = dbias_ref.shape[1] // length
     lo_places = lax.broadcasted_iota(jnp.int32, (32, 128), 0)
@@ -462,6 +473,8 @@
     acc = jnp.zeros((16 * heads, 32), F32)
     tiles = length // 128
     for band in range(tiles):
+        if band:
+            between()
         live = range(band, tiles)
 
         def body(b, acc):
@@ -508,7 +521,7 @@
         kv_scr, q2_scr, do_scr, lse2_scr, delta_scr,
         vt_scr, ot_scr, u_scr, df_scr, r_scr, dk_scr, dv_scr,
         grads, land, small, small_land, wide_scr, hs_scr, table_scr, buckets_t_scr,
-        load_sem, send_sem, recv_sem, own_sem, back_send, back_recv, back_own, group_send, group_recv, store_sem, ready_sem,
+        load_sem, send_sem, recv_sem, own_sem, back_send, back_recv, back_own, group_send, group_recv, store_sem, ready_sem, late_sem,
     ) = rest[35:]
     seqs, mem_total, width = mem_scr.shape
     length, hidden, heads = tok_ref.shape[1], u_scr.shape[1], bias_ref.shape[0]
@@ -561,12 +574,13 @@
         return remote(some, some, back_send.at[s], back_recv.at[s], partner(me, places, 1))
 
     plain, swapped = stage_orders(sizes)
-    pools = {"first": w2s, "second": w1s, "land": land}
+    spare = pl.ds(length, mem_total - length)
+    pools = {"first": w2s, "second": w1s, "key": dk_scr.at[spare], "value": dv_scr.at[spare], "land": land}
     buffers = {"grads": grads, "kv": kv_scr}
     reductions = []
-    for r, (buf, start, rows, out_start, lands) in enumerate(layout):
+    for r, (buf, start, rows, out_start, lands, color) in enumerate(layout):
         reductions.append(Reduction(
-            buffers[buf], start, rows, grads_hbm, out_start, swapped if r % 2 else plain, 16,
+            buffers[buf], start, rows, grads_hbm, out_start, swapped if color == 1 else plain, 16,
             [(pools[name], at) for name, at in lands], group_send.at[r], group_recv.at[r], store_sem.at[r],
         ))
     last = len(layout)
@@ -584,21 +598,22 @@
 
     steps = 4 * seqs
     begin_first, begin_second = 3 * (3 * seqs - 1), 3 * 3 * seqs
+    planned = len(plain) == 5 and places == 8 and seqs == 4
     acts = {p: [] for p in range(3 * steps)}
+    sends = {p: [] for p in range(3 * steps)}
     moved = [0] * len(reductions)
-    for group, begin, table in ((first, begin_first, FIRST_POINTS), (second, begin_second, SECOND_POINTS)):
-        for n, r in enumerate(group):
-            for p in table[n % len(table)]:
-                if begin + p < 3 * steps and moved[r] <= len(reductions[r]):
-                    acts[begin + p].append((r, moved[r]))
-                    moved[r] += 1
     queue = [(s, k) for s in range(seqs) for k in order]
-    sends = {p: [] for p in range(3 * steps)}
-    for p in range(3 * steps):
-        quota = -(-len(order) * PIECES[p % len(PIECES)] // 7)
-        while quota and queue and p >= 3 * (seqs + 2 * queue[0][0] + 2):
+    for p in range(3 * seqs, 3 * steps):
+        if planned:
+            count = SENDS[p - 3 * seqs]
+        else:
+            count = -(-len(order) * 2 // 7)
+        while count and queue and p >= 3 * (seqs + 2 * queue[0][0] + 2):
             sends[p].append(queue.pop(0))
-            quota -= 1
+            count -= 1
+        for r in ACTS[p - 3 * seqs] if planned else ():
+            acts[p].append((r, moved[r]))
+            moved[r] += 1
 
     def point(part, low, high):
         for step in range(low, high):
@@ -634,7 +649,8 @@
         for ref in (acc, small, wide_scr, hs_scr):
             ref[...] = jnp.zeros_like(ref)
         for h in range(heads):
-            table_scr[h] = table_ref[h : h + 1, :]
+            table_scr[h] = jnp.zeros(table_scr.shape[1:], F32)
+            table_scr[h, :, : table_ref.shape[1]] = table_ref[h : h + 1, :]
         bucket_load.wait()
         buckets_t_scr[...] = buckets_t_scr[...].T
         fill_bias(buckets_t_scr[...], table_scr, bias_ref)
@@ -710,7 +726,7 @@
         point(0, seqs, 3 * seqs)
         cross_backward(
             mlen_ref[s], mem_scr.at[s], q2_scr, k2_scr, v2_scr, lse2_scr, delta_scr, do_scr, wck, wcv,
-            dk_scr, dv_scr, ot_scr, vt_scr, acc_at(KEY), acc_at(VALUE), sums_b,
+            dk_scr, dv_scr, ot_scr, vt_scr, acc_at(KEY), acc_at(VALUE), sums_b, u_scr,
             [lambda: point(1, seqs, 3 * seqs), lambda: point(2, seqs, 3 * seqs)],
         )
         own_back(s).start()
@@ -736,6 +752,7 @@
             rows = pl.ds(pl.multiple_of(base + b * 256, 256), 256)
             grads[rows, :] = acc[rows, :].astype(BF16)
 
+        signal_all(late_sem, flips)
         st_scr[...] = jnp.zeros_like(st_scr)
         acc[pl.ds(0, 3 * width), :] = jnp.zeros((3 * width, width), F32)
 
@@ -783,23 +800,33 @@
         small[HEAD_ROWS : HEAD_ROWS + heads] = jnp.broadcast_to(
             jnp.sum(hs_scr[...], axis=1, keepdims=True), (heads, width)
         )
+        def move(r):
+            if r < 0:
+                if queue:
+                    send_back(*queue.pop(0))
+            elif moved[r] <= len(reductions[r]):
+                reductions[r].advance(moved[r])
+                moved[r] += 1
+
+        if flips:
+            pl.semaphore_wait(late_sem, len(flips))
         for r in third:
-            reductions[r].advance(0)
-            moved[r] = 1
-        for r in first + second:
-            reductions[r].advance(moved[r])
-            moved[r] += 1
-        bucket_totals(buckets_t_scr, st_scr, small.at[pl.ds(TABLE_ROWS, heads)])
+            move(r)
+
+        def between():
+            for r in BETWEEN if planned else first + second + third:
+                move(r)
+
+        bucket_totals(buckets_t_scr, st_scr, small.at[pl.ds(TABLE_ROWS, heads)], between)
+        for r in TAIL if planned else ():
+            move(r)
         left = third + [last] + second + first
         while any(moved[r] <= len(reductions[r]) for r in left):
             for r in left:
-                reductions[r].advance(moved[r])
-                moved[r] += 1
-            for _ in range(-(-len(order) * 2 // 7)):
-                if queue:
-                    send_back(*queue.pop(0))
-        for s, k in queue:
-            send_back(s, k)
+                move(r)
+            move(-1)
+        while queue:
+            move(-1)
         for s in range(seqs):
             own_back(s).wait()
             if places > 1:
@@ -808,30 +835,69 @@
                 all_back(s).wait_recv()
 
 
-FIRST_POINTS = ((0, 1, 2, 4, 6, 8, 10, 12), (0, 1, 2, 4, 6, 8, 10, 12), (1, 2, 3, 5, 7, 9, 11, 13), (1, 2, 3, 5, 7, 9, 11, 13))
-SECOND_POINTS = ((1, 3, 5, 7, 9), (1, 3, 5, 7, 9), (2, 4, 6, 8, 10), (2, 4, 6, 8, 10))
-PIECES = (2, 2, 2)
-
-
-def reduction_layout(sizes, width, hidden):
+ACTS = (
+    (),
+    (),
+    (),
+    (),
+    (),
+    (),
+    (),
+    (),
+    (),
+    (),
+    (),
+    (),
+    (),
+    (),
+    (),
+    (),
+    (),
+    (),
+    (),
+    (),
+    (),
+    (0, 1, 2, 3),
+    (0,),
+    (1, 2, 3),
+    (4, 5, 6, 7),
+    (0, 4, 5, 6),
+    (1, 7, 2),
+    (),
+    (0, 3),
+    (),
+    (),
+    (0, 4, 2),
+    (5, 3),
+    (6,),
+    (2, 1, 3, 0, 4),
+    (5, 7),
+)
+SENDS = (0, 0, 0, 0, 0, 0, 0, 0, 0, 0, 0, 0, 0, 0, 0, 1, 0, 2, 2, 2, 1, 0, 2, 2, 0, 2, 0, 1, 0, 2, 0, 0, 2, 0, 0, 2)
+BETWEEN = (0, 1, 2, 3, 4, 5, 6, 7, 8, 9, 10)
+TAIL = (11, 11, 8, 10, 0, 1, 11, 9, 2, 3, 8, -1, 10, 4, 6, 5, 7, 9, 1, 0, 2, 11, 3, 8, 2, 10, 4, -1, -1, 6, 0, 3, 5, 9, 7, 1, 11, 0, 8, 10, 4, 2, 2, 5, 6, 4, -1, -1, 9, 7, 11, 3, 8, 6, 5, 10, 3, 1, 11, 6, -1, -1, 7, 9, 8, 4, 10, 1, 4, 5, 11, 1, 5, 11, 6, 9, 8, 6, 7, 9, 10, 8, 7, 8, 7, 9, 10, 9, 10)
+MEMBERS = (('first', 0, 2), ('first', 1, 2), ('first', 0, 2), ('first', 0, 2), ('second', 0, 2), ('second', 0, 1), ('second', 0, 1), ('second', 0, 1), ('third', 1, 1), ('third', 1, 1), ('third', 0, 1))
+
+
+def reduction_layout(sizes, width, hidden, spare):
     plain, _ = stage_orders(sizes)
     base = 2 * hidden
-    members = [("grads", k * hidden // 2, hidden // 2, k * hidden // 2) for k in range(4)]
-    members += [("grads", base, 2 * width, base), ("grads", base + 2 * width, 2 * width, base + 2 * width)]
-    members += [("grads", base + 4 * width, width, base + 4 * width)]
-    members += [("kv", 0, width, base + 5 * width), ("kv", width, width, base + 6 * width)]
-    members += [("kv", 2 * width, width, base + 7 * width)]
-    used = {"first": 0, "second": 0, "land": 0}
+    members, at = [], {"first": 0, "second": 2 * hidden, "third": 0}
+    for name, color, units in MEMBERS:
+        rows = units * width
+        out_start = at[name] + (base + 5 * width if name == "third" else 0)
+        members.append(("kv" if name == "third" else "grads", at[name], rows, out_start, color))
+        at[name] += rows
+    used = {"first": 0, "second": 0, "key": 0, "value": 0, "land": 0}
     layout = []
-    for buf, start, rows, out_start in members:
+    for buf, start, rows, out_start, color in members:
         lands = []
         for size in fold_sizes(rows, plain, 16):
-            name = "land"
-            if buf == "grads":
-                name = next((n for n in ("first", "second") if used[n] + size <= hidden), "land")
+            room = {"first": hidden, "second": hidden} if buf == "grads" else {"key": spare, "value": spare}
+            name = next((n for n in room if used[n] + size <= room[n]), "land")
             lands.append((name, used[name]))
             used[name] += size
-        layout.append((buf, start, rows, out_start, lands))
+        layout.append((buf, start, rows, out_start, lands, color))
     return layout, max(used["land"], 16)
 
 
@@ -840,7 +906,7 @@
     places, _, piece, _ = memory.shape
     mem_total = places * piece
     heads, hidden = head_scale.shape[0], w1.shape[1]
-    layout, land = reduction_layout(sizes, width, hidden)
+    layout, land = reduction_layout(sizes, width, hidden, mem_total - length)
     plain, _ = stage_orders(sizes)
     small_land = max(sum(fold_sizes(SMALL_ROWS, plain, 8)), 8)
     slots = max(2 * len(plain), 1)
@@ -864,7 +930,7 @@
         ((width, mem_total), BF16), ((width, length), F32), ((length, hidden), F32), ((length, hidden), F32),
         ((length, 128), F32), ((max(mem_total, hidden // width * length), width), BF16), ((mem_total, width), BF16),
         ((2 * hidden + 5 * width, width), BF16), ((land, width), BF16), ((SMALL_ROWS, width), F32), ((small_land, width), F32),
-        ((24, hidden), F32), ((heads, length), F32), ((heads, 1, table.shape[1]), F32), ((length, length), jnp.int32),
+        ((24, hidden), F32), ((heads, length), F32), ((heads, 1, 512), F32), ((length, length), jnp.int32),
     ]
     dma = pltpu.SemaphoreType.DMA
     groups = len(layout) + 1
@@ -882,7 +948,7 @@
             out_specs=[seq(middle), seq(late), anywhere, anywhere, anywhere],
             scratch_shapes=[pltpu.VMEM(shape, dtype) for shape, dtype in scratch] + [
                 dma((hidden // width + 2,)), dma((seqs,)), dma((seqs,)), dma((seqs,)), dma((seqs,)), dma((seqs,)),
-                dma((seqs,)), dma((groups, slots)), dma((groups, slots)), dma((groups,)), pltpu.SemaphoreType.REGULAR,
+                dma((seqs,)), dma((groups, slots)), dma((groups, slots)), dma((groups,)), pltpu.SemaphoreType.REGULAR, pltpu.SemaphoreType.REGULAR,
             ],
         ),
         compiler_params=pltpu.CompilerParams(
@@ -892,69 +958,73 @@
     )(tlen, mlen, head_scale, tokens, cotangent, mask, buckets, table, memory, w1, w2, *vecs, *wides, *weights)
 
 
-def unpack_kernel(grads_ref, small_ref, *refs):
-    big, vectors, (table_ref, scale_ref, slots, sem) = refs[:10], refs[10:-4], refs[-4:]
+def unpack_kernel(count, grads_hbm, small_ref, *refs):
+    kept, refs = refs[:count], refs[count:]
+    passed, refs = refs[:count], refs[count:]
+    big, vectors, tail = refs[:10], refs[10:28], refs[28:]
+    table_ref, scale_ref, rough, exact = tail[:4]
+    holds, (in_sem, out_sem, hold_in, hold_out) = tail[4:-4], tail[-4:]
     dw1, dw2, rest = big[0], big[1], big[2:]
-    width = grads_ref.shape[0]
+    width = grads_hbm.shape[1]
     parts = dw1.shape[1] // width
     targets = [dw1.at[:, pl.ds(c * width, width)] for c in range(parts)]
     targets += [dw2.at[pl.ds(c * width, width)] for c in range(parts)] + list(rest)
-    t = pl.program_id(0)
-    depth = slots.shape[0]
-    slot = lax.rem(t, depth)
-
-    def settle(k):
-        pltpu.make_async_copy(slots.at[k], rest[0], sem.at[k]).wait()
-
-    @pl.when(t >= depth)
-    def _():
-        settle(slot)
-
-    slots[slot] = grads_ref[...].astype(F32)
-    for k, target in enumerate(targets):
-
-        @pl.when(t == k)
-        def _():
-            pltpu.make_async_copy(slots.at[k % depth], target, sem.at[k % depth]).start()
-
-    @pl.when(t == 0)
-    def _():
-        for row, ref in zip(VECTOR_ROWS, vectors):
-            for c in range(ref.shape[1] // width):
-                ref[:, c * width : (c + 1) * width] = small_ref[row + c : row + c + 1]
-        heads = scale_ref.shape[1]
-        buckets = table_ref.shape[0]
-        table_ref[...] = small_ref[48 : 48 + heads].T[:buckets]
-        block = small_ref[40 : 40 + heads]
-        diagonal = lax.broadcasted_iota(jnp.int32, block.shape, 0) == lax.broadcasted_iota(jnp.int32, block.shape, 1)
-        scale_ref[...] = colsum(jnp.where(diagonal, block, 0.0))[:, :heads]
-
-    @pl.when(t == len(targets) - 1)
-    def _():
-        for k in range(depth):
-            settle(k)
+    rows = [pl.ds(k * width, width) for k in range(len(targets))]
+    into = [pltpu.make_async_copy(grads_hbm.at[r], rough.at[r], in_sem.at[k]) for k, r in enumerate(rows)]
+    out = [pltpu.make_async_copy(exact.at[r], target, out_sem.at[k]) for k, (r, target) in enumerate(zip(rows, targets))]
+    take = [pltpu.make_async_copy(a, hold, hold_in.at[k]) for k, (a, hold) in enumerate(zip(kept, holds))]
+    give = [pltpu.make_async_copy(hold, a, hold_out.at[k]) for k, (a, hold) in enumerate(zip(passed, holds))]
+    for c in into + take:
+        c.start()
+    for row, ref in zip(VECTOR_ROWS, vectors):
+        for c in range(ref.shape[1] // width):
+            ref[:, c * width : (c + 1) * width] = small_ref[row + c : row + c + 1]
+    heads = scale_ref.shape[1]
+    table_ref[...] = small_ref[TABLE_ROWS : TABLE_ROWS + heads, : table_ref.shape[1]]
+    block = small_ref[HEAD_ROWS : HEAD_ROWS + heads]
+    diagonal = lax.broadcasted_iota(jnp.int32, block.shape, 0) == lax.broadcasted_iota(jnp.int32, block.shape, 1)
+    scale_ref[...] = colsum(jnp.where(diagonal, block, 0.0))[:, :heads]
+    step = 64
+    for k in range(len(targets)):
+        into[k].wait()
+
+        @pl.loop(0, width // step)
+        def _(b):
+            part = pl.ds(pl.multiple_of(k * width + b * step, step), step)
+            exact[part, :] = rough[part, :].astype(F32)
+
+        out[k].start()
+    for a, b in zip(take, give):
+        a.wait()
+        b.start()
+    for c in out + give:
+        c.wait()
 
 
 VECTOR_ROWS = (24, 25, 26, 27, 28, 29, 30, 31, 32, 4, 5, 3, 1, 2, 0, 16, 8, 12)
 
 
-def unpack(grads, small, hidden, heads, buckets):
-    width = grads.shape[1]
+def unpack(grads, small, kept, hidden, heads, buckets):
+    total, width = grads.shape
     sds = jax.ShapeDtypeStruct
     big = [sds((width, hidden), F32), sds((hidden, width), F32)] + [sds((width, width), F32)] * 8
     vectors = [sds((1, width), F32)] * 15 + [sds((1, hidden), F32)] * 3
-    tail = [sds((buckets, heads), F32), sds((1, heads), F32)]
-    whole = lambda a: pl.BlockSpec(a.shape, lambda t: (0,) * len(a.shape))
-    steps = grads.shape[0] // width
-    return pl.pallas_call(
-        unpack_kernel,
-        out_shape=big + vectors + tail,
-        grid=(steps,),
-        in_specs=[pl.BlockSpec((width, width), lambda t: (t, 0)), whole(small)],
-        out_specs=[pl.BlockSpec(memory_space=pl.ANY)] * 10 + [whole(a) for a in vectors + tail],
-        scratch_shapes=[pltpu.VMEM((4, width, width), F32), pltpu.SemaphoreType.DMA((4,))],
+    tail = [sds((heads, buckets), F32), sds((1, heads), F32)]
+    anywhere, inside = pl.BlockSpec(memory_space=pl.ANY), pl.BlockSpec(memory_space=pltpu.VMEM)
+    dma = pltpu.SemaphoreType.DMA
+    count = len(kept)
+    outs = pl.pallas_call(
+        functools.partial(unpack_kernel, count),
+        out_shape=[sds(a.shape, a.dtype) for a in kept] + big + vectors + tail,
+        in_specs=[anywhere, inside] + [anywhere] * count,
+        out_specs=[anywhere] * (count + 10) + [inside] * (len(vectors) + len(tail)),
+        scratch_shapes=[pltpu.VMEM((total, width), BF16), pltpu.VMEM((total, width), F32)]
+        + [pltpu.VMEM(a.shape, a.dtype) for a in kept]
+        + [dma((total // width,)), dma((total // width,)), dma((count,)), dma((count,))],
+        compiler_params=pltpu.CompilerParams(vmem_limit_bytes=VMEM_LIMIT),
         name="unpack",
-    )(grads, small)
+    )(grads, small, *kept)
+    return outs[:count], outs[count:]
 
 
 def local(
@@ -967,7 +1037,7 @@
     heads = head_scale.shape[0]
     bucket_count = position_table.shape[0]
     hidden = inner_weight.shape[1]
-    table_t = jnp.pad(position_table.T, ((0, 0), (0, 512 - bucket_count)))
+    table_t = position_table.T
     row = lambda v: v.reshape(1, -1)
     vecs = [row(v) for v in (
         self_gain, self_shift, query_bias, value_bias, output_bias, output_bias, cross_gain, cross_shift,
@@ -980,14 +1050,16 @@
         memory, inner_weight, outer_weight, vecs, wides,
         [query_weight, key_weight, value_weight, output_weight, cross_query, cross_key, cross_value, cross_output],
     )
-    outs = unpack(grads, small, hidden, heads, bucket_count)
+    (layer_output, dtok, memory_gradient), outs = unpack(
+        grads, small, [layer_output, dtok, memory_gradient], hidden, heads, bucket_count
+    )
     dw1, dw2, dwco, dwo, dwcq, dwck, dwcv, dwq, dwk, dwv = outs[:10]
     (
         d_self_gain, d_self_shift, d_query_bias, d_value_bias, d_output_bias, d_cross_gain, d_cross_shift,
         d_cross_query_bias, d_cross_value_bias, d_post_gain, d_post_shift, d_cross_output_bias, d_feed_gain,
         d_feed_shift, d_outer_bias, d_inner_bias, d_inner_gain, d_inner_shift,
     ) = [v.reshape(-1) for v in outs[10:28]]
-    d_table, d_scale = outs[28], outs[29].reshape(-1)
+    d_table, d_scale = outs[28].T, outs[29].reshape(-1)
     return (
         layer_output, dtok, memory_gradient,
         d_self_gain, d_self_shift, dwq, d_query_bias, dwk, dwv, d_value_bias, d_table, d_scale,

time: 319 us -> 282 us (0.88)
  Pallas kernels: 308 us -> 281 us
  local copies, waits for them, and re-layouts: 9.57 us -> 0 us
    pallas_call x1, Pallas kernels: 293 us -> 265 us  [whole_layer(): pl.pallas_call(functools.partial(layer_kernel, sizes, layout), out_shape=...]
    unnamed x8 -> x0, local copies, waits for them, and re-layouts: 8.25 us -> none
where the time goes in v4:
time: 282 us
  Pallas kernels  281 us (100%)
    pallas_call x1, Pallas kernels, whole_layer(): pl.pallas_call(functools.partial(layer_kernel, sizes, layout), out_shape=...  265 us
    pallas_call x1, Pallas kernels, unpack(): pl.pallas_call(functools.partial(unpack_kernel, count), out_shape=[sds(a....  15.7 us

profile of v4, /device:TPU:0, one launch (start us, length us, event | category | flops | bytes accessed | tf_op | source)
XLA Modules:
  0.0 281.6 jit_solution(1942861182374756312)
XLA Ops:
  0.7 265.3 %layer.1 = (bf16[4,256,512]{2,1,0:T(8,128)(2,1)}, bf16[4,256,512]{2,1,0:T(8,128)(2,1)}, bf16[8,4,128,512]{3,2,1,0:T(8,128)(2,1)}, bf16[8192,512]{1,0:T(8,128)(2,1)}, f32[64,512]{1,0:T(8,128)}) custom-call(s32[4]{0:T(128)} %tlen_ref.1, s32[4]{0:T(128)} %mlen_ref.1, f32[8]{0:T(128)} %hs_ref.1, bf16[4,256,512]{2,1,0:T(8,128)(2,1)} %tok_ref.1, ...), custom_call_target="tpu_custom_call" | custom-call | tf_op jit(solution)/shard_map/layer/pallas_call | solution.py:937
  266.0 15.7 %unpack.1 = (bf16[4,256,512]{2,1,0:T(8,128)(2,1)}, bf16[4,256,512]{2,1,0:T(8,128)(2,1)}, bf16[8,4,128,512]{3,2,1,0:T(8,128)(2,1)}, f32[512,2048]{1,0:T(8,128)}, ...) custom-call(bf16[8192,512]{1,0:T(8,128)(2,1)} %get-tuple-element.71., ...), custom_call_target="tpu_custom_call" | custom-call | tf_op jit(solution)/shard_map/unpack/pallas_call | solution.py:1016

commit v5 on v4

--- a/solution.py
+++ b/solution.py
@@ -513,7 +513,7 @@
 def layer_kernel(sizes, layout, tlen_ref, mlen_ref, hs_ref, tok_ref, cot_ref, mask_ref, buckets_ref, table_ref, *rest):
     mem_hbm, w1_hbm, w2_hbm = rest[:3]
     vec_ref, wide_ref = rest[3:19], rest[19:22]
-    wq, wk, wv, wo, wcq, wck, wcv, wco = rest[22:30]
+    weights_hbm = rest[22:30]
     out_ref, dtok_ref, dmem_hbm, grads_hbm, small_hbm = rest[30:35]
     (
         mem_scr, w1s, w2s, acc, bias_ref, st_scr,
@@ -522,7 +522,9 @@
         vt_scr, ot_scr, u_scr, df_scr, r_scr, dk_scr, dv_scr,
         grads, land, small, small_land, wide_scr, hs_scr, table_scr, buckets_t_scr,
         load_sem, send_sem, recv_sem, own_sem, back_send, back_recv, back_own, group_send, group_recv, store_sem, ready_sem, late_sem,
+        weight_sem, *weight_scr,
     ) = rest[35:]
+    wq, wk, wv, wo, wcq, wck, wcv, wco = weight_scr
     seqs, mem_total, width = mem_scr.shape
     length, hidden, heads = tok_ref.shape[1], u_scr.shape[1], bias_ref.shape[0]
     places, piece = mem_hbm.shape[0], mem_hbm.shape[2]
@@ -640,6 +642,12 @@
         if peers:
             barrier = pltpu.get_barrier_semaphore()
             signal_all(barrier, peers)
+        weight_loads = [
+            pltpu.make_async_copy(a, b, weight_sem.at[k]) for k, (a, b) in enumerate(zip(weights_hbm, weight_scr))
+        ]
+        for c in weight_loads:
+            c.start()
+        if peers:
             pl.semaphore_wait(barrier, len(peers))
         for s in range(seqs):
             for k in order:
@@ -654,6 +662,8 @@
         bucket_load.wait()
         buckets_t_scr[...] = buckets_t_scr[...].T
         fill_bias(buckets_t_scr[...], table_scr, bias_ref)
+        for c in weight_loads:
+            c.wait()
 
     @pl.when(t < seqs)
     def _():
@@ -857,26 +867,26 @@
     (),
     (),
     (),
-    (0, 1, 2, 3),
-    (0,),
-    (1, 2, 3),
-    (4, 5, 6, 7),
-    (0, 4, 5, 6),
-    (1, 7, 2),
-    (),
-    (0, 3),
-    (),
-    (),
-    (0, 4, 2),
-    (5, 3),
-    (6,),
-    (2, 1, 3, 0, 4),
-    (5, 7),
+    (0, 1),
+    (2, 3, 0, 1),
+    (2, 3),
+    (4, 5, 0, 1),
+    (4, 5, 2),
+    (),
+    (1,),
+    (3, 2, 0),
+    (1,),
+    (),
+    (2, 3, 0, 4, 1),
+    (),
+    (),
+    (5, 3, 2, 4, 0),
+    (1,),
 )
-SENDS = (0, 0, 0, 0, 0, 0, 0, 0, 0, 0, 0, 0, 0, 0, 0, 1, 0, 2, 2, 2, 1, 0, 2, 2, 0, 2, 0, 1, 0, 2, 0, 0, 2, 0, 0, 2)
-BETWEEN = (0, 1, 2, 3, 4, 5, 6, 7, 8, 9, 10)
-TAIL = (11, 11, 8, 10, 0, 1, 11, 9, 2, 3, 8, -1, 10, 4, 6, 5, 7, 9, 1, 0, 2, 11, 3, 8, 2, 10, 4, -1, -1, 6, 0, 3, 5, 9, 7, 1, 11, 0, 8, 10, 4, 2, 2, 5, 6, 4, -1, -1, 9, 7, 11, 3, 8, 6, 5, 10, 3, 1, 11, 6, -1, -1, 7, 9, 8, 4, 10, 1, 4, 5, 11, 1, 5, 11, 6, 9, 8, 6, 7, 9, 10, 8, 7, 8, 7, 9, 10, 9, 10)
-MEMBERS = (('first', 0, 2), ('first', 1, 2), ('first', 0, 2), ('first', 0, 2), ('second', 0, 2), ('second', 0, 1), ('second', 0, 1), ('second', 0, 1), ('third', 1, 1), ('third', 1, 1), ('third', 0, 1))
+SENDS = (0, 0, 0, 0, 0, 0, 0, 0, 0, 0, 0, 0, 0, 1, 2, 0, 2, 2, 1, 2, 0, 0, 2, 2, 0, 1, 0, 2, 0, 0, 2, 0, 0, 2, 0, 0)
+BETWEEN = (2, 3, 4, 5, 6, 7, 8, -1)
+TAIL = (0, 9, 1, 2, 3, 6, 9, 5, 4, 8, 7, 6, 0, 9, 1, 3, -1, -1, 7, 5, 2, 6, 4, 8, 9, 0, 7, 3, 4, -1, -1, 1, 8, 9, 5, 6, 7, 1, 0, 2, 0, -1, -1, 8, 4, 2, 5, 9, 3, 6, 7, 3, 6, 8, 7, 5, 4, 9, 8, 6, 7, 4, 8, 6, 5, 9, 6, 7, 5, 9, 8, 7, 8)
+MEMBERS = (('first', 1, 2), ('first', 0, 2), ('first', 0, 2), ('first', 0, 2), ('second', 0, 3), ('second', 0, 2), ('third', 1, 1), ('third', 1, 1), ('third', 0, 1))
 
 
 def reduction_layout(sizes, width, hidden, spare):
@@ -944,12 +954,13 @@
             num_scalar_prefetch=3,
             grid=(4 * seqs,),
             in_specs=[seq(ends), seq(middle), const(mask), anywhere, const(table), anywhere, anywhere, anywhere]
-            + [const(a) for a in vecs + wides + weights],
+            + [const(a) for a in vecs + wides] + [anywhere] * len(weights),
             out_specs=[seq(middle), seq(late), anywhere, anywhere, anywhere],
             scratch_shapes=[pltpu.VMEM(shape, dtype) for shape, dtype in scratch] + [
                 dma((hidden // width + 2,)), dma((seqs,)), dma((seqs,)), dma((seqs,)), dma((seqs,)), dma((seqs,)),
                 dma((seqs,)), dma((groups, slots)), dma((groups, slots)), dma((groups,)), pltpu.SemaphoreType.REGULAR, pltpu.SemaphoreType.REGULAR,
-            ],
+                dma((len(weights),)),
+            ] + [pltpu.VMEM(a.shape, BF16) for a in weights],
         ),
         compiler_params=pltpu.CompilerParams(
             vmem_limit_bytes=VMEM_LIMIT, collective_id=0 if several else None, has_side_effects=True

time: 282 us -> 272 us (0.965)
  Pallas kernels: 281 us -> 271 us
    pallas_call x1, Pallas kernels: 265 us -> 255 us  [whole_layer(): pl.pallas_call(functools.partial(layer_kernel, sizes, layout), out_shape=...]
where the time goes in v5:
time: 272 us
  Pallas kernels  271 us (100%)
    pallas_call x1, Pallas kernels, whole_layer(): pl.pallas_call(functools.partial(layer_kernel, sizes, layout), out_shape=...  255 us
    pallas_call x1, Pallas kernels, unpack(): pl.pallas_call(functools.partial(unpack_kernel, count), out_shape=[sds(a....  15.7 us

profile of v5, /device:TPU:0, one launch (start us, length us, event | category | flops | bytes accessed | tf_op | source)
XLA Modules:
  0.0 271.7 jit_solution(5803796849747661980)
XLA Ops:
  0.7 255.4 %layer.1 = (bf16[4,256,512]{2,1,0:T(8,128)(2,1)}, bf16[4,256,512]{2,1,0:T(8,128)(2,1)}, bf16[8,4,128,512]{3,2,1,0:T(8,128)(2,1)}, bf16[8192,512]{1,0:T(8,128)(2,1)}, f32[64,512]{1,0:T(8,128)}) custom-call(s32[4]{0:T(128)} %tlen_ref.1, s32[4]{0:T(128)} %mlen_ref.1, f32[8]{0:T(128)} %hs_ref.1, bf16[4,256,512]{2,1,0:T(8,128)(2,1)} %tok_ref.1, ...), custom_call_target="tpu_custom_call" | custom-call | tf_op jit(solution)/shard_map/layer/pallas_call | solution.py:947
  256.1 15.7 %unpack.1 = (bf16[4,256,512]{2,1,0:T(8,128)(2,1)}, bf16[4,256,512]{2,1,0:T(8,128)(2,1)}, bf16[8,4,128,512]{3,2,1,0:T(8,128)(2,1)}, f32[512,2048]{1,0:T(8,128)}, ...) custom-call(bf16[8192,512]{1,0:T(8,128)(2,1)} %get-tuple-element.71., ...), custom_call_target="tpu_custom_call" | custom-call | tf_op jit(solution)/shard_map/unpack/pallas_call | solution.py:1027

commit v6 on v5

--- a/solution.py
+++ b/solution.py
@@ -245,11 +245,12 @@
     x1_ref[...] = x0 + mm(c1, wo[...]) + vec_ref[OUTPUT_BIAS][...]
 
 
-def cross_forward(mlen, mem_ref, vec_ref, x1, wcq, wck, wcv, q_ref, k_ref, v_ref, lse_ref, ot_ref, vt_ref, st_ref):
+def cross_forward(mlen, mem_ref, vec_ref, x1, wcq, wck, wcv, q_ref, k_ref, v_ref, lse_ref, ot_ref, vt_ref, st_ref, arrive):
     length, mem_total = x1.shape[0], mem_ref.shape[0]
     hat, _ = normalize(x1)
     h2 = (hat * vec_ref[CROSS_GAIN][...] + vec_ref[CROSS_SHIFT][...]).astype(BF16)
     q_ref[...] = ((mm(h2, wcq[...]) + vec_ref[CROSS_QUERY_BIAS][...]) * 0.125).astype(BF16)
+    arrive()
     step = 256
 
     @pl.loop(0, mem_total // step, unroll=4)
@@ -682,14 +683,16 @@
 
     @pl.when((t >= seqs) & (t < 3 * seqs) & (inner % 2 == 0))
     def _():
-        own_in(s).wait()
-        if places > 1:
-            all_in(s).wait_recv()
-        point(0, seqs, 3 * seqs)
+        def arrive():
+            own_in(s).wait()
+            if places > 1:
+                all_in(s).wait_recv()
+            point(0, seqs, 3 * seqs)
+
         x1 = x1_scr[s]
         cross_forward(
             mlen_ref[s], mem_scr.at[s], vec_ref, x1, wcq, wck, wcv,
-            q2_scr, k2_scr, v2_scr, lse2_scr, ot_scr, vt_scr, st_scr,
+            q2_scr, k2_scr, v2_scr, lse2_scr, ot_scr, vt_scr, st_scr, arrive,
         )
         point(1, seqs, 3 * seqs)
         hat, scale = normalize(ot_scr[...].T)

time: 272 us -> 271 us (level)
  no operation moved by 1% of the time
where the time goes in v6:
time: 271 us
  Pallas kernels  271 us (100%)
    pallas_call x1, Pallas kernels, whole_layer(): pl.pallas_call(functools.partial(layer_kernel, sizes, layout), out_shape=...  255 us
    pallas_call x1, Pallas kernels, unpack(): pl.pallas_call(functools.partial(unpack_kernel, count), out_shape=[sds(a....  15.7 us

profile of v6, /device:TPU:0, one launch (start us, length us, event | category | flops | bytes accessed | tf_op | source)
XLA Modules:
  0.0 271.3 jit_solution(16778069245884758955)
XLA Ops:
  0.7 254.9 %layer.1 = (bf16[4,256,512]{2,1,0:T(8,128)(2,1)}, bf16[4,256,512]{2,1,0:T(8,128)(2,1)}, bf16[8,4,128,512]{3,2,1,0:T(8,128)(2,1)}, bf16[8192,512]{1,0:T(8,128)(2,1)}, f32[64,512]{1,0:T(8,128)}) custom-call(s32[4]{0:T(128)} %tlen_ref.1, s32[4]{0:T(128)} %mlen_ref.1, f32[8]{0:T(128)} %hs_ref.1, bf16[4,256,512]{2,1,0:T(8,128)(2,1)} %tok_ref.1, ...), custom_call_target="tpu_custom_call" | custom-call | tf_op jit(solution)/shard_map/layer/pallas_call | solution.py:950
  255.6 15.7 %unpack.1 = (bf16[4,256,512]{2,1,0:T(8,128)(2,1)}, bf16[4,256,512]{2,1,0:T(8,128)(2,1)}, bf16[8,4,128,512]{3,2,1,0:T(8,128)(2,1)}, f32[512,2048]{1,0:T(8,128)}, ...) custom-call(bf16[8192,512]{1,0:T(8,128)(2,1)} %get-tuple-element.71., ...), custom_call_target="tpu_custom_call" | custom-call | tf_op jit(solution)/shard_map/unpack/pallas_call | solution.py:1030
